TPU v7x, 256 devices: a whole 4x4x8 slice. The times are simulated.
256 devices in a mesh: path: 16 (over z, core), fsdp: 16 (over y, x).
Axes of the slice: x: 4, y: 4, z: 8, core: 2. Of those that a mesh axis runs over, the one named last changes fastest.
Arguments:
- path_delta: bfloat16 [16, 4, 512, 4096], P('path', None, 'fsdp'), may hold values from -20 to 20
- feedback: float32 [16, 4, 512, 4096], P('path', None, 'fsdp'), may hold values from -4 to 4
- global_params: float32 [4, 2, 512, 4096], P(None, None, 'fsdp', 'path'), may hold values from -0.09375 to 0.09375
- momentum: float32 [4, 2, 512, 4096], P(None, None, 'fsdp', 'path'), may hold values from -2 to 2
- routes: int32 [16, 4], replicated, may hold values from 0 to 1
- token_counts: int32 [16, 4], replicated, may hold values from 1 to 16
- skip_flags: int32 [4, 2], replicated, may hold values from 0 to 1, as said below
Outputs:
- feedback_next: float32 [16, 4, 512, 4096], P('path', None, 'fsdp')
- momentum_next: float32 [4, 2, 512, 4096], P(None, None, 'fsdp', 'path')
- params_next: float32 [4, 2, 512, 4096], P(None, None, 'fsdp', 'path')
- path_params: bfloat16 [16, 4, 512, 4096], P('path', None, 'fsdp')
Inputs may be any that keep to these rules, and one draw needn't show every extreme that they name: `skip_flags`: at most one of the two modules of a level skips.
All inputs are finite; a program needn't handle non-finite values.
Results may differ from a plain program's by a relative error of at most 0.012.
Values may be sent and summed in bfloat16 or wider, within the bound.
No kernel may reach another device: no remote copies, remote signals or barrier semaphores. Data moves between devices by JAX's collectives and lax.ppermute only.
A program may use at most 64 MiB of HBM per device.

v0:
```python
import functools

import jax
import jax.numpy as jnp
from jax import lax
from jax.sharding import Mesh
from jax.sharding import PartitionSpec as P

PATH = ("path_0", "path_1")
PATH_FSDP = ("path_0", "path_1", "fsdp_0", "fsdp_1")
FSDP = ("fsdp_0", "fsdp_1")


clip_rms = 0.2
outer_rate = 0.7
momentum_coef = 0.9
epsilon_sq = 1e-06


def cut_along(x, dim, count):
    before, after = (x.shape[:dim], x.shape[dim + 1 :])
    return jnp.moveaxis(x.reshape(*before, count, -1, *after), dim, 0)


def joined_along(parts, dim):
    parts = jnp.moveaxis(parts, 0, dim)
    dims = parts.shape
    return parts.reshape(*dims[:dim], dims[dim] * dims[dim + 1], *dims[dim + 2 :])


def turned_blocks(parts, axes, sequence):
    dims = [lax.axis_size(a) for a in axes]
    parts = parts.reshape(*dims, *parts.shape[1:])
    for k in sequence:
        parts = lax.all_to_all(parts, axes[k], split_axis=k, concat_axis=k, tiled=True)
    return parts.reshape(-1, *parts.shape[len(axes) :])


def one_axis_at_a_time(x, axes, sequence, split_dim, concat_dim):
    parts = cut_along(x, split_dim, lax.axis_size(axes))
    return joined_along(turned_blocks(parts, axes, sequence), concat_dim)


def over_axes(x, axes):
    return functools.reduce(lax.psum, axes, x)


def on_device(path_delta, feedback, global_params, momentum, routes, token_counts, skip_flags):
    own_index = lax.axis_index(PATH)
    counts = token_counts.astype(jnp.float32)
    same = (routes[:, None, :] == routes[None, :, :]).astype(jnp.float32)
    denom = jnp.sum(same * counts[None, :, :], axis=1)
    weight = counts / denom
    skipped_path = jnp.where(routes == 1, skip_flags[None, :, 1], skip_flags[None, :, 0])
    live = (1 - skipped_path).astype(jnp.float32)
    own_weight = lax.dynamic_slice_in_dim(weight, own_index, 1, 0)[0]
    own_live = lax.dynamic_slice_in_dim(live, own_index, 1, 0)[0]
    corrected = path_delta[0].astype(jnp.float32) + feedback[0]
    scaled = (own_weight[:, None, None] * corrected).astype(jnp.bfloat16)
    sent = jnp.where(own_live[:, None, None] > 0, scaled, jnp.zeros_like(scaled))
    feedback_next = corrected - own_live[:, None, None] * (
        sent.astype(jnp.float32) / own_weight[:, None, None]
    )
    onehot = routes[:, :, None] == jnp.arange(2, dtype=jnp.int32)[None, None, :]
    pieces = one_axis_at_a_time(sent[None], PATH, (1, 0), 3, 0)
    average = jnp.einsum(
        "plm,plrc->lmrc", onehot.astype(jnp.bfloat16), pieces, preferred_element_type=jnp.float32
    )
    local_sq = jnp.sum(average * average, axis=(2, 3))
    total_sq = over_axes(local_sq, PATH_FSDP)
    entries = average.shape[2] * average.shape[3] * lax.axis_size(PATH) * lax.axis_size(FSDP)
    factor = jnp.minimum(1.0, clip_rms / jnp.sqrt(total_sq / entries + epsilon_sq))
    clipped = factor[:, :, None, None] * average
    skipped = (skip_flags > 0)[:, :, None, None]
    momentum_next = jnp.where(skipped, momentum, momentum_coef * momentum + clipped)
    params_next = jnp.where(
        skipped,
        global_params,
        global_params - outer_rate * (clipped + momentum_coef * momentum_next),
    )
    narrow = params_next.astype(jnp.bfloat16)
    outgoing = jnp.where((routes == 1)[:, :, None, None], narrow[None, :, 1], narrow[None, :, 0])
    returned = lax.all_to_all(outgoing, PATH, split_axis=0, concat_axis=3, tiled=True)
    return (feedback_next[None], momentum_next, params_next, returned)


def solution(mesh):
    finer = Mesh(mesh.devices.reshape(8, 2, 4, 4), ("path_0", "path_1", "fsdp_0", "fsdp_1"))
    in_specs = (
        P(PATH, None, FSDP, None),
        P(PATH, None, FSDP, None),
        P(None, None, FSDP, PATH),
        P(None, None, FSDP, PATH),
        P(),
        P(),
        P(),
    )
    out_specs = (
        P(PATH, None, FSDP, None),
        P(None, None, FSDP, PATH),
        P(None, None, FSDP, PATH),
        P(PATH, None, FSDP, None),
    )
    return jax.shard_map(
        on_device, mesh=finer, in_specs=in_specs, out_specs=out_specs, check_vma=False
    )
```

profile of v0, /device:TPU:1, one launch (start us, length us, event | category | flops | bytes accessed | tf_op | source)
XLA Modules:
  0.0 129.8 jit_solution(9711249741714412921)
XLA Ops:
  0.6 0.7 convert_element_type.42
  1.3 0.9 select_reduce_fusion
  2.2 0.7 convert_divide_fusion
  2.9 0.8 slice_bitcast_fusion.1
  3.7 0.8 subtract_convert_fusion
  4.7 3.7 %multiply_subtract_fusion = (f32[1,4,32,4096]{3,2,1,0:T(8,128)}, f32[1,4,32,4096]{3,2,1,0:T(8,128)S(1)}) fusion(f32[4]{0:T(128)S(1)} %get-tuple-element.45, f32[4]{0:T(128)S(1)} %get-tuple-element.46, pred[4]{0:T(512)(128)(4,1)S(1)} %broadcast_compare_fusion.2, f32[1,4,32,4096]{3,2,1,0:T(8,128)} %param.8, bf16[1,4,32,4096]{3,2,1,0:T(8,128)(2,1)} %param.7), kind=kLoop, calls=%fused_computation.1 | loop fusion | flops 4718592 | bytes 7340068 | tf_op jit(solution)/shard_map/sub | solution.py:61
  8.4 0.7 copy.105
  9.8 0.6 copy.91
  10.4 7.4 %all_to_all.28 = bf16[8,2,1,4,32,256]{5,0,4,3,2,1:T(8,128)(2,1)S(1)} all-to-all(bf16[8,2,1,4,32,256]{5,0,4,3,2,1:T(8,128)(2,1)S(1)} %copy.91), channel_id=1, replica_groups=mesh['path_0'=8,'path_1'=2,'fsdp_0'=4,'fsdp_1'=4] {'path_1'}, dimensions={1} | all-to-all | bytes 2097152 | tf_op jit(solution)/shard_map/all_to_all | solution.py:35
  17.9 1.1 copy.92
  18.9 34.2 %all_to_all.29 = bf16[8,2,1,4,32,256]{5,1,4,3,2,0:T(2,128)(2,1)S(1)} all-to-all(bf16[8,2,1,4,32,256]{5,1,4,3,2,0:T(2,128)(2,1)S(1)} %copy.92), channel_id=1, replica_groups=mesh['path_0'=8,'path_1'=2,'fsdp_0'=4,'fsdp_1'=4] {'path_0'}, dimensions={0} | all-to-all | bytes 2097152 | tf_op jit(solution)/shard_map/all_to_all | solution.py:35
  53.1 0.8 copy.93
  53.9 0.4 reshape_reshape.3
  54.8 10.7 %psum.28 = f32[4,2]{1,0:T(4,128)S(1)} all-reduce(f32[4,2]{1,0:T(4,128)S(1)} %get-tuple-element.43), channel_id=1, replica_groups=mesh['path_0'=8,'path_1'=2,'fsdp_0'=4,'fsdp_1'=4] {'path_0'}, use_global_device_ids=true, to_apply=%region_2.3 | all-reduce | flops 8 | bytes 64 | tf_op jit(solution)/shard_map/psum | solution.py:45
  65.5 7.9 %psum.29 = f32[4,2]{1,0:T(4,128)S(1)} all-reduce(f32[4,2]{1,0:T(4,128)S(1)} %psum.28), channel_id=1, replica_groups=mesh['path_0'=8,'path_1'=2,'fsdp_0'=4,'fsdp_1'=4] {'path_1'}, use_global_device_ids=true, to_apply=%region_3.4 | all-reduce | flops 8 | bytes 64 | tf_op jit(solution)/shard_map/psum | solution.py:45
  73.5 8.7 %psum.30 = f32[4,2]{1,0:T(4,128)S(1)} all-reduce(f32[4,2]{1,0:T(4,128)S(1)} %psum.29), channel_id=1, replica_groups=mesh['path_0'=8,'path_1'=2,'fsdp_0'=4,'fsdp_1'=4] {'fsdp_0'}, use_global_device_ids=true, to_apply=%region_4.5 | all-reduce | flops 8 | bytes 64 | tf_op jit(solution)/shard_map/psum | solution.py:45
  82.3 8.4 %psum.31 = f32[4,2]{1,0:T(4,128)S(1)} all-reduce(f32[4,2]{1,0:T(4,128)S(1)} %psum.30), channel_id=1, replica_groups=mesh['path_0'=8,'path_1'=2,'fsdp_0'=4,'fsdp_1'=4] {'fsdp_1'}, use_global_device_ids=true, to_apply=%region_5.6 | all-reduce | flops 8 | bytes 64 | tf_op jit(solution)/shard_map/psum | solution.py:45
  90.8 0.7 fusion.8
  91.7 1.1 broadcast_select_fusion
  92.8 8.0 %all-to-all-start.2 = ((bf16[16,4,32,256]{3,2,1,0:T(8,128)(2,1)}), bf16[16,4,32,256]{3,2,1,0:T(8,128)(2,1)S(1)}, u32[]{:S(2)}, u32[]{:S(2)}) async-start(bf16[16,4,32,256]{3,2,1,0:T(8,128)(2,1)} %broadcast_select_fusion), calls=%async_computation.2 | async-start | bytes 2097152 | tf_op jit(solution)/shard_map/all_to_all | solution.py:83
  100.8 0.7 copy.99
  101.5 0.7 copy.100
  102.3 26.5 %all-to-all-done.2 = bf16[16,4,32,256]{3,2,1,0:T(8,128)(2,1)S(1)} async-done(((bf16[16,4,32,256]{3,2,1,0:T(8,128)(2,1)}), bf16[16,4,32,256]{3,2,1,0:T(8,128)(2,1)S(1)}, u32[]{:S(2)}, u32[]{:S(2)}) %all-to-all-start.2) | async-done | bytes 1048608 | tf_op jit(solution)/shard_map/all_to_all | solution.py:83
  128.7 1.1 copy.104
  (20 shorter events, 1.8 us)
Async XLA Ops:
  53.1 1.3 copy-start.2
  53.9 11.6 %copy-start.3 = (s32[4,2]{0,1:T(2,128)S(1)}, s32[4,2]{0,1:T(2,128)}, u32[]{:S(2)}) copy-start(s32[4,2]{0,1:T(2,128)} %param.13) | copy-start | bytes 100
  53.9 36.8 %copy-start = (f32[4,2,32,256]{3,2,1,0:T(8,128)S(1)}, f32[4,2,32,256]{3,2,1,0:T(8,128)}, u32[]{:S(2)}) copy-start(f32[4,2,32,256]{3,2,1,0:T(8,128)} %param.10) | copy-start | bytes 786436
  53.9 36.8 %copy-start.1 = (f32[4,2,32,256]{3,2,1,0:T(8,128)S(1)}, f32[4,2,32,256]{3,2,1,0:T(8,128)}, u32[]{:S(2)}) copy-start(f32[4,2,32,256]{3,2,1,0:T(8,128)} %param.9) | copy-start | bytes 786436
  92.8 36.0 %all-to-all-start.2 = ((bf16[16,4,32,256]{3,2,1,0:T(8,128)(2,1)}), bf16[16,4,32,256]{3,2,1,0:T(8,128)(2,1)S(1)}, u32[]{:S(2)}, u32[]{:S(2)}) async-start(bf16[16,4,32,256]{3,2,1,0:T(8,128)(2,1)} %broadcast_select_fusion), calls=%async_computation.2 | async-start | bytes 2097152 | tf_op jit(solution)/shard_map/all_to_all | solution.py:83
where the time goes:
time: 130 us
  blocking collectives  77.3 us (59%)
  waiting for transfers between devices  26.5 us (20%)
  other arithmetic  8.95 us (7%)
  starting transfers between devices  8.03 us (6%)
  local copies, waits for them, and re-layouts  7.89 us (6%)
    all_to_all x2, blocking collectives, turned_blocks(): lax.all_to_all(parts, axes[k], split_axis=k, concat_axis=k, tiled=True)  41.6 us
    psum x4, blocking collectives, over_axes(): return functools.reduce(lax.psum, axes, x)  35.7 us
    all_to_all x1, waiting for transfers between devices, on_device(): lax.all_to_all(outgoing, PATH, split_axis=0, concat_axis=3, tiled=True)  26.5 us
    all_to_all x1, starting transfers between devices, on_device(): lax.all_to_all(outgoing, PATH, split_axis=0, concat_axis=3, tiled=True)  8.03 us
    sub x1, other arithmetic, on_device(): corrected - own_live[:, None, None] * (sent.astype(jnp.float32) / own_wei...  3.72 us
  transfers between devices with their start and end apart: 1, of which 1 were waited for; matrix products, arithmetic and copies ran while one was open for 1% of the time, Pallas kernels for 0%

commit v1 on v0

v1 whole, which is shorter than its diff:
```python
import jax
import jax.numpy as jnp
from jax import lax
from jax.experimental import pallas as pl
from jax.experimental.pallas import tpu as pltpu
from jax.sharding import Mesh
from jax.sharding import PartitionSpec as P

PATH = ("z", "core")
FSDP = ("y", "x")
PLANE = ("core", "y", "x")
CHIPS = 8
PATHS = 16
LEVELS = 4
SLABS = 8
BLOCK = 256

CLIP_RMS = 0.2
OUTER_RATE = 0.7
MOMENTUM_COEF = 0.9
EPSILON_SQ = 1e-06
CLIPPED_COEF = OUTER_RATE * (1.0 + MOMENTUM_COEF)
MOMENTUM_SHARE = OUTER_RATE * MOMENTUM_COEF * MOMENTUM_COEF

SMEM = pl.BlockSpec(memory_space=pltpu.SMEM)
VMEM = pl.BlockSpec(memory_space=pltpu.VMEM)


def place():
    z, core = lax.axis_index("z"), lax.axis_index("core")
    return z, core, 1 - 2 * core


def chip_at(z, sign, steps):
    return (z + sign * steps) & (CHIPS - 1)


def path_terms(l, routes, counts, flags, rows):
    z, core, _ = place()
    p = 2 * z + core
    own = routes[p, l]
    denom = jnp.int32(0)
    for q in range(PATHS):
        denom += jnp.where(routes[q, l] == own, counts[q, l], 0)
    shape = (rows, BLOCK)
    top = jnp.full(shape, counts[p, l], jnp.int32).astype(jnp.float32)
    bottom = jnp.full(shape, denom, jnp.int32).astype(jnp.float32)
    live = flags[l, own] == 0
    return top, bottom, live


def sent_kernel(routes, counts, flags, delta, feedback, keep, give):
    core = lax.axis_index("core")
    top, bottom, live = path_terms(pl.program_id(0), routes, counts, flags, delta.shape[1])
    weight = jnp.where(live, top / bottom, 0.0)
    for half, out in ((core, keep), (1 - core, give)):
        for block in range(CHIPS):
            at = pl.ds(pl.multiple_of((2 * block + half) * BLOCK, BLOCK), BLOCK)
            corrected = delta[0, :, at].astype(jnp.float32) + feedback[0, :, at]
            out[0, block] = (weight * corrected).astype(jnp.bfloat16)


def feedback_kernel(routes, counts, flags, delta, feedback, out):
    top, bottom, live = path_terms(pl.program_id(0), routes, counts, flags, delta.shape[1])
    weight = top / bottom
    back = jnp.where(live, bottom / top, 0.0)
    for block in range(2 * CHIPS):
        at = pl.ds(block * BLOCK, BLOCK)
        corrected = delta[0, :, at].astype(jnp.float32) + feedback[0, :, at]
        sent = (weight * corrected).astype(jnp.bfloat16).astype(jnp.float32)
        out[0, :, at] = corrected - sent * back


def pair_kernel(routes, flags, keep, got, params, momentum, plus, minus, hold):
    z, core, sign = place()
    own, sibling = 2 * z + core, 2 * z + 1 - core

    def write(out, slot, steps):
        q = chip_at(z, sign, steps)
        l, m = q >> 1, q & 1
        mine = jnp.where(routes[own, l] == m, 1.0, 0.0)
        other = jnp.where(routes[sibling, l] == m, 1.0, 0.0)
        for block in range(CHIPS):
            total = mine * keep[l, block].astype(jnp.float32) + other * got[l, block].astype(jnp.float32)
            out[slot, block] = total.astype(jnp.bfloat16)
        share = jnp.where(flags[l, m] > 0, 0.0, MOMENTUM_SHARE)
        out[slot, CHIPS] = (params[q] - share * momentum[q]).astype(jnp.bfloat16)

    for slot, steps in enumerate((1, -2, 3)):
        write(plus, slot, steps)
    for slot, steps in enumerate((-1, -4)):
        write(minus, slot, steps)
    for slot, steps in enumerate((0, -3, 2)):
        write(hold, slot, steps)


def owner_kernel(hold, plus, minus, near, far, average, base, partial):
    z, _, sign = place()
    squares = jnp.zeros(average.shape[1:], jnp.float32)
    for block in range(CHIPS):
        total = hold[0, block].astype(jnp.float32)
        for part in (plus[0, block], minus[0, block], near[block], far[block]):
            total += part.astype(jnp.float32)
        average[block] = total
        squares += total * total
    lanes = jnp.sum(squares, axis=0, keepdims=True)
    lanes = lanes[:, :128] + lanes[:, 128:]
    partial[...] = jnp.broadcast_to(lanes[None], partial.shape)
    for steps, part in (
        (0, hold[0, CHIPS]),
        (-1, plus[0, CHIPS]),
        (1, minus[0, CHIPS]),
        (-2, near[CHIPS]),
        (-3, near[CHIPS + 1]),
        (3, far[CHIPS]),
        (2, far[CHIPS + 1]),
        (4, far[CHIPS + 2]),
    ):
        base[chip_at(z, sign, steps)] = part


def new_kernel(entries, average, base, partials, far, near, own):
    z, _, sign = place()
    total = jnp.sum(jnp.sum(partials[...], axis=0), keepdims=True)
    factor = jnp.minimum(1.0, CLIP_RMS / jnp.sqrt(total / entries + EPSILON_SQ))
    for block in range(CHIPS):
        clipped = factor * average[block]
        new = (base[block].astype(jnp.float32) - CLIPPED_COEF * clipped).astype(jnp.bfloat16)
        far[block] = new
        near[block] = new
        own[block] = new
    for out, jumps in ((far, (3, 4, 2)), (near, (-2, -3)), (own, (0, 1, -1))):
        for slot, steps in enumerate(jumps):
            at = chip_at(z, sign, steps)
            out[CHIPS + slot] = (factor * average[at]).astype(jnp.bfloat16)


def slab_parts(own, near, far, plus, minus):
    return (
        (lambda b: own[b], own.at[CHIPS]),
        (lambda b: minus[0, b], minus.at[0, CHIPS]),
        (lambda b: near[b], near.at[CHIPS]),
        (lambda b: minus[2, b], minus.at[2, CHIPS]),
        (lambda b: plus[1, b], plus.at[1, CHIPS]),
        (lambda b: far[b], far.at[CHIPS]),
        (lambda b: minus[1, b], minus.at[1, CHIPS]),
        (lambda b: plus[0, b], plus.at[0, CHIPS]),
    )


def give_kernel(routes, own, near, far, plus, minus, out):
    z, core, sign = place()
    sibling = 2 * z + 1 - core
    parts = slab_parts(own, near, far, plus, minus)
    for l in range(LEVELS):
        at = ((2 * l + routes[sibling, l] - z) * sign) & (CHIPS - 1)
        for slot, (read, _) in enumerate(parts):

            @pl.when(at == slot)
            def _(l=l, read=read):
                for block in range(CHIPS):
                    out[l, block] = read(block)


def state_kernel(flags, own, near, far, plus, minus, params, momentum, momentum_out, params_out):
    z, _, sign = place()
    parts = slab_parts(own, near, far, plus, minus)
    for slot, (_, ref) in enumerate(parts):
        q = chip_at(z, sign, slot)
        skipped = flags[q >> 1, q & 1] > 0
        clipped = ref[...].astype(jnp.float32)
        before, old = momentum[q], params[q]
        after = jnp.where(skipped, before, MOMENTUM_COEF * before + clipped)
        momentum_out[q] = after
        new = old - OUTER_RATE * (clipped + MOMENTUM_COEF * after)
        params_out[q] = jnp.where(skipped, old, new)


def join_kernel(routes, own, near, far, plus, minus, got, out):
    z, core, sign = place()
    path = 2 * z + core
    parts = slab_parts(own, near, far, plus, minus)
    for l in range(LEVELS):
        at = ((2 * l + routes[path, l] - z) * sign) & (CHIPS - 1)
        for slot, (read, _) in enumerate(parts):

            @pl.when(at == slot)
            def _(l=l, read=read):
                for block in range(CHIPS):
                    out[l, :, pl.ds(pl.multiple_of((2 * block + core) * BLOCK, BLOCK), BLOCK)] = read(block)

        for block in range(CHIPS):
            out[l, :, pl.ds(pl.multiple_of((2 * block + 1 - core) * BLOCK, BLOCK), BLOCK)] = got[l, block]


def cost(bytes_accessed):
    return pl.CostEstimate(flops=0, bytes_accessed=bytes_accessed, transcendentals=0)


def call(kernel, outs, args, scalars):
    shapes = [jax.ShapeDtypeStruct(s, d) for s, d in outs]
    size = sum(a.size * a.dtype.itemsize for a in args) + sum(s.size * s.dtype.itemsize for s in shapes)
    return pl.pallas_call(
        kernel,
        out_shape=shapes,
        in_specs=[SMEM] * scalars + [VMEM] * (len(args) - scalars),
        out_specs=[VMEM] * len(shapes),
        cost_estimate=cost(size),
        compiler_params=pltpu.CompilerParams(vmem_limit_bytes=24 * 2**20),
    )(*args)


def levelwise(kernel, outs, routes, counts, flags, delta, feedback):
    shapes = [jax.ShapeDtypeStruct(s, d) for s, d in outs]

    def one(shape):
        return pl.BlockSpec((1, *shape[1:]), lambda l: (l, *[0] * (len(shape) - 1)))

    size = delta.size * 6 + sum(s.size * s.dtype.itemsize for s in shapes)
    return pl.pallas_call(
        kernel,
        grid=(LEVELS,),
        out_shape=shapes,
        in_specs=[SMEM] * 3 + [one(delta.shape), one(feedback.shape)],
        out_specs=[one(s.shape) for s in shapes],
        cost_estimate=cost(size),
        compiler_params=pltpu.CompilerParams(vmem_limit_bytes=24 * 2**20),
    )(routes, counts, flags, delta, feedback)


def jump(x, steps):
    def target(p):
        z, core = divmod(p, 2)
        sign = 1 - 2 * core
        return 2 * ((z + sign * steps) % CHIPS) + core

    return lax.ppermute(x, PATH, [(p, target(p)) for p in range(PATHS)])


def swap(x):
    return lax.ppermute(x, "core", [(0, 1), (1, 0)])


def on_device(path_delta, feedback, global_params, momentum, routes, token_counts, skip_flags):
    delta, feedback = path_delta[0], feedback[0]
    rows = delta.shape[1]
    params = global_params.reshape(SLABS, rows, BLOCK)
    momentum = momentum.reshape(SLABS, rows, BLOCK)
    f32, bf16 = jnp.float32, jnp.bfloat16
    half = (LEVELS, CHIPS, rows, BLOCK)

    keep, give = levelwise(sent_kernel, [(half, bf16)] * 2, routes, token_counts, skip_flags, delta, feedback)
    got = swap(give)
    plus, minus, hold = call(
        pair_kernel,
        [((n, CHIPS + 1, rows, BLOCK), bf16) for n in (3, 2, 3)],
        (routes, skip_flags, keep, got, params, momentum),
        2,
    )
    plus = jump(plus, 1)
    minus = jump(minus, -1)
    (feedback_next,) = levelwise(
        feedback_kernel, [(delta.shape, f32)], routes, token_counts, skip_flags, delta, feedback
    )
    near = jnp.concatenate([hold[2, :CHIPS] + plus[2, :CHIPS], hold[2, CHIPS:], plus[2, CHIPS:]])
    near = jump(near, 2)
    far = jnp.concatenate(
        [
            hold[1, :CHIPS] + plus[1, :CHIPS] + minus[1, :CHIPS],
            hold[1, CHIPS:],
            plus[1, CHIPS:],
            minus[1, CHIPS:],
        ]
    )
    far = jump(far, -3)
    plane = lax.axis_size(PLANE)
    average, base, partial = call(
        owner_kernel,
        [((CHIPS, rows, BLOCK), f32), ((CHIPS, rows, BLOCK), bf16), ((plane, 1, 128), f32)],
        (hold, plus, minus, near, far),
        0,
    )
    partials = lax.all_to_all(partial, PLANE, 0, 0)
    entries = rows * lax.axis_size(FSDP) * CHIPS * 2 * BLOCK

    def fresh(*refs):
        new_kernel(entries, *refs)

    far, near, own = call(
        fresh,
        [((CHIPS + n, rows, BLOCK), bf16) for n in (3, 2, 3)],
        (average, base, partials),
        0,
    )
    far = jump(far, 3)
    near = jump(near, -2)
    one = CHIPS + 1
    plus = jnp.stack(
        [
            jnp.concatenate([own[:CHIPS], own[one : one + 1]]),
            jnp.concatenate([far[:CHIPS], far[one : one + 1]]),
        ]
    )
    plus = jump(plus, 1)
    minus = jnp.stack(
        [
            jnp.concatenate([own[:CHIPS], own[one + 1 :]]),
            jnp.concatenate([far[:CHIPS], far[one + 1 :]]),
            jnp.concatenate([near[:CHIPS], near[one:]]),
        ]
    )
    minus = jump(minus, -1)
    slabs = (own, near, far, plus, minus)
    (give,) = call(give_kernel, [(half, bf16)], (routes, *slabs), 1)
    got = swap(give)
    momentum_next, params_next = call(
        state_kernel, [(params.shape, f32)] * 2, (skip_flags, *slabs, params, momentum), 1
    )
    (path_params,) = call(join_kernel, [(delta.shape, bf16)], (routes, *slabs, got), 1)
    shape = global_params.shape
    return feedback_next[None], momentum_next.reshape(shape), params_next.reshape(shape), path_params[None]


def solution(mesh):
    finer = Mesh(mesh.devices.reshape(8, 2, 4, 4), (*PATH, *FSDP))
    by_path, by_column = P(PATH, None, FSDP, None), P(None, None, FSDP, PATH)
    return jax.shard_map(
        on_device,
        mesh=finer,
        in_specs=(by_path, by_path, by_column, by_column, P(), P(), P()),
        out_specs=(by_path, by_column, by_column, by_path),
        check_vma=False,
    )
```

time: 130 us -> 89.3 us (0.69)
  blocking collectives: 77.3 us -> 14.1 us
  starting transfers between devices: 8.03 us -> 22 us
  waiting for transfers between devices: 26.5 us -> 36.8 us
  Pallas kernels: 0 us -> 9.9 us
  other arithmetic: 8.95 us -> 0.25 us
  local copies, waits for them, and re-layouts: 7.89 us -> 5.16 us
    ppermute x0 -> x10, waiting for transfers between devices: none -> 36.8 us  [the longest x8 35.3 us: jump(): return lax.ppermute(x, PATH, [(p, target(p)) for p in range(PATHS)])]
    psum x4 -> x0, blocking collectives: 35.7 us -> none  [over_axes(): return functools.reduce(lax.psum, axes, x)]
    all_to_all x2 -> x1, blocking collectives: 41.6 us -> 14.1 us  [on_device(): partials = lax.all_to_all(partial, PLANE, 0, 0)]
    all_to_all x1 -> x0, waiting for transfers between devices: 26.5 us -> none  [on_device(): lax.all_to_all(outgoing, PATH, split_axis=0, concat_axis=3, tiled=True)]
    ppermute x0 -> x10, starting transfers between devices: none -> 22 us  [the longest x8 16.1 us: jump(): return lax.ppermute(x, PATH, [(p, target(p)) for p in range(PATHS)])]
    pallas_call x0 -> x8, Pallas kernels: none -> 9.9 us  [the longest x6 5.66 us: call(): pl.pallas_call(kernel, out_shape=shapes, in_specs=[SMEM] * scalars + [VME...]
    all_to_all x1 -> x0, starting transfers between devices: 8.03 us -> none  [on_device(): lax.all_to_all(outgoing, PATH, split_axis=0, concat_axis=3, tiled=True)]
    sub x1 -> x0, other arithmetic: 3.72 us -> none  [on_device(): corrected - own_live[:, None, None] * (sent.astype(jnp.float32) / own_wei...]
  transfers between devices with their start and end apart: 1 -> 10, of which waited for: 1 -> 7; matrix products, arithmetic and copies ran while one was open for 1% -> 0% of each run, Pallas kernels for 0% -> 5%
where the time goes in v1:
time: 89.3 us; the launch traced here: 89.1 us
  waiting for transfers between devices  36.8 us (41%)
  starting transfers between devices  22 us (25%)
  blocking collectives  14.1 us (16%)
  Pallas kernels  9.9 us (11%)
  local copies, waits for them, and re-layouts  5.16 us (6%)
    ppermute x8, waiting for transfers between devices, jump(): return lax.ppermute(x, PATH, [(p, target(p)) for p in range(PATHS)])  35.3 us
    ppermute x8, starting transfers between devices, jump(): return lax.ppermute(x, PATH, [(p, target(p)) for p in range(PATHS)])  16.1 us
    all_to_all x1, blocking collectives, on_device(): partials = lax.all_to_all(partial, PLANE, 0, 0)  14.1 us
    ppermute x2, starting transfers between devices, swap(): return lax.ppermute(x, 'core', [(0, 1), (1, 0)])  5.95 us
    pallas_call x6, Pallas kernels, call(): pl.pallas_call(kernel, out_shape=shapes, in_specs=[SMEM] * scalars + [VME...  5.66 us
    unnamed x15, local copies, waits for them, and re-layouts  5.12 us
    pallas_call x2, Pallas kernels, levelwise(): pl.pallas_call(kernel, grid=(LEVELS,), out_shape=shapes, in_specs=[SMEM]...  4.24 us
  transfers between devices with their start and end apart: 10, of which 7 were waited for; matrix products, arithmetic and copies ran while one was open for 0% of the time, Pallas kernels for 5%

profile of v1, /device:TPU:1, one launch (start us, length us, event | category | flops | bytes accessed | tf_op | source)
XLA Modules:
  0.0 89.1 jit_solution(17086240386382866472)
XLA Ops:
  0.6 0.8 copy.13.flags
  2.9 1.6 %copy-done = f32[1,4,32,4096]{3,2,1,0:T(8,128)S(1)} copy-done((f32[1,4,32,4096]{3,2,1,0:T(8,128)S(1)}, f32[1,4,32,4096]{3,2,1,0:T(8,128)}, u32[]{:S(2)}) %copy-start) | copy-done | bytes 2097176
  4.5 1.2 %copy-done.2 = bf16[1,4,32,4096]{3,2,1,0:T(8,128)(2,1)S(1)} copy-done((bf16[1,4,32,4096]{3,2,1,0:T(8,128)(2,1)S(1)}, bf16[1,4,32,4096]{3,2,1,0:T(8,128)(2,1)}, u32[]{:S(2)}) %copy-start.2) | copy-done | bytes 1048600
  5.7 1.4 %shard_map.103 = (bf16[4,8,32,256]{3,2,1,0:T(8,128)(2,1)S(1)}, bf16[4,8,32,256]{3,2,1,0:T(8,128)(2,1)S(1)}) custom-call(s32[16,4]{1,0:T(8,128)S(1)} %copy.11.routes, s32[16,4]{1,0:T(8,128)S(1)} %copy.12.counts, s32[4,2]{1,0:T(4,128)S(1)} %copy.13.flags, bf16[4,32,4096]{2,1,0:T(8,128)(2,1)S(1)} %bitcast.34, f32[4,32,4096]{2,1,0:T(8,128)S(1)} %bitcast.32), custom_call_target="tpu_custom_call" | custom-call | bytes 4194304 | tf_op jit(solution)/shard_map/pallas_call | solution.py:220
  7.1 3.3 %collective-permute-start = (bf16[4,8,32,256]{3,2,1,0:T(8,128)(2,1)S(1)}, bf16[4,8,32,256]{3,2,1,0:T(8,128)(2,1)S(1)}, u32[]{:S(2)}, u32[]{:S(2)}) collective-permute-start(bf16[4,8,32,256]{3,2,1,0:T(8,128)(2,1)S(1)} %get-tuple-element.18), channel_id=1, source_target_pairs={{0,16},{16,0},{1,17},{17,1},{2,18},{18,2},{3,19},{19,3},{4,20},{20... | collective-permute-start | bytes 1572872 | tf_op jit(solution)/shard_map/ppermute | solution.py:241
  10.4 1.5 %collective-permute-done.got = bf16[4,8,32,256]{3,2,1,0:T(8,128)(2,1)S(1)} collective-permute-done((bf16[4,8,32,256]{3,2,1,0:T(8,128)(2,1)S(1)}, bf16[4,8,32,256]{3,2,1,0:T(8,128)(2,1)S(1)}, u32[]{:S(2)}, u32[]{:S(2)}) %collective-permute-start) | collective-permute-done | bytes 524320 | tf_op jit(solution)/shard_map/ppermute | solution.py:241
  12.0 1.1 %shard_map.104 = (bf16[3,9,32,256]{3,2,1,0:T(8,128)(2,1)S(1)}, bf16[2,9,32,256]{3,2,1,0:T(8,128)(2,1)S(1)}, bf16[3,9,32,256]{3,2,1,0:T(8,128)(2,1)S(1)}) custom-call(s32[16,4]{1,0:T(8,128)S(1)} %copy.11.routes, s32[4,2]{1,0:T(4,128)S(1)} %copy.13.flags, bf16[4,8,32,256]{3,2,1,0:T(8,128)(2,1)S(1)} %get-tuple-element.17.keep, ...), custom_call_target="tpu_custom_call" | custom-call | bytes 2752800 | tf_op jit(solution)/shard_map/pallas_call | solution.py:203
  13.2 3.9 %collective-permute-start.1 = (bf16[3,9,32,256]{3,2,1,0:T(8,128)(2,1)S(1)}, bf16[3,9,32,256]{3,2,1,0:T(8,128)(2,1)S(1)}, u32[]{:S(2)}, u32[]{:S(2)}) collective-permute-start(bf16[3,9,32,256]{3,2,1,0:T(8,128)(2,1)S(1)} %get-tuple-element.20), channel_id=1, source_target_pairs={{0,32},{16,240},{32,64},{48,16},{64,96},{80,48},{96,128},{112,80},... | collective-permute-start | bytes 1327112 | tf_op jit(solution)/shard_map/ppermute | solution.py:237
  17.1 4.0 %collective-permute-done.2.minus = bf16[2,9,32,256]{3,2,1,0:T(8,128)(2,1)S(1)} collective-permute-done((bf16[2,9,32,256]{3,2,1,0:T(8,128)(2,1)S(1)}, bf16[2,9,32,256]{3,2,1,0:T(8,128)(2,1)S(1)}, u32[]{:S(2)}, u32[]{:S(2)}) %collective-permute-start.2) | collective-permute-done | bytes 294944 | tf_op jit(solution)/shard_map/ppermute | solution.py:237
  21.1 4.4 %collective-permute-done.1.plus = bf16[3,9,32,256]{3,2,1,0:T(8,128)(2,1)S(1)} collective-permute-done((bf16[3,9,32,256]{3,2,1,0:T(8,128)(2,1)S(1)}, bf16[3,9,32,256]{3,2,1,0:T(8,128)(2,1)S(1)}, u32[]{:S(2)}, u32[]{:S(2)}) %collective-permute-start.1) | collective-permute-done | bytes 442400 | tf_op jit(solution)/shard_map/ppermute | solution.py:237
  25.6 2.7 %collective-permute-start.4 = (bf16[11,32,256]{2,1,0:T(8,128)(2,1)S(1)}, bf16[11,32,256]{2,1,0:T(8,128)(2,1)S(1)}, u32[]{:S(2)}, u32[]{:S(2)}) collective-permute-start(bf16[11,32,256]{2,1,0:T(8,128)(2,1)S(1)} %pad_maximum_fusion.2), channel_id=1, source_target_pairs={{0,160},{16,112},{32,192},{48,144},{64,224},{80,176},{96,0},{112,2... | collective-permute-start | bytes 540680 | tf_op jit(solution)/shard_map/ppermute | solution.py:237
  28.8 12.0 %collective-permute-done.3.near = bf16[10,32,256]{2,1,0:T(8,128)(2,1)S(1)} collective-permute-done((bf16[10,32,256]{2,1,0:T(8,128)(2,1)S(1)}, bf16[10,32,256]{2,1,0:T(8,128)(2,1)S(1)}, u32[]{:S(2)}, u32[]{:S(2)}) %collective-permute-start.3) | collective-permute-done | bytes 163872 | tf_op jit(solution)/shard_map/ppermute | solution.py:237
  41.0 14.1 %all_to_all.5.refs_2_ = f32[32,1,128]{2,1,0:T(1,128)S(1)} all-to-all(f32[32,1,128]{2,1,0:T(1,128)S(1)} %get-tuple-element.24), channel_id=1, replica_groups=mesh['z'=8,'core'=2,'y'=4,'x'=4] {'core','y','x'}, dimensions={0} | all-to-all | bytes 32768 | tf_op jit(solution)/shard_map/all_to_all | solution.py:283
  55.6 4.9 %collective-permute-start.6 = (bf16[11,32,256]{2,1,0:T(8,128)(2,1)S(1)}, bf16[11,32,256]{2,1,0:T(8,128)(2,1)S(1)}, u32[]{:S(2)}, u32[]{:S(2)}) collective-permute-start(bf16[11,32,256]{2,1,0:T(8,128)(2,1)S(1)} %get-tuple-element.27), channel_id=1, source_target_pairs={{0,96},{16,176},{32,128},{48,208},{64,160},{80,240},{96,192},{112,... | collective-permute-start | bytes 540680 | tf_op jit(solution)/shard_map/ppermute | solution.py:237
  60.5 1.3 %collective-permute-done.5.near = bf16[10,32,256]{2,1,0:T(8,128)(2,1)S(1)} collective-permute-done((bf16[10,32,256]{2,1,0:T(8,128)(2,1)S(1)}, bf16[10,32,256]{2,1,0:T(8,128)(2,1)S(1)}, u32[]{:S(2)}, u32[]{:S(2)}) %collective-permute-start.5) | collective-permute-done | bytes 163872 | tf_op jit(solution)/shard_map/ppermute | solution.py:237
  61.9 5.8 %collective-permute-done.6.far = bf16[11,32,256]{2,1,0:T(8,128)(2,1)S(1)} collective-permute-done((bf16[11,32,256]{2,1,0:T(8,128)(2,1)S(1)}, bf16[11,32,256]{2,1,0:T(8,128)(2,1)S(1)}, u32[]{:S(2)}, u32[]{:S(2)}) %collective-permute-start.6) | collective-permute-done | bytes 180256 | tf_op jit(solution)/shard_map/ppermute | solution.py:237
  67.8 2.1 %collective-permute-start.8 = (bf16[3,9,32,256]{3,2,1,0:T(8,128)(2,1)S(1)}, bf16[3,9,32,256]{3,2,1,0:T(8,128)(2,1)S(1)}, u32[]{:S(2)}, u32[]{:S(2)}) collective-permute-start(bf16[3,9,32,256]{3,2,1,0:T(8,128)(2,1)S(1)} %pad_maximum_fusion), channel_id=1, source_target_pairs={{0,224},{16,48},{32,0},{48,80},{64,32},{80,112},{96,64},{112,144},... | collective-permute-start | bytes 1327112 | tf_op jit(solution)/shard_map/ppermute | solution.py:237
  69.9 1.7 %collective-permute-start.7 = (bf16[2,9,32,256]{3,2,1,0:T(8,128)(2,1)S(1)}, bf16[2,9,32,256]{3,2,1,0:T(8,128)(2,1)S(1)}, u32[]{:S(2)}, u32[]{:S(2)}) collective-permute-start(bf16[2,9,32,256]{3,2,1,0:T(8,128)(2,1)S(1)} %pad_maximum_fusion.1), channel_id=1, source_target_pairs={{0,32},{16,240},{32,64},{48,16},{64,96},{80,48},{96,128},{112,80},... | collective-permute-start | bytes 884744 | tf_op jit(solution)/shard_map/ppermute | solution.py:237
  71.7 7.7 %collective-permute-done.7.plus = bf16[2,9,32,256]{3,2,1,0:T(8,128)(2,1)S(1)} collective-permute-done((bf16[2,9,32,256]{3,2,1,0:T(8,128)(2,1)S(1)}, bf16[2,9,32,256]{3,2,1,0:T(8,128)(2,1)S(1)}, u32[]{:S(2)}, u32[]{:S(2)}) %collective-permute-start.7) | collective-permute-done | bytes 294944 | tf_op jit(solution)/shard_map/ppermute | solution.py:237
  79.4 0.9 shard_map.108
  80.2 2.6 %collective-permute-start.9 = (bf16[4,8,32,256]{3,2,1,0:T(8,128)(2,1)S(1)}, bf16[4,8,32,256]{3,2,1,0:T(8,128)(2,1)S(1)}, u32[]{:S(2)}, u32[]{:S(2)}) collective-permute-start(bf16[4,8,32,256]{3,2,1,0:T(8,128)(2,1)S(1)} %shard_map.108), channel_id=1, source_target_pairs={{0,16},{16,0},{1,17},{17,1},{2,18},{18,2},{3,19},{19,3},{4,20},{20... | collective-permute-start | bytes 1572872 | tf_op jit(solution)/shard_map/ppermute | solution.py:241
  82.9 2.9 %shard_map.102 = f32[4,32,4096]{2,1,0:T(8,128)} custom-call(s32[16,4]{1,0:T(8,128)S(1)} %copy.11.routes, s32[16,4]{1,0:T(8,128)S(1)} %copy.12.counts, s32[4,2]{1,0:T(4,128)S(1)} %copy.13.flags, bf16[4,32,4096]{2,1,0:T(8,128)(2,1)S(1)} %bitcast.35, f32[4,32,4096]{2,1,0:T(8,128)S(1)} %bitcast.33), custom_call_target="tpu_custom_call" | custom-call | bytes 5242880 | tf_op jit(solution)/shard_map/pallas_call | solution.py:220
  85.7 1.5 %shard_map.107 = (f32[8,32,256]{2,1,0:T(8,128)}, f32[8,32,256]{2,1,0:T(8,128)}) custom-call(s32[4,2]{1,0:T(4,128)S(1)} %copy.13.flags, bf16[11,32,256]{2,1,0:T(8,128)(2,1)S(1)} %get-tuple-element.25.own, bf16[10,32,256]{2,1,0:T(8,128)(2,1)S(1)} %collective-permute-done.5.near, bf16[11,32,256]{2,1,0:T(8,128)(2,1)S(1)} %collective-permute-done.6.far, ...), custom_call_target="tpu_custom_call" | custom-call | bytes 2310176 | tf_op jit(solution)/shard_map/pallas_call | solution.py:203
  87.2 1.9 %shard_map.109 = bf16[4,32,4096]{2,1,0:T(8,128)(2,1)} custom-call(s32[16,4]{1,0:T(8,128)S(1)} %copy.11.routes, bf16[11,32,256]{2,1,0:T(8,128)(2,1)S(1)} %get-tuple-element.25.own, bf16[10,32,256]{2,1,0:T(8,128)(2,1)S(1)} %collective-permute-done.5.near, bf16[11,32,256]{2,1,0:T(8,128)(2,1)S(1)} %collective-permute-done.6.far, ...), custom_call_target="tpu_custom_call" | custom-call | bytes 2834688 | tf_op jit(solution)/shard_map/pallas_call | solution.py:203
  (37 shorter events, 2.9 us)
Async XLA Ops:
  2.9 1.6 %copy-start = (f32[1,4,32,4096]{3,2,1,0:T(8,128)S(1)}, f32[1,4,32,4096]{3,2,1,0:T(8,128)}, u32[]{:S(2)}) copy-start(f32[1,4,32,4096]{3,2,1,0:T(8,128)} %param.8) | copy-start | bytes 6291460
  4.5 1.2 %copy-start.2 = (bf16[1,4,32,4096]{3,2,1,0:T(8,128)(2,1)S(1)}, bf16[1,4,32,4096]{3,2,1,0:T(8,128)(2,1)}, u32[]{:S(2)}) copy-start(bf16[1,4,32,4096]{3,2,1,0:T(8,128)(2,1)} %param.7) | copy-start | bytes 3145732
  5.7 6.3 %copy-start.4 = (f32[4,2,32,256]{3,2,1,0:T(8,128)S(1)}, f32[4,2,32,256]{3,2,1,0:T(8,128)}, u32[]{:S(2)}) copy-start(f32[4,2,32,256]{3,2,1,0:T(8,128)} %param.9) | copy-start | bytes 786436
  5.7 6.3 %copy-start.5 = (f32[4,2,32,256]{3,2,1,0:T(8,128)S(1)}, f32[4,2,32,256]{3,2,1,0:T(8,128)}, u32[]{:S(2)}) copy-start(f32[4,2,32,256]{3,2,1,0:T(8,128)} %param.10) | copy-start | bytes 786436
  7.1 4.9 %collective-permute-start = (bf16[4,8,32,256]{3,2,1,0:T(8,128)(2,1)S(1)}, bf16[4,8,32,256]{3,2,1,0:T(8,128)(2,1)S(1)}, u32[]{:S(2)}, u32[]{:S(2)}) collective-permute-start(bf16[4,8,32,256]{3,2,1,0:T(8,128)(2,1)S(1)} %get-tuple-element.18), channel_id=1, source_target_pairs={{0,16},{16,0},{1,17},{17,1},{2,18},{18,2},{3,19},{19,3},{4,20},{20... | collective-permute-start | bytes 1572872 | tf_op jit(solution)/shard_map/ppermute | solution.py:241
  13.1 8.0 %collective-permute-start.2 = (bf16[2,9,32,256]{3,2,1,0:T(8,128)(2,1)S(1)}, bf16[2,9,32,256]{3,2,1,0:T(8,128)(2,1)S(1)}, u32[]{:S(2)}, u32[]{:S(2)}) collective-permute-start(bf16[2,9,32,256]{3,2,1,0:T(8,128)(2,1)S(1)} %get-tuple-element.21), channel_id=1, source_target_pairs={{0,224},{16,48},{32,0},{48,80},{64,32},{80,112},{96,64},{112,144},... | collective-permute-start | bytes 884744 | tf_op jit(solution)/shard_map/ppermute | solution.py:237
  13.2 12.3 %collective-permute-start.1 = (bf16[3,9,32,256]{3,2,1,0:T(8,128)(2,1)S(1)}, bf16[3,9,32,256]{3,2,1,0:T(8,128)(2,1)S(1)}, u32[]{:S(2)}, u32[]{:S(2)}) collective-permute-start(bf16[3,9,32,256]{3,2,1,0:T(8,128)(2,1)S(1)} %get-tuple-element.20), channel_id=1, source_target_pairs={{0,32},{16,240},{32,64},{48,16},{64,96},{80,48},{96,128},{112,80},... | collective-permute-start | bytes 1327112 | tf_op jit(solution)/shard_map/ppermute | solution.py:237
  25.6 15.2 %collective-permute-start.4 = (bf16[11,32,256]{2,1,0:T(8,128)(2,1)S(1)}, bf16[11,32,256]{2,1,0:T(8,128)(2,1)S(1)}, u32[]{:S(2)}, u32[]{:S(2)}) collective-permute-start(bf16[11,32,256]{2,1,0:T(8,128)(2,1)S(1)} %pad_maximum_fusion.2), channel_id=1, source_target_pairs={{0,160},{16,112},{32,192},{48,144},{64,224},{80,176},{96,0},{112,2... | collective-permute-start | bytes 540680 | tf_op jit(solution)/shard_map/ppermute | solution.py:237
  28.3 12.5 %collective-permute-start.3 = (bf16[10,32,256]{2,1,0:T(8,128)(2,1)S(1)}, bf16[10,32,256]{2,1,0:T(8,128)(2,1)S(1)}, u32[]{:S(2)}, u32[]{:S(2)}) collective-permute-start(bf16[10,32,256]{2,1,0:T(8,128)(2,1)S(1)} %pad_maximum_fusion.3), channel_id=1, source_target_pairs={{0,64},{16,208},{32,96},{48,240},{64,128},{80,16},{96,160},{112,48... | collective-permute-start | bytes 491528 | tf_op jit(solution)/shard_map/ppermute | solution.py:237
  55.3 6.5 %collective-permute-start.5 = (bf16[10,32,256]{2,1,0:T(8,128)(2,1)S(1)}, bf16[10,32,256]{2,1,0:T(8,128)(2,1)S(1)}, u32[]{:S(2)}, u32[]{:S(2)}) collective-permute-start(bf16[10,32,256]{2,1,0:T(8,128)(2,1)S(1)} %get-tuple-element.26), channel_id=1, source_target_pairs={{0,192},{16,80},{32,224},{48,112},{64,0},{80,144},{96,32},{112,176... | collective-permute-start | bytes 491528 | tf_op jit(solution)/shard_map/ppermute | solution.py:237
  55.6 12.1 %collective-permute-start.6 = (bf16[11,32,256]{2,1,0:T(8,128)(2,1)S(1)}, bf16[11,32,256]{2,1,0:T(8,128)(2,1)S(1)}, u32[]{:S(2)}, u32[]{:S(2)}) collective-permute-start(bf16[11,32,256]{2,1,0:T(8,128)(2,1)S(1)} %get-tuple-element.27), channel_id=1, source_target_pairs={{0,96},{16,176},{32,128},{48,208},{64,160},{80,240},{96,192},{112,... | collective-permute-start | bytes 540680 | tf_op jit(solution)/shard_map/ppermute | solution.py:237
  61.8 21.0 %copy-start.1 = (f32[1,4,32,4096]{3,2,1,0:T(8,128)S(1)}, f32[1,4,32,4096]{3,2,1,0:T(8,128)}, u32[]{:S(2)}) copy-start(f32[1,4,32,4096]{3,2,1,0:T(8,128)} %param.8) | copy-start | bytes 6291460
  61.9 21.0 %copy-start.3 = (bf16[1,4,32,4096]{3,2,1,0:T(8,128)(2,1)S(1)}, bf16[1,4,32,4096]{3,2,1,0:T(8,128)(2,1)}, u32[]{:S(2)}) copy-start(bf16[1,4,32,4096]{3,2,1,0:T(8,128)(2,1)} %param.7) | copy-start | bytes 3145732
  67.8 11.6 %collective-permute-start.8 = (bf16[3,9,32,256]{3,2,1,0:T(8,128)(2,1)S(1)}, bf16[3,9,32,256]{3,2,1,0:T(8,128)(2,1)S(1)}, u32[]{:S(2)}, u32[]{:S(2)}) collective-permute-start(bf16[3,9,32,256]{3,2,1,0:T(8,128)(2,1)S(1)} %pad_maximum_fusion), channel_id=1, source_target_pairs={{0,224},{16,48},{32,0},{48,80},{64,32},{80,112},{96,64},{112,144},... | collective-permute-start | bytes 1327112 | tf_op jit(solution)/shard_map/ppermute | solution.py:237
  69.9 9.4 %collective-permute-start.7 = (bf16[2,9,32,256]{3,2,1,0:T(8,128)(2,1)S(1)}, bf16[2,9,32,256]{3,2,1,0:T(8,128)(2,1)S(1)}, u32[]{:S(2)}, u32[]{:S(2)}) collective-permute-start(bf16[2,9,32,256]{3,2,1,0:T(8,128)(2,1)S(1)} %pad_maximum_fusion.1), channel_id=1, source_target_pairs={{0,32},{16,240},{32,64},{48,16},{64,96},{80,48},{96,128},{112,80},... | collective-permute-start | bytes 884744 | tf_op jit(solution)/shard_map/ppermute | solution.py:237
  80.2 6.9 %collective-permute-start.9 = (bf16[4,8,32,256]{3,2,1,0:T(8,128)(2,1)S(1)}, bf16[4,8,32,256]{3,2,1,0:T(8,128)(2,1)S(1)}, u32[]{:S(2)}, u32[]{:S(2)}) collective-permute-start(bf16[4,8,32,256]{3,2,1,0:T(8,128)(2,1)S(1)} %shard_map.108), channel_id=1, source_target_pairs={{0,16},{16,0},{1,17},{17,1},{2,18},{18,2},{3,19},{19,3},{4,20},{20... | collective-permute-start | bytes 1572872 | tf_op jit(solution)/shard_map/ppermute | solution.py:241

commit v2 on v0

v2 whole, which is shorter than its diff:
```python
import jax
import jax.numpy as jnp
from jax import lax
from jax.experimental import pallas as pl
from jax.experimental.pallas import tpu as pltpu
from jax.sharding import Mesh
from jax.sharding import PartitionSpec as P

PATH = ("z", "core")
FSDP = ("y", "x")
CHIPS = 8
PATHS = 16
LEVELS = 4
MODULES = 8
BLOCK = 256

CLIP_RMS = 0.2
OUTER_RATE = 0.7
MOMENTUM_COEF = 0.9
EPSILON_SQ = 1e-06
CLIPPED_COEF = OUTER_RATE * (1.0 + MOMENTUM_COEF)
MOMENTUM_SHARE = OUTER_RATE * MOMENTUM_COEF * MOMENTUM_COEF

OWN_UPPER, SIBLING_UPPER, SKIPPED, WEIGHT, BACK, TABLE = 0, 4, 8, 16, 20, 24

VMEM = pl.BlockSpec(memory_space=pltpu.VMEM)
HBM = pl.BlockSpec(memory_space=pltpu.HBM)


def place():
    z, core = lax.axis_index("z"), lax.axis_index("core")
    return z, core, 1 - 2 * core


def chip_at(z, sign, steps):
    return (z + sign * steps) & (CHIPS - 1)


def send_half(weight, delta, feedback, half, out):
    for block in range(CHIPS):
        at = pl.ds(pl.multiple_of((2 * block + half) * BLOCK, BLOCK), BLOCK)
        corrected = delta[:, at].astype(jnp.float32) + feedback[:, at]
        out[block] = (weight * corrected).astype(jnp.bfloat16)


def give_kernel(routes_hbm, counts_hbm, flags_hbm, delta, feedback, give, table, *scratch):
    routes, counts, flags, delta_in, feedback_in, sems, table_sems = scratch
    _, rows, _ = delta.shape
    z, core, _ = place()
    path, sibling = 2 * z + core, 2 * z + 1 - core
    small = [
        pltpu.make_async_copy(src, dst, table_sems.at[i])
        for i, (src, dst) in enumerate(((routes_hbm, routes), (counts_hbm, counts), (flags_hbm, flags)))
    ]
    for copy in small:
        copy.start()
    copies = [
        (
            pltpu.make_async_copy(delta.at[l], delta_in.at[l], sems.at[0, l]),
            pltpu.make_async_copy(feedback.at[l], feedback_in.at[l], sems.at[1, l]),
        )
        for l in range(LEVELS)
    ]
    for pair in copies:
        for copy in pair:
            copy.start()
    for copy in small:
        copy.wait()
    tile = table.shape[1:]

    def splat(value):
        return jnp.full(tile, value, jnp.int32).astype(jnp.float32)

    for q in range(MODULES):
        table[SKIPPED + q] = splat(flags[q & 1, q >> 1])
    for l in range(LEVELS):
        own = routes[l, path]
        denom = jnp.int32(0)
        for p in range(PATHS):
            denom += jnp.where(routes[l, p] == own, counts[l, p], 0)
        top, bottom = splat(counts[l, path]), splat(denom)
        ratio = top / bottom
        high = ratio.astype(jnp.bfloat16).astype(jnp.float32)
        rest = (top - high * bottom) - (ratio - high) * bottom
        ratio = ratio + rest / bottom
        live = flags[own, l] == 0
        table[OWN_UPPER + l] = splat(own)
        table[SIBLING_UPPER + l] = splat(routes[l, sibling])
        table[WEIGHT + l] = ratio
        table[BACK + l] = jnp.where(live, bottom / top, 0.0)
        weight = jnp.where(live, ratio, 0.0)[:1]
        for copy in copies[l]:
            copy.wait()
        send_half(weight, delta_in.at[l], feedback_in.at[l], 1 - core, give.at[l])


def keep_kernel(table, delta, feedback, keep):
    core = lax.axis_index("core")
    for l in range(LEVELS):
        weight = jnp.where(table[BACK + l] > 0, table[WEIGHT + l], 0.0)[:1]
        send_half(weight, delta.at[l], feedback.at[l], core, keep.at[l])


def feedback_kernel(table, delta, feedback, out):
    l = pl.program_id(0)
    weight, back = table[WEIGHT + l][:1], table[BACK + l][:1]
    for block in range(2 * CHIPS):
        at = pl.ds(block * BLOCK, BLOCK)
        corrected = delta[0, :, at].astype(jnp.float32) + feedback[0, :, at]
        sent = (weight * corrected).astype(jnp.bfloat16).astype(jnp.float32)
        out[0, :, at] = corrected - sent * back


def write_pairs(table, keep, got, out, jumps):
    z, _, sign = place()
    for l in range(LEVELS):
        own, sibling = table[OWN_UPPER + l][:1], table[SIBLING_UPPER + l][:1]
        for slot, steps in enumerate(jumps):
            chip = chip_at(z, sign, steps)
            first, second = keep[l, chip].astype(jnp.float32), got[l, chip].astype(jnp.float32)
            upper = own * first + sibling * second
            lower = (1.0 - own) * first + (1.0 - sibling) * second
            out[slot, 2 * l] = lower.astype(jnp.bfloat16)
            out[slot, 2 * l + 1] = upper.astype(jnp.bfloat16)


def outgoing_kernel(table, keep, got, plus, minus):
    write_pairs(table, keep, got, plus, (1, -2, 3))
    write_pairs(table, keep, got, minus, (-1, -4))


def staying_kernel(table, keep, got, hold):
    write_pairs(table, keep, got, hold, (0, -3, 2))


def start_kernel(table, params, momentum, start):
    for q in range(MODULES):
        share = MOMENTUM_SHARE * (1.0 - table[SKIPPED + q][:1])
        start[q] = (params[q] - share * momentum[q]).astype(jnp.bfloat16)


def owner_kernel(hold, plus, minus, near, far, average, narrow, partial):
    for q in range(MODULES):
        total = hold[0, q].astype(jnp.float32)
        for part in (plus[0, q], minus[0, q], near[q], far[q]):
            total += part.astype(jnp.float32)
        average[q] = total
        narrow[q] = total.astype(jnp.bfloat16)
        squares = total * total
        squares = squares[:, :128] + squares[:, 128:]
        partial[q : q + 1] = jnp.sum(squares, axis=0, keepdims=True)


def factors(entries, sums):
    total = jnp.sum(sums, axis=1, keepdims=True)
    return jnp.minimum(1.0, CLIP_RMS / jnp.sqrt(total / entries + EPSILON_SQ))


def state_kernel(entries, table, sums, average, params, momentum, momentum_out, params_out):
    factor = factors(entries, jnp.sum(sums[...], axis=0))
    for q in range(MODULES):
        skipped = table[SKIPPED + q][:1] > 0
        clipped = factor[q : q + 1] * average[q]
        before, old = momentum[q], params[q]
        after = jnp.where(skipped, before, MOMENTUM_COEF * before + clipped)
        momentum_out[q] = after
        params_out[q] = jnp.where(skipped, old, old - OUTER_RATE * (clipped + MOMENTUM_COEF * after))


def parts_of(own, near, far, plus, minus):
    return (own, minus.at[0], near, minus.at[2], plus.at[1], far, minus.at[1], plus.at[0])


def new_kernel(entries, row, table, sums, *refs):
    z, _, sign = place()
    *parts, out = refs
    starts, averages = parts_of(*parts[:5]), parts_of(*parts[5:])
    factor = CLIPPED_COEF * factors(entries, jnp.sum(sums[...], axis=0))
    for l in range(LEVELS):
        upper = table[row + l][:1]
        scale_low, scale_high = (1.0 - upper) * factor[2 * l : 2 * l + 1], upper * factor[2 * l + 1 : 2 * l + 2]
        for slot in range(CHIPS):
            start, average = starts[slot], averages[slot]
            base = jnp.where(upper > 0, start[2 * l + 1].astype(jnp.float32), start[2 * l].astype(jnp.float32))
            moved = scale_low * average[2 * l].astype(jnp.float32) + scale_high * average[2 * l + 1].astype(jnp.float32)
            out[l, chip_at(z, sign, slot)] = (base - moved).astype(jnp.bfloat16)


def join_kernel(mine, got, out):
    core = lax.axis_index("core")
    for half, part in ((core, mine), (1 - core, got)):
        for block in range(CHIPS):
            at = pl.ds(pl.multiple_of((2 * block + half) * BLOCK, BLOCK), BLOCK)
            out[0, :, at] = part[0, block]


def cost(bytes_accessed):
    return pl.CostEstimate(flops=0, bytes_accessed=bytes_accessed, transcendentals=0)


def size_of(arrays):
    return sum(a.size * a.dtype.itemsize for a in arrays)


def call(kernel, outs, *args):
    shapes = [jax.ShapeDtypeStruct(s, d) for s, d in outs]
    return pl.pallas_call(
        kernel,
        out_shape=shapes,
        in_specs=[VMEM] * len(args),
        out_specs=[VMEM] * len(shapes),
        cost_estimate=cost(size_of(args) + size_of(shapes)),
        compiler_params=pltpu.CompilerParams(vmem_limit_bytes=24 * 2**20),
    )(*args)


def levelwise(kernel, outs, fixed, *args):
    shapes = [jax.ShapeDtypeStruct(s, d) for s, d in outs]

    def one(shape):
        return pl.BlockSpec((1, *shape[1:]), lambda l: (l, *[0] * (len(shape) - 1)))

    return pl.pallas_call(
        kernel,
        grid=(LEVELS,),
        out_shape=shapes,
        in_specs=[VMEM] * len(fixed) + [one(a.shape) for a in args],
        out_specs=[one(s.shape) for s in shapes],
        cost_estimate=cost(size_of(args) + size_of(shapes)),
        compiler_params=pltpu.CompilerParams(vmem_limit_bytes=24 * 2**20),
    )(*fixed, *args)


def given_half(routes, counts, flags, delta, feedback):
    _, rows, _ = delta.shape
    half = jax.ShapeDtypeStruct((LEVELS, CHIPS, rows, BLOCK), jnp.bfloat16)
    table = jax.ShapeDtypeStruct((TABLE, 8, BLOCK), jnp.float32)
    return pl.pallas_call(
        give_kernel,
        out_shape=[half, table],
        in_specs=[HBM] * 5,
        out_specs=[VMEM] * 2,
        scratch_shapes=[
            pltpu.SMEM(routes.shape, jnp.int32),
            pltpu.SMEM(counts.shape, jnp.int32),
            pltpu.SMEM(flags.shape, jnp.int32),
            pltpu.VMEM(delta.shape, delta.dtype),
            pltpu.VMEM(feedback.shape, feedback.dtype),
            pltpu.SemaphoreType.DMA((2, LEVELS)),
            pltpu.SemaphoreType.DMA((3,)),
        ],
        cost_estimate=cost(half.size * 16),
        compiler_params=pltpu.CompilerParams(vmem_limit_bytes=56 * 2**20),
    )(routes, counts, flags, delta, feedback)


def jump(x, steps):
    def target(p):
        z, core = divmod(p, 2)
        sign = 1 - 2 * core
        return 2 * ((z + sign * steps) % CHIPS) + core

    return lax.ppermute(x, PATH, [(p, target(p)) for p in range(PATHS)])


def swap(x):
    return lax.ppermute(x, "core", [(0, 1), (1, 0)])


def spread_far(x):
    return jump(x, 3), jump(x, -2)


def spread_near(x, far, near):
    plus = jump(jnp.stack([x, far]), 1)
    minus = jump(jnp.stack([x, far, near]), -1)
    return x, near, far, plus, minus


def summed(x, axes):
    parts = jnp.broadcast_to(x[None], (lax.axis_size(axes), *x.shape))
    return lax.all_to_all(parts, axes, 0, 0)


def on_device(path_delta, feedback, global_params, momentum, routes, token_counts, skip_flags):
    delta, feedback = path_delta[0], feedback[0]
    rows = delta.shape[1]
    params = global_params.reshape(MODULES, rows, BLOCK)
    momentum = momentum.reshape(MODULES, rows, BLOCK)
    f32, bf16 = jnp.float32, jnp.bfloat16
    half, block = (LEVELS, CHIPS, rows, BLOCK), (MODULES, rows, BLOCK)
    entries = rows * lax.axis_size(FSDP) * BLOCK * lax.axis_size(PATH)

    give, table = given_half(routes.T, token_counts.T, skip_flags.T, delta, feedback)
    got = swap(give)
    (keep,) = call(keep_kernel, [(half, bf16)], table, delta, feedback)
    plus, minus = call(outgoing_kernel, [((3, *block), bf16), ((2, *block), bf16)], table, keep, got)
    later, _ = lax.optimization_barrier((table, minus))
    plus, minus = jump(plus, 1), jump(minus, -1)
    (start,) = call(start_kernel, [(block, bf16)], later, params, momentum)
    later, _ = lax.optimization_barrier((later, start))
    (hold,) = call(staying_kernel, [((3, *block), bf16)], later, keep, got)
    (feedback_next,) = levelwise(feedback_kernel, [(delta.shape, f32)], (later,), delta, feedback)
    far, near = spread_far(start)
    hold, feedback_next = lax.optimization_barrier((hold, feedback_next))
    reduced_near = jump(hold[2] + plus[2], 2)
    reduced_far = jump(hold[1] + plus[1] + minus[1], -3)
    starts = spread_near(start, far, near)
    average, narrow, partial = call(
        owner_kernel,
        [(block, f32), (block, bf16), ((MODULES, 128), f32)],
        hold,
        plus,
        minus,
        reduced_near,
        reduced_far,
    )
    sums = jnp.sum(summed(partial, FSDP), axis=0)
    far, near = spread_far(narrow)
    narrow, sums = lax.optimization_barrier((narrow, sums))
    averages = spread_near(narrow, far, near)
    sums = summed(sums, PATH)

    def bound(kernel, *values):
        return lambda *refs: kernel(*values, *refs)

    momentum_next, params_next = call(
        bound(state_kernel, entries), [(block, f32)] * 2, table, sums, average, params, momentum
    )
    (give,) = call(
        bound(new_kernel, entries, SIBLING_UPPER), [(half, bf16)], table, sums, *starts, *averages
    )
    got = swap(give)
    (mine,) = call(bound(new_kernel, entries, OWN_UPPER), [(half, bf16)], table, sums, *starts, *averages)
    (path_params,) = levelwise(join_kernel, [(delta.shape, bf16)], (), mine, got)
    shape = global_params.shape
    return feedback_next[None], momentum_next.reshape(shape), params_next.reshape(shape), path_params[None]


def solution(mesh):
    finer = Mesh(mesh.devices.reshape(8, 2, 4, 4), (*PATH, *FSDP))
    by_path, by_column = P(PATH, None, FSDP, None), P(None, None, FSDP, PATH)
    return jax.shard_map(
        on_device,
        mesh=finer,
        in_specs=(by_path, by_path, by_column, by_column, P(), P(), P()),
        out_specs=(by_path, by_column, by_column, by_path),
        check_vma=False,
    )
```

time: 130 us -> 80.3 us (0.62)
  blocking collectives: 77.3 us -> 0 us
  starting transfers between devices: 8.03 us -> 38.8 us
  Pallas kernels: 0 us -> 8.92 us
  other arithmetic: 8.95 us -> 2.34 us
  local copies, waits for them, and re-layouts: 7.89 us -> 2.33 us
    all_to_all x2 -> x0, blocking collectives: 41.6 us -> none  [turned_blocks(): lax.all_to_all(parts, axes[k], split_axis=k, concat_axis=k, tiled=True)]
    psum x4 -> x0, blocking collectives: 35.7 us -> none  [over_axes(): return functools.reduce(lax.psum, axes, x)]
    ppermute x0 -> x14, starting transfers between devices: none -> 21.2 us  [the longest x12 17.6 us: jump(): return lax.ppermute(x, PATH, [(p, target(p)) for p in range(PATHS)])]
    ppermute x0 -> x14, waiting for transfers between devices: none -> 14 us  [the longest x12 13 us: jump(): return lax.ppermute(x, PATH, [(p, target(p)) for p in range(PATHS)])]
    all_to_all x1 -> x2, waiting for transfers between devices: 26.5 us -> 12.9 us  [summed(): return lax.all_to_all(parts, axes, 0, 0)]
    all_to_all x1 -> x2, starting transfers between devices: 8.03 us -> 17.6 us  [summed(): return lax.all_to_all(parts, axes, 0, 0)]
    pallas_call x0 -> x11, Pallas kernels: none -> 8.92 us  [the longest x2 3.55 us: levelwise(): pl.pallas_call(kernel, grid=(LEVELS,), out_shape=shapes, in_specs=[VMEM]...]
    sub x1 -> x0, other arithmetic: 3.72 us -> none  [on_device(): corrected - own_live[:, None, None] * (sent.astype(jnp.float32) / own_wei...]
  transfers between devices with their start and end apart: 1 -> 16, of which waited for: 1 -> 6; matrix products, arithmetic and copies ran while one was open for 1% -> 4% of each run, Pallas kernels for 0% -> 5%
where the time goes in v2:
time: 80.3 us; the launch traced here: 80 us
  starting transfers between devices  38.8 us (48%)
  waiting for transfers between devices  26.9 us (33%)
  Pallas kernels  8.92 us (11%)
  other arithmetic  2.34 us (3%)
  local copies, waits for them, and re-layouts  2.33 us (3%)
    ppermute x12, starting transfers between devices, jump(): return lax.ppermute(x, PATH, [(p, target(p)) for p in range(PATHS)])  17.6 us
    all_to_all x2, starting transfers between devices, summed(): return lax.all_to_all(parts, axes, 0, 0)  17.6 us
    ppermute x12, waiting for transfers between devices, jump(): return lax.ppermute(x, PATH, [(p, target(p)) for p in range(PATHS)])  13 us
    all_to_all x2, waiting for transfers between devices, summed(): return lax.all_to_all(parts, axes, 0, 0)  12.9 us
    ppermute x2, starting transfers between devices, swap(): return lax.ppermute(x, 'core', [(0, 1), (1, 0)])  3.58 us
    pallas_call x2, Pallas kernels, levelwise(): pl.pallas_call(kernel, grid=(LEVELS,), out_shape=shapes, in_specs=[VMEM]...  3.55 us
    pallas_call x1, Pallas kernels, given_half(): pl.pallas_call(give_kernel, out_shape=[half, table], in_specs=[HBM] * 5,...  2.94 us
    pallas_call x8, Pallas kernels, call(): pl.pallas_call(kernel, out_shape=shapes, in_specs=[VMEM] * len(args), out...  2.42 us
  transfers between devices with their start and end apart: 16, of which 6 were waited for; matrix products, arithmetic and copies ran while one was open for 4% of the time, Pallas kernels for 5%

profile of v2, /device:TPU:1, one launch (start us, length us, event | category | flops | bytes accessed | tf_op | source)
XLA Modules:
  0.0 80.0 jit_solution(15778834728752165434)
XLA Ops:
  0.7 2.9 %shard_map.102 = (bf16[4,8,32,256]{3,2,1,0:T(8,128)(2,1)}, f32[24,8,256]{2,1,0:T(8,128)}) custom-call(s32[4,16]{1,0:T(4,128)} %bitcast.43, s32[4,16]{1,0:T(4,128)} %bitcast.44, s32[2,4]{1,0:T(2,128)} %bitcast.45, bf16[4,32,4096]{2,1,0:T(8,128)(2,1)} %bitcast.24, f32[4,32,4096]{2,1,0:T(8,128)} %bitcast.21), custom_call_target="tpu_custom_call" | custom-call | bytes 4194304 | tf_op jit(solution)/shard_map/pallas_call | solution.py:238
  3.6 3.3 %collective-permute-start = (bf16[4,8,32,256]{3,2,1,0:T(8,128)(2,1)}, bf16[4,8,32,256]{3,2,1,0:T(8,128)(2,1)S(1)}, u32[]{:S(2)}, u32[]{:S(2)}) collective-permute-start(bf16[4,8,32,256]{3,2,1,0:T(8,128)(2,1)} %get-tuple-element.20), channel_id=1, source_target_pairs={{0,16},{16,0},{1,17},{17,1},{2,18},{18,2},{3,19},{19,3},{4,20},{20... | collective-permute-start | bytes 1572872 | tf_op jit(solution)/shard_map/ppermute | solution.py:267
  6.9 0.9 %copy-done.1 = f32[24,8,256]{2,1,0:T(8,128)S(1)} copy-done((f32[24,8,256]{2,1,0:T(8,128)S(1)}, f32[24,8,256]{2,1,0:T(8,128)}, u32[]{:S(2)}) %copy-start.1) | copy-done | bytes 196632
  9.0 3.9 %collective-permute-start.1 = (bf16[3,8,32,256]{3,2,1,0:T(8,128)(2,1)S(1)}, bf16[3,8,32,256]{3,2,1,0:T(8,128)(2,1)S(1)}, u32[]{:S(2)}, u32[]{:S(2)}) collective-permute-start(bf16[3,8,32,256]{3,2,1,0:T(8,128)(2,1)S(1)} %get-tuple-element.26), channel_id=1, source_target_pairs={{0,32},{16,240},{32,64},{48,16},{64,96},{80,48},{96,128},{112,80},... | collective-permute-start | bytes 1179656 | tf_op jit(solution)/shard_map/ppermute | solution.py:263
  13.0 2.0 %shard_map.107 = f32[4,32,4096]{2,1,0:T(8,128)} custom-call(f32[24,8,256]{2,1,0:T(8,128)S(1)} %copy-done.2, bf16[4,32,4096]{2,1,0:T(8,128)(2,1)S(1)} %bitcast.26, f32[4,32,4096]{2,1,0:T(8,128)S(1)} %bitcast.23), custom_call_target="tpu_custom_call" | custom-call | bytes 5242880 | tf_op jit(solution)/shard_map/pallas_call | solution.py:223
  15.1 6.2 %collective-permute-done.2.minus = bf16[2,8,32,256]{3,2,1,0:T(8,128)(2,1)S(1)} collective-permute-done((bf16[2,8,32,256]{3,2,1,0:T(8,128)(2,1)S(1)}, bf16[2,8,32,256]{3,2,1,0:T(8,128)(2,1)S(1)}, u32[]{:S(2)}, u32[]{:S(2)}) %collective-permute-start.2) | collective-permute-done | bytes 262176 | tf_op jit(solution)/shard_map/ppermute | solution.py:263
  21.4 1.4 %collective-permute-start.3 = (bf16[8,32,256]{2,1,0:T(8,128)(2,1)S(1)}, bf16[8,32,256]{2,1,0:T(8,128)(2,1)S(1)}, u32[]{:S(2)}, u32[]{:S(2)}) collective-permute-start(bf16[8,32,256]{2,1,0:T(8,128)(2,1)S(1)} %get-tuple-element.35), channel_id=1, source_target_pairs={{0,64},{16,208},{32,96},{48,240},{64,128},{80,16},{96,160},{112,48... | collective-permute-start | bytes 393224 | tf_op jit(solution)/shard_map/ppermute | solution.py:263
  22.8 4.5 %collective-permute-start.6 = (bf16[8,32,256]{2,1,0:T(8,128)(2,1)S(1)}, bf16[8,32,256]{2,1,0:T(8,128)(2,1)S(1)}, u32[]{:S(2)}, u32[]{:S(2)}) collective-permute-start(bf16[8,32,256]{2,1,0:T(8,128)(2,1)S(1)} %shard_map.105.refs_2_), channel_id=1, source_target_pairs={{0,96},{16,176},{32,128},{48,208},{64,160},{80,240},{96,192},{112,... | collective-permute-start | bytes 393224 | tf_op jit(solution)/shard_map/ppermute | solution.py:263
  27.3 1.0 %collective-permute-start.5 = (bf16[8,32,256]{2,1,0:T(8,128)(2,1)S(1)}, bf16[8,32,256]{2,1,0:T(8,128)(2,1)S(1)}, u32[]{:S(2)}, u32[]{:S(2)}) collective-permute-start(bf16[8,32,256]{2,1,0:T(8,128)(2,1)S(1)} %shard_map.105.refs_2_), channel_id=1, source_target_pairs={{0,192},{16,80},{32,224},{48,112},{64,0},{80,144},{96,32},{112,176... | collective-permute-start | bytes 393224 | tf_op jit(solution)/shard_map/ppermute | solution.py:263
  28.3 6.7 %collective-permute-done.4.far = bf16[8,32,256]{2,1,0:T(8,128)(2,1)S(1)} collective-permute-done((bf16[8,32,256]{2,1,0:T(8,128)(2,1)S(1)}, bf16[8,32,256]{2,1,0:T(8,128)(2,1)S(1)}, u32[]{:S(2)}, u32[]{:S(2)}) %collective-permute-start.4) | collective-permute-done | bytes 131104 | tf_op jit(solution)/shard_map/ppermute | solution.py:263
  35.1 1.6 %collective-permute-start.10 = (bf16[8,32,256]{2,1,0:T(8,128)(2,1)S(1)}, bf16[8,32,256]{2,1,0:T(8,128)(2,1)S(1)}, u32[]{:S(2)}, u32[]{:S(2)}) collective-permute-start(bf16[8,32,256]{2,1,0:T(8,128)(2,1)S(1)} %get-tuple-element.33.refs_7_), channel_id=1, source_target_pairs={{0,96},{16,176},{32,128},{48,208},{64,160},{80,240},{96,192},{112,... | collective-permute-start | bytes 393224 | tf_op jit(solution)/shard_map/ppermute | solution.py:263
  36.8 0.7 collective-permute-start.9
  38.1 6.8 %all-to-all-start = ((f32[16,8,128]{2,1,0:T(8,128)}), f32[16,8,128]{2,1,0:T(8,128)S(1)}, u32[]{:S(2)}, u32[]{:S(2)}) async-start(f32[16,8,128]{2,1,0:T(8,128)} %broadcast_in_dim.9), calls=%async_computation | async-start | bytes 131072 | tf_op jit(solution)/shard_map/all_to_all | solution.py:282
  44.9 1.3 %collective-permute-start.8 = (bf16[3,8,32,256]{3,2,1,0:T(8,128)(2,1)S(1)}, bf16[3,8,32,256]{3,2,1,0:T(8,128)(2,1)S(1)}, u32[]{:S(2)}, u32[]{:S(2)}) collective-permute-start(bf16[3,8,32,256]{3,2,1,0:T(8,128)(2,1)S(1)} %pad_maximum_fusion), channel_id=1, source_target_pairs={{0,224},{16,48},{32,0},{48,80},{64,32},{80,112},{96,64},{112,144},... | collective-permute-start | bytes 1179656 | tf_op jit(solution)/shard_map/ppermute | solution.py:263
  46.3 5.1 %all-to-all-done = f32[16,8,128]{2,1,0:T(8,128)S(1)} async-done(((f32[16,8,128]{2,1,0:T(8,128)}), f32[16,8,128]{2,1,0:T(8,128)S(1)}, u32[]{:S(2)}, u32[]{:S(2)}) %all-to-all-start) | async-done | bytes 65568 | tf_op jit(solution)/shard_map/all_to_all | solution.py:282
  51.4 0.8 pad_maximum_fusion.1
  52.2 1.3 %collective-permute-start.12 = (bf16[3,8,32,256]{3,2,1,0:T(8,128)(2,1)}, bf16[3,8,32,256]{3,2,1,0:T(8,128)(2,1)S(1)}, u32[]{:S(2)}, u32[]{:S(2)}) collective-permute-start(bf16[3,8,32,256]{3,2,1,0:T(8,128)(2,1)} %pad_maximum_fusion.1), channel_id=1, source_target_pairs={{0,224},{16,48},{32,0},{48,80},{64,32},{80,112},{96,64},{112,144},... | collective-permute-start | bytes 1179656 | tf_op jit(solution)/shard_map/ppermute | solution.py:263
  53.5 0.7 pad_maximum_fusion.2
  54.2 1.4 %collective-permute-start.7 = (bf16[2,8,32,256]{3,2,1,0:T(8,128)(2,1)}, bf16[2,8,32,256]{3,2,1,0:T(8,128)(2,1)S(1)}, u32[]{:S(2)}, u32[]{:S(2)}) collective-permute-start(bf16[2,8,32,256]{3,2,1,0:T(8,128)(2,1)} %pad_maximum_fusion.2), channel_id=1, source_target_pairs={{0,32},{16,240},{32,64},{48,16},{64,96},{80,48},{96,128},{112,80},... | collective-permute-start | bytes 786440 | tf_op jit(solution)/shard_map/ppermute | solution.py:263
  55.6 0.7 pad_maximum_fusion.3
  57.4 10.8 %all-to-all-start.1 = ((f32[16,8,128]{2,1,0:T(8,128)}), f32[16,8,128]{2,1,0:T(8,128)S(1)}, u32[]{:S(2)}, u32[]{:S(2)}) async-start(f32[16,8,128]{2,1,0:T(8,128)} %broadcast_in_dim.20), calls=%async_computation.1 | async-start | bytes 131072 | tf_op jit(solution)/shard_map/all_to_all | solution.py:282
  68.3 7.8 %all-to-all-done.1.refs_1_ = f32[16,8,128]{2,1,0:T(8,128)S(1)} async-done(((f32[16,8,128]{2,1,0:T(8,128)}), f32[16,8,128]{2,1,0:T(8,128)S(1)}, u32[]{:S(2)}, u32[]{:S(2)}) %all-to-all-start.1) | async-done | bytes 65568 | tf_op jit(solution)/shard_map/all_to_all | solution.py:282
  76.7 1.0 %shard_map.109 = (f32[8,32,256]{2,1,0:T(8,128)}, f32[8,32,256]{2,1,0:T(8,128)}) custom-call(f32[24,8,256]{2,1,0:T(8,128)S(1)} %copy-done.2, f32[16,8,128]{2,1,0:T(8,128)S(1)} %all-to-all-done.1.refs_1_, f32[8,32,256]{2,1,0:T(8,128)S(1)} %get-tuple-element.30.refs_2_, f32[8,32,256]{2,1,0:T(8,128)S(1)} %bitcast.38, f32[8,32,256]{2,1,0:T(8,128)S(1)} %bitcast.40), custom_call_target="tpu_custom_call" | custom-call | bytes 1572864 | tf_op jit(solution)/shard_map/pallas_call | solution.py:207
  78.5 1.5 %shard_map.112 = bf16[4,32,4096]{2,1,0:T(8,128)(2,1)} custom-call(bf16[4,8,32,256]{3,2,1,0:T(8,128)(2,1)S(1)} %shard_map.110.mine, bf16[4,8,32,256]{3,2,1,0:T(8,128)(2,1)S(1)} %collective-permute-done.13.got), custom_call_target="tpu_custom_call" | custom-call | bytes 2097152 | tf_op jit(solution)/shard_map/pallas_call | solution.py:223
  (39 shorter events, 4.7 us)
Async XLA Ops:
  0.6 6.3 %copy-start.3 = (bf16[1,4,32,4096]{3,2,1,0:T(8,128)(2,1)S(1)}, bf16[1,4,32,4096]{3,2,1,0:T(8,128)(2,1)}, u32[]{:S(2)}) copy-start(bf16[1,4,32,4096]{3,2,1,0:T(8,128)(2,1)} %param.7) | copy-start | bytes 3145732
  0.6 6.3 %copy-start = (f32[1,4,32,4096]{3,2,1,0:T(8,128)S(1)}, f32[1,4,32,4096]{3,2,1,0:T(8,128)}, u32[]{:S(2)}) copy-start(f32[1,4,32,4096]{3,2,1,0:T(8,128)} %param.8) | copy-start | bytes 6291460
  3.6 5.1 %collective-permute-start = (bf16[4,8,32,256]{3,2,1,0:T(8,128)(2,1)}, bf16[4,8,32,256]{3,2,1,0:T(8,128)(2,1)S(1)}, u32[]{:S(2)}, u32[]{:S(2)}) collective-permute-start(bf16[4,8,32,256]{3,2,1,0:T(8,128)(2,1)} %get-tuple-element.20), channel_id=1, source_target_pairs={{0,16},{16,0},{1,17},{17,1},{2,18},{18,2},{3,19},{19,3},{4,20},{20... | collective-permute-start | bytes 1572872 | tf_op jit(solution)/shard_map/ppermute | solution.py:267
  6.9 0.9 %copy-start.1 = (f32[24,8,256]{2,1,0:T(8,128)S(1)}, f32[24,8,256]{2,1,0:T(8,128)}, u32[]{:S(2)}) copy-start(f32[24,8,256]{2,1,0:T(8,128)} %get-tuple-element.23.table.refs_0_) | copy-start | bytes 589828
  7.9 0.9 %copy-start.2 = (f32[24,8,256]{2,1,0:T(8,128)S(1)}, f32[24,8,256]{2,1,0:T(8,128)}, u32[]{:S(2)}) copy-start(f32[24,8,256]{2,1,0:T(8,128)} %get-tuple-element.23.table.refs_0_) | copy-start | bytes 589828
  7.9 5.1 %copy-start.4 = (f32[4,2,32,256]{3,2,1,0:T(8,128)S(1)}, f32[4,2,32,256]{3,2,1,0:T(8,128)}, u32[]{:S(2)}) copy-start(f32[4,2,32,256]{3,2,1,0:T(8,128)} %param.9) | copy-start | bytes 786436
  7.9 5.1 %copy-start.5 = (f32[4,2,32,256]{3,2,1,0:T(8,128)S(1)}, f32[4,2,32,256]{3,2,1,0:T(8,128)}, u32[]{:S(2)}) copy-start(f32[4,2,32,256]{3,2,1,0:T(8,128)} %param.10) | copy-start | bytes 786436
  9.0 12.3 %collective-permute-start.1 = (bf16[3,8,32,256]{3,2,1,0:T(8,128)(2,1)S(1)}, bf16[3,8,32,256]{3,2,1,0:T(8,128)(2,1)S(1)}, u32[]{:S(2)}, u32[]{:S(2)}) collective-permute-start(bf16[3,8,32,256]{3,2,1,0:T(8,128)(2,1)S(1)} %get-tuple-element.26), channel_id=1, source_target_pairs={{0,32},{16,240},{32,64},{48,16},{64,96},{80,48},{96,128},{112,80},... | collective-permute-start | bytes 1179656 | tf_op jit(solution)/shard_map/ppermute | solution.py:263
  12.9 8.4 %collective-permute-start.2 = (bf16[2,8,32,256]{3,2,1,0:T(8,128)(2,1)S(1)}, bf16[2,8,32,256]{3,2,1,0:T(8,128)(2,1)S(1)}, u32[]{:S(2)}, u32[]{:S(2)}) collective-permute-start(bf16[2,8,32,256]{3,2,1,0:T(8,128)(2,1)S(1)} %get-tuple-element.21), channel_id=1, source_target_pairs={{0,224},{16,48},{32,0},{48,80},{64,32},{80,112},{96,64},{112,144},... | collective-permute-start | bytes 786440 | tf_op jit(solution)/shard_map/ppermute | solution.py:263
  21.4 6.9 %collective-permute-start.3 = (bf16[8,32,256]{2,1,0:T(8,128)(2,1)S(1)}, bf16[8,32,256]{2,1,0:T(8,128)(2,1)S(1)}, u32[]{:S(2)}, u32[]{:S(2)}) collective-permute-start(bf16[8,32,256]{2,1,0:T(8,128)(2,1)S(1)} %get-tuple-element.35), channel_id=1, source_target_pairs={{0,64},{16,208},{32,96},{48,240},{64,128},{80,16},{96,160},{112,48... | collective-permute-start | bytes 393224 | tf_op jit(solution)/shard_map/ppermute | solution.py:263
  22.8 12.2 %collective-permute-start.4 = (bf16[8,32,256]{2,1,0:T(8,128)(2,1)S(1)}, bf16[8,32,256]{2,1,0:T(8,128)(2,1)S(1)}, u32[]{:S(2)}, u32[]{:S(2)}) collective-permute-start(bf16[8,32,256]{2,1,0:T(8,128)(2,1)S(1)} %get-tuple-element.34), channel_id=1, source_target_pairs={{0,160},{16,112},{32,192},{48,144},{64,224},{80,176},{96,0},{112,2... | collective-permute-start | bytes 393224 | tf_op jit(solution)/shard_map/ppermute | solution.py:263
  22.8 22.1 %collective-permute-start.6 = (bf16[8,32,256]{2,1,0:T(8,128)(2,1)S(1)}, bf16[8,32,256]{2,1,0:T(8,128)(2,1)S(1)}, u32[]{:S(2)}, u32[]{:S(2)}) collective-permute-start(bf16[8,32,256]{2,1,0:T(8,128)(2,1)S(1)} %shard_map.105.refs_2_), channel_id=1, source_target_pairs={{0,96},{16,176},{32,128},{48,208},{64,160},{80,240},{96,192},{112,... | collective-permute-start | bytes 393224 | tf_op jit(solution)/shard_map/ppermute | solution.py:263
  27.3 17.6 %collective-permute-start.5 = (bf16[8,32,256]{2,1,0:T(8,128)(2,1)S(1)}, bf16[8,32,256]{2,1,0:T(8,128)(2,1)S(1)}, u32[]{:S(2)}, u32[]{:S(2)}) collective-permute-start(bf16[8,32,256]{2,1,0:T(8,128)(2,1)S(1)} %shard_map.105.refs_2_), channel_id=1, source_target_pairs={{0,192},{16,80},{32,224},{48,112},{64,0},{80,144},{96,32},{112,176... | collective-permute-start | bytes 393224 | tf_op jit(solution)/shard_map/ppermute | solution.py:263
  35.1 16.3 %collective-permute-start.10 = (bf16[8,32,256]{2,1,0:T(8,128)(2,1)S(1)}, bf16[8,32,256]{2,1,0:T(8,128)(2,1)S(1)}, u32[]{:S(2)}, u32[]{:S(2)}) collective-permute-start(bf16[8,32,256]{2,1,0:T(8,128)(2,1)S(1)} %get-tuple-element.33.refs_7_), channel_id=1, source_target_pairs={{0,96},{16,176},{32,128},{48,208},{64,160},{80,240},{96,192},{112,... | collective-permute-start | bytes 393224 | tf_op jit(solution)/shard_map/ppermute | solution.py:263
  36.8 14.7 %collective-permute-start.9 = (bf16[8,32,256]{2,1,0:T(8,128)(2,1)S(1)}, bf16[8,32,256]{2,1,0:T(8,128)(2,1)S(1)}, u32[]{:S(2)}, u32[]{:S(2)}) collective-permute-start(bf16[8,32,256]{2,1,0:T(8,128)(2,1)S(1)} %get-tuple-element.33.refs_7_), channel_id=1, source_target_pairs={{0,192},{16,80},{32,224},{48,112},{64,0},{80,144},{96,32},{112,176... | collective-permute-start | bytes 393224 | tf_op jit(solution)/shard_map/ppermute | solution.py:263
  38.1 13.3 %all-to-all-start = ((f32[16,8,128]{2,1,0:T(8,128)}), f32[16,8,128]{2,1,0:T(8,128)S(1)}, u32[]{:S(2)}, u32[]{:S(2)}) async-start(f32[16,8,128]{2,1,0:T(8,128)} %broadcast_in_dim.9), calls=%async_computation | async-start | bytes 131072 | tf_op jit(solution)/shard_map/all_to_all | solution.py:282
  44.9 23.3 %collective-permute-start.8 = (bf16[3,8,32,256]{3,2,1,0:T(8,128)(2,1)S(1)}, bf16[3,8,32,256]{3,2,1,0:T(8,128)(2,1)S(1)}, u32[]{:S(2)}, u32[]{:S(2)}) collective-permute-start(bf16[3,8,32,256]{3,2,1,0:T(8,128)(2,1)S(1)} %pad_maximum_fusion), channel_id=1, source_target_pairs={{0,224},{16,48},{32,0},{48,80},{64,32},{80,112},{96,64},{112,144},... | collective-permute-start | bytes 1179656 | tf_op jit(solution)/shard_map/ppermute | solution.py:263
  52.2 23.9 %collective-permute-start.12 = (bf16[3,8,32,256]{3,2,1,0:T(8,128)(2,1)}, bf16[3,8,32,256]{3,2,1,0:T(8,128)(2,1)S(1)}, u32[]{:S(2)}, u32[]{:S(2)}) collective-permute-start(bf16[3,8,32,256]{3,2,1,0:T(8,128)(2,1)} %pad_maximum_fusion.1), channel_id=1, source_target_pairs={{0,224},{16,48},{32,0},{48,80},{64,32},{80,112},{96,64},{112,144},... | collective-permute-start | bytes 1179656 | tf_op jit(solution)/shard_map/ppermute | solution.py:263
  54.2 14.1 %collective-permute-start.7 = (bf16[2,8,32,256]{3,2,1,0:T(8,128)(2,1)}, bf16[2,8,32,256]{3,2,1,0:T(8,128)(2,1)S(1)}, u32[]{:S(2)}, u32[]{:S(2)}) collective-permute-start(bf16[2,8,32,256]{3,2,1,0:T(8,128)(2,1)} %pad_maximum_fusion.2), channel_id=1, source_target_pairs={{0,32},{16,240},{32,64},{48,16},{64,96},{80,48},{96,128},{112,80},... | collective-permute-start | bytes 786440 | tf_op jit(solution)/shard_map/ppermute | solution.py:263
  56.3 19.7 %collective-permute-start.11 = (bf16[2,8,32,256]{3,2,1,0:T(8,128)(2,1)}, bf16[2,8,32,256]{3,2,1,0:T(8,128)(2,1)S(1)}, u32[]{:S(2)}, u32[]{:S(2)}) collective-permute-start(bf16[2,8,32,256]{3,2,1,0:T(8,128)(2,1)} %pad_maximum_fusion.3), channel_id=1, source_target_pairs={{0,32},{16,240},{32,64},{48,16},{64,96},{80,48},{96,128},{112,80},... | collective-permute-start | bytes 786440 | tf_op jit(solution)/shard_map/ppermute | solution.py:263
  57.4 18.6 %all-to-all-start.1 = ((f32[16,8,128]{2,1,0:T(8,128)}), f32[16,8,128]{2,1,0:T(8,128)S(1)}, u32[]{:S(2)}, u32[]{:S(2)}) async-start(f32[16,8,128]{2,1,0:T(8,128)} %broadcast_in_dim.20), calls=%async_computation.1 | async-start | bytes 131072 | tf_op jit(solution)/shard_map/all_to_all | solution.py:282
  76.5 2.0 %collective-permute-start.13 = (bf16[4,8,32,256]{3,2,1,0:T(8,128)(2,1)S(1)}, bf16[4,8,32,256]{3,2,1,0:T(8,128)(2,1)S(1)}, u32[]{:S(2)}, u32[]{:S(2)}) collective-permute-start(bf16[4,8,32,256]{3,2,1,0:T(8,128)(2,1)S(1)} %shard_map.111), channel_id=1, source_target_pairs={{0,16},{16,0},{1,17},{17,1},{2,18},{18,2},{3,19},{19,3},{4,20},{20... | collective-permute-start | bytes 1572872 | tf_op jit(solution)/shard_map/ppermute | solution.py:267

commit v3 on v2

--- a/solution.py
+++ b/solution.py
@@ -139,59 +139,79 @@
         start[q] = (params[q] - share * momentum[q]).astype(jnp.bfloat16)
 
 
-def owner_kernel(hold, plus, minus, near, far, average, narrow, partial):
+def owner_kernel(hold, plus, minus, near, far, average, narrow):
     for q in range(MODULES):
         total = hold[0, q].astype(jnp.float32)
         for part in (plus[0, q], minus[0, q], near[q], far[q]):
             total += part.astype(jnp.float32)
         average[q] = total
         narrow[q] = total.astype(jnp.bfloat16)
-        squares = total * total
-        squares = squares[:, :128] + squares[:, 128:]
-        partial[q : q + 1] = jnp.sum(squares, axis=0, keepdims=True)
-
-
-def factors(entries, sums):
-    total = jnp.sum(sums, axis=1, keepdims=True)
-    return jnp.minimum(1.0, CLIP_RMS / jnp.sqrt(total / entries + EPSILON_SQ))
-
-
-def state_kernel(entries, table, sums, average, params, momentum, momentum_out, params_out):
-    factor = factors(entries, jnp.sum(sums[...], axis=0))
+
+
+def squares_kernel(own, far, near, out):
+    lane = lax.broadcasted_iota(jnp.int32, (1, out.shape[1]), 1)
     for q in range(MODULES):
-        skipped = table[SKIPPED + q][:1] > 0
-        clipped = factor[q : q + 1] * average[q]
-        before, old = momentum[q], params[q]
+        row = jnp.zeros(lane.shape, jnp.float32)
+        for i, block in enumerate((own, far, near)):
+            value = block[q].astype(jnp.float32)
+            total = jnp.sum(jnp.sum(value * value, axis=0, keepdims=True), axis=1, keepdims=True)
+            row = jnp.where(lane == i, total, row)
+        out[q : q + 1] = row
+
+
+def second_kernel(own, far, near, plus, minus):
+    for q in range(MODULES):
+        plus[q] = own[q]
+        plus[MODULES + q] = far[q]
+        minus[q] = own[q]
+        minus[MODULES + q] = far[q]
+        minus[2 * MODULES + q] = near[q]
+
+
+def parts_of(own, near, far, plus, minus):
+    def piece(ref, at):
+        return ref.at[pl.ds(at * MODULES, MODULES)]
+
+    return (own, piece(minus, 0), near, piece(minus, 2), piece(plus, 1), far, piece(minus, 1), piece(plus, 0))
+
+
+def select(row, table, parts, out):
+    z, _, sign = place()
+    for which in range(2):
+        for slot, part in enumerate(parts_of(*parts[5 * which : 5 * which + 5])):
+            chip = chip_at(z, sign, slot)
+            for l in range(LEVELS):
+                upper = table[row + l][:1]
+                value = jnp.where(upper > 0, part[2 * l + 1].astype(jnp.float32), part[2 * l].astype(jnp.float32))
+                out[which, l, chip] = value.astype(jnp.bfloat16)
+
+
+def select_kernel(row, table, *refs):
+    *parts, out = refs
+    select(row, table, parts, out)
+
+
+def last_kernel(entries, table, sums, other_sums, mine, got, average, params, momentum, path_out, momentum_out, params_out):
+    l = pl.program_id(0)
+    core = lax.axis_index("core")
+    total = jnp.sum(sums[...] + other_sums[...], axis=1, keepdims=True)
+    factor = jnp.minimum(1.0, CLIP_RMS / jnp.sqrt(total / entries + EPSILON_SQ))
+    row = lax.broadcasted_iota(jnp.int32, factor.shape, 0)
+    low, high = (jnp.sum(jnp.where(row == 2 * l + m, factor, 0.0), axis=0, keepdims=True) for m in range(2))
+    for m, scale in enumerate((low, high)):
+        skipped = table[SKIPPED + 2 * l + m][:1] > 0
+        clipped = scale * average[m]
+        before, old = momentum[m], params[m]
         after = jnp.where(skipped, before, MOMENTUM_COEF * before + clipped)
-        momentum_out[q] = after
-        params_out[q] = jnp.where(skipped, old, old - OUTER_RATE * (clipped + MOMENTUM_COEF * after))
-
-
-def parts_of(own, near, far, plus, minus):
-    return (own, minus.at[0], near, minus.at[2], plus.at[1], far, minus.at[1], plus.at[0])
-
-
-def new_kernel(entries, row, table, sums, *refs):
-    z, _, sign = place()
-    *parts, out = refs
-    starts, averages = parts_of(*parts[:5]), parts_of(*parts[5:])
-    factor = CLIPPED_COEF * factors(entries, jnp.sum(sums[...], axis=0))
-    for l in range(LEVELS):
-        upper = table[row + l][:1]
-        scale_low, scale_high = (1.0 - upper) * factor[2 * l : 2 * l + 1], upper * factor[2 * l + 1 : 2 * l + 2]
-        for slot in range(CHIPS):
-            start, average = starts[slot], averages[slot]
-            base = jnp.where(upper > 0, start[2 * l + 1].astype(jnp.float32), start[2 * l].astype(jnp.float32))
-            moved = scale_low * average[2 * l].astype(jnp.float32) + scale_high * average[2 * l + 1].astype(jnp.float32)
-            out[l, chip_at(z, sign, slot)] = (base - moved).astype(jnp.bfloat16)
-
-
-def join_kernel(mine, got, out):
-    core = lax.axis_index("core")
+        momentum_out[m] = after
+        params_out[m] = jnp.where(skipped, old, old - OUTER_RATE * (clipped + MOMENTUM_COEF * after))
+    upper = table[OWN_UPPER + l][:1] > 0
+    scale = CLIPPED_COEF * jnp.where(upper, high, low)
     for half, part in ((core, mine), (1 - core, got)):
         for block in range(CHIPS):
             at = pl.ds(pl.multiple_of((2 * block + half) * BLOCK, BLOCK), BLOCK)
-            out[0, :, at] = part[0, block]
+            new = part[0, l, block].astype(jnp.float32) - scale * part[1, l, block].astype(jnp.float32)
+            path_out[0, :, at] = new.astype(jnp.bfloat16)
 
 
 def cost(bytes_accessed):
@@ -218,7 +238,7 @@
     shapes = [jax.ShapeDtypeStruct(s, d) for s, d in outs]
 
     def one(shape):
-        return pl.BlockSpec((1, *shape[1:]), lambda l: (l, *[0] * (len(shape) - 1)))
+        return pl.BlockSpec((shape[0] // LEVELS, *shape[1:]), lambda l: (l, *[0] * (len(shape) - 1)))
 
     return pl.pallas_call(
         kernel,
@@ -229,6 +249,34 @@
         cost_estimate=cost(size_of(args) + size_of(shapes)),
         compiler_params=pltpu.CompilerParams(vmem_limit_bytes=24 * 2**20),
     )(*fixed, *args)
+
+
+def last(entries, table, sums, other_sums, mine, got, average, params, momentum):
+    _, _, _, rows, _ = mine.shape
+    outs = [
+        jax.ShapeDtypeStruct((LEVELS, rows, 2 * CHIPS * BLOCK), jnp.bfloat16),
+        *[jax.ShapeDtypeStruct(average.shape, jnp.float32)] * 2,
+    ]
+
+    def one(shape):
+        return pl.BlockSpec((shape[0] // LEVELS, *shape[1:]), lambda l: (l, *[0] * (len(shape) - 1)))
+
+    return pl.pallas_call(
+        lambda *refs: last_kernel(entries, *refs),
+        grid=(LEVELS,),
+        out_shape=outs,
+        in_specs=[
+            VMEM,
+            VMEM,
+            VMEM,
+            VMEM,
+            VMEM,
+            *[one(average.shape)] * 3,
+        ],
+        out_specs=[one(o.shape) for o in outs],
+        cost_estimate=cost(size_of((mine, got, average, params, momentum)) + size_of(outs)),
+        compiler_params=pltpu.CompilerParams(vmem_limit_bytes=24 * 2**20),
+    )(table, sums, other_sums, mine, got, average, params, momentum)
 
 
 def given_half(routes, counts, flags, delta, feedback):
@@ -254,13 +302,16 @@
     )(routes, counts, flags, delta, feedback)
 
 
-def jump(x, steps):
+def moved(x, up, down):
     def target(p):
         z, core = divmod(p, 2)
-        sign = 1 - 2 * core
-        return 2 * ((z + sign * steps) % CHIPS) + core
+        return 2 * ((z + (down if core else up)) % CHIPS) + core
 
     return lax.ppermute(x, PATH, [(p, target(p)) for p in range(PATHS)])
+
+
+def jump(x, steps):
+    return moved(x, steps, -steps)
 
 
 def swap(x):
@@ -272,14 +323,14 @@
 
 
 def spread_near(x, far, near):
-    plus = jump(jnp.stack([x, far]), 1)
-    minus = jump(jnp.stack([x, far, near]), -1)
-    return x, near, far, plus, minus
-
-
-def summed(x, axes):
-    parts = jnp.broadcast_to(x[None], (lax.axis_size(axes), *x.shape))
-    return lax.all_to_all(parts, axes, 0, 0)
+    _, *tile = x.shape
+    plus, minus = call(second_kernel, [((n * MODULES, *tile), x.dtype) for n in (2, 3)], x, far, near)
+    return x, near, far, jump(plus, 1), jump(minus, -1)
+
+
+def over_plane(x):
+    parts = jnp.broadcast_to(x[None], (lax.axis_size(FSDP), *x.shape))
+    return jnp.sum(lax.all_to_all(parts, FSDP, 0, 0), axis=0)
 
 
 def on_device(path_delta, feedback, global_params, momentum, routes, token_counts, skip_flags):
@@ -306,33 +357,34 @@
     reduced_near = jump(hold[2] + plus[2], 2)
     reduced_far = jump(hold[1] + plus[1] + minus[1], -3)
     starts = spread_near(start, far, near)
-    average, narrow, partial = call(
+    average, narrow = call(
         owner_kernel,
-        [(block, f32), (block, bf16), ((MODULES, 128), f32)],
+        [(block, f32), (block, bf16)],
         hold,
         plus,
         minus,
         reduced_near,
         reduced_far,
     )
-    sums = jnp.sum(summed(partial, FSDP), axis=0)
     far, near = spread_far(narrow)
-    narrow, sums = lax.optimization_barrier((narrow, sums))
     averages = spread_near(narrow, far, near)
-    sums = summed(sums, PATH)
-
-    def bound(kernel, *values):
-        return lambda *refs: kernel(*values, *refs)
-
-    momentum_next, params_next = call(
-        bound(state_kernel, entries), [(block, f32)] * 2, table, sums, average, params, momentum
+    (squares,) = call(squares_kernel, [((MODULES, 128), f32)], narrow, far, near)
+    sums = over_plane(squares)
+    later, sums = lax.optimization_barrier((table, sums))
+    lane = lax.broadcasted_iota(jnp.int32, sums.shape, 1)
+    sums = sums + jump(jnp.where(lane < 2, sums, 0.0), 1) + jump(sums, -1)
+    other_sums = swap(sums)
+
+    def bound(kernel, value):
+        return lambda *refs: kernel(value, *refs)
+
+    chosen = [((2, *half), bf16)]
+    (give,) = call(bound(select_kernel, SIBLING_UPPER), chosen, later, *starts, *averages)
+    got = swap(give)
+    (mine,) = call(bound(select_kernel, OWN_UPPER), chosen, later, *starts, *averages)
+    path_params, momentum_next, params_next = last(
+        entries, table, sums, other_sums, mine, got, average, params, momentum
     )
-    (give,) = call(
-        bound(new_kernel, entries, SIBLING_UPPER), [(half, bf16)], table, sums, *starts, *averages
-    )
-    got = swap(give)
-    (mine,) = call(bound(new_kernel, entries, OWN_UPPER), [(half, bf16)], table, sums, *starts, *averages)
-    (path_params,) = levelwise(join_kernel, [(delta.shape, bf16)], (), mine, got)
     shape = global_params.shape
     return feedback_next[None], momentum_next.reshape(shape), params_next.reshape(shape), path_params[None]
 

time: 80.3 us -> 78.3 us (0.975)
  blocking collectives: 0 us -> 13.1 us
  waiting for transfers between devices: 26.9 us -> 19.5 us
  starting transfers between devices: 38.8 us -> 33.8 us
  other arithmetic: 2.34 us -> 0.07 us
  local copies, waits for them, and re-layouts: 2.33 us -> 1.07 us
  Pallas kernels: 8.92 us -> 9.91 us
    all_to_all x2 -> x0, starting transfers between devices: 17.6 us -> none  [summed(): return lax.all_to_all(parts, axes, 0, 0)]
    all_to_all x0 -> x1, blocking collectives: none -> 13.1 us  [over_plane(): return jnp.sum(lax.all_to_all(parts, FSDP, 0, 0), axis=0)]
    all_to_all x2 -> x0, waiting for transfers between devices: 12.9 us -> none  [summed(): return lax.all_to_all(parts, axes, 0, 0)]
    ppermute x12 -> x14, starting transfers between devices: 17.6 us -> 27.6 us  [moved(): return lax.ppermute(x, PATH, [(p, target(p)) for p in range(PATHS)])]
    ppermute x12 -> x14, waiting for transfers between devices: 13 us -> 18 us  [moved(): return lax.ppermute(x, PATH, [(p, target(p)) for p in range(PATHS)])]
    ppermute x2 -> x3, starting transfers between devices: 3.58 us -> 6.19 us  [swap(): return lax.ppermute(x, 'core', [(0, 1), (1, 0)])]
    another operation x4 -> x0, other arithmetic: 2.29 us -> none  [the longest x2 1.45 us: spread_near(): plus = jump(jnp.stack([x, far]), 1)]
    pallas_call x0 -> x1, Pallas kernels: none -> 2.03 us  [last(): pl.pallas_call(lambda *refs: last_kernel(entries, *refs), grid=(LEVELS,),...]
  transfers between devices with their start and end apart: 16 -> 17, of which waited for: 6 -> 9; matrix products, arithmetic and copies ran while one was open for 4% -> 0% of each run, Pallas kernels for 5% -> 6%
where the time goes in v3:
time: 78.3 us; the launch traced here: 78.1 us
  starting transfers between devices  33.8 us (43%)
  waiting for transfers between devices  19.5 us (25%)
  blocking collectives  13.1 us (17%)
  Pallas kernels  9.91 us (13%)
  local copies, waits for them, and re-layouts  1.07 us (1%)
    ppermute x14, starting transfers between devices, moved(): return lax.ppermute(x, PATH, [(p, target(p)) for p in range(PATHS)])  27.6 us
    ppermute x14, waiting for transfers between devices, moved(): return lax.ppermute(x, PATH, [(p, target(p)) for p in range(PATHS)])  18 us
    all_to_all x1, blocking collectives, over_plane(): return jnp.sum(lax.all_to_all(parts, FSDP, 0, 0), axis=0)  13.1 us
    ppermute x3, starting transfers between devices, swap(): return lax.ppermute(x, 'core', [(0, 1), (1, 0)])  6.19 us
    pallas_call x1, Pallas kernels, given_half(): pl.pallas_call(give_kernel, out_shape=[half, table], in_specs=[HBM] * 5,...  2.94 us
    pallas_call x10, Pallas kernels, call(): pl.pallas_call(kernel, out_shape=shapes, in_specs=[VMEM] * len(args), out...  2.92 us
    pallas_call x1, Pallas kernels, last(): pl.pallas_call(lambda *refs: last_kernel(entries, *refs), grid=(LEVELS,),...  2.03 us
    pallas_call x1, Pallas kernels, levelwise(): pl.pallas_call(kernel, grid=(LEVELS,), out_shape=shapes, in_specs=[VMEM]...  2.02 us
  transfers between devices with their start and end apart: 17, of which 9 were waited for; matrix products, arithmetic and copies ran while one was open for 0% of the time, Pallas kernels for 6%

profile of v3, /device:TPU:1, one launch (start us, length us, event | category | flops | bytes accessed | tf_op | source)
XLA Modules:
  0.0 78.1 jit_solution(14628545702712936474)
XLA Ops:
  0.7 2.9 %shard_map.102 = (bf16[4,8,32,256]{3,2,1,0:T(8,128)(2,1)}, f32[24,8,256]{2,1,0:T(8,128)}) custom-call(s32[4,16]{1,0:T(4,128)} %bitcast.26, s32[4,16]{1,0:T(4,128)} %bitcast.27, s32[2,4]{1,0:T(2,128)} %bitcast.28, bf16[4,32,4096]{2,1,0:T(8,128)(2,1)} %bitcast.18, f32[4,32,4096]{2,1,0:T(8,128)} %bitcast.15), custom_call_target="tpu_custom_call" | custom-call | bytes 4194304 | tf_op jit(solution)/shard_map/pallas_call | solution.py:286
  3.6 3.3 %collective-permute-start = (bf16[4,8,32,256]{3,2,1,0:T(8,128)(2,1)}, bf16[4,8,32,256]{3,2,1,0:T(8,128)(2,1)S(1)}, u32[]{:S(2)}, u32[]{:S(2)}) collective-permute-start(bf16[4,8,32,256]{3,2,1,0:T(8,128)(2,1)} %get-tuple-element.24), channel_id=1, source_target_pairs={{0,16},{16,0},{1,17},{17,1},{2,18},{18,2},{3,19},{19,3},{4,20},{20... | collective-permute-start | bytes 1572872 | tf_op jit(solution)/shard_map/ppermute | solution.py:318
  6.9 0.9 %copy-done.1 = f32[24,8,256]{2,1,0:T(8,128)S(1)} copy-done((f32[24,8,256]{2,1,0:T(8,128)S(1)}, f32[24,8,256]{2,1,0:T(8,128)}, u32[]{:S(2)}) %copy-start.1) | copy-done | bytes 196632
  9.0 3.9 %collective-permute-start.1 = (bf16[3,8,32,256]{3,2,1,0:T(8,128)(2,1)S(1)}, bf16[3,8,32,256]{3,2,1,0:T(8,128)(2,1)S(1)}, u32[]{:S(2)}, u32[]{:S(2)}) collective-permute-start(bf16[3,8,32,256]{3,2,1,0:T(8,128)(2,1)S(1)} %get-tuple-element.30), channel_id=1, source_target_pairs={{0,32},{16,240},{32,64},{48,16},{64,96},{80,48},{96,128},{112,80},... | collective-permute-start | bytes 1179656 | tf_op jit(solution)/shard_map/ppermute | solution.py:310
  13.0 2.0 %shard_map.107 = f32[4,32,4096]{2,1,0:T(8,128)} custom-call(f32[24,8,256]{2,1,0:T(8,128)S(1)} %copy-done.2, bf16[4,32,4096]{2,1,0:T(8,128)(2,1)S(1)} %bitcast.20, f32[4,32,4096]{2,1,0:T(8,128)S(1)} %bitcast.17), custom_call_target="tpu_custom_call" | custom-call | bytes 5242880 | tf_op jit(solution)/shard_map/pallas_call | solution.py:243
  15.1 6.2 %collective-permute-done.2.minus = bf16[2,8,32,256]{3,2,1,0:T(8,128)(2,1)S(1)} collective-permute-done((bf16[2,8,32,256]{3,2,1,0:T(8,128)(2,1)S(1)}, bf16[2,8,32,256]{3,2,1,0:T(8,128)(2,1)S(1)}, u32[]{:S(2)}, u32[]{:S(2)}) %collective-permute-start.2) | collective-permute-done | bytes 262176 | tf_op jit(solution)/shard_map/ppermute | solution.py:310
  21.5 1.4 %collective-permute-start.3 = (bf16[8,32,256]{2,1,0:T(8,128)(2,1)S(1)}, bf16[8,32,256]{2,1,0:T(8,128)(2,1)S(1)}, u32[]{:S(2)}, u32[]{:S(2)}) collective-permute-start(bf16[8,32,256]{2,1,0:T(8,128)(2,1)S(1)} %get-tuple-element.43), channel_id=1, source_target_pairs={{0,64},{16,208},{32,96},{48,240},{64,128},{80,16},{96,160},{112,48... | collective-permute-start | bytes 393224 | tf_op jit(solution)/shard_map/ppermute | solution.py:310
  22.9 4.4 %collective-permute-start.11 = (bf16[8,32,256]{2,1,0:T(8,128)(2,1)S(1)}, bf16[8,32,256]{2,1,0:T(8,128)(2,1)S(1)}, u32[]{:S(2)}, u32[]{:S(2)}) collective-permute-start(bf16[8,32,256]{2,1,0:T(8,128)(2,1)S(1)} %shard_map.105.own.refs_1_), channel_id=1, source_target_pairs={{0,96},{16,176},{32,128},{48,208},{64,160},{80,240},{96,192},{112,... | collective-permute-start | bytes 393224 | tf_op jit(solution)/shard_map/ppermute | solution.py:310
  27.3 1.0 %collective-permute-start.10 = (bf16[8,32,256]{2,1,0:T(8,128)(2,1)S(1)}, bf16[8,32,256]{2,1,0:T(8,128)(2,1)S(1)}, u32[]{:S(2)}, u32[]{:S(2)}) collective-permute-start(bf16[8,32,256]{2,1,0:T(8,128)(2,1)S(1)} %shard_map.105.own.refs_1_), channel_id=1, source_target_pairs={{0,192},{16,80},{32,224},{48,112},{64,0},{80,144},{96,32},{112,176... | collective-permute-start | bytes 393224 | tf_op jit(solution)/shard_map/ppermute | solution.py:310
  28.3 3.4 %collective-permute-done.4.far = bf16[8,32,256]{2,1,0:T(8,128)(2,1)S(1)} collective-permute-done((bf16[8,32,256]{2,1,0:T(8,128)(2,1)S(1)}, bf16[8,32,256]{2,1,0:T(8,128)(2,1)S(1)}, u32[]{:S(2)}, u32[]{:S(2)}) %collective-permute-start.4) | collective-permute-done | bytes 131104 | tf_op jit(solution)/shard_map/ppermute | solution.py:310
  31.8 4.4 %collective-permute-start.6 = (bf16[8,32,256]{2,1,0:T(8,128)(2,1)S(1)}, bf16[8,32,256]{2,1,0:T(8,128)(2,1)S(1)}, u32[]{:S(2)}, u32[]{:S(2)}) collective-permute-start(bf16[8,32,256]{2,1,0:T(8,128)(2,1)S(1)} %get-tuple-element.31.own.refs_6_), channel_id=1, source_target_pairs={{0,192},{16,80},{32,224},{48,112},{64,0},{80,144},{96,32},{112,176... | collective-permute-start | bytes 393224 | tf_op jit(solution)/shard_map/ppermute | solution.py:310
  36.2 2.4 %collective-permute-start.5 = (bf16[8,32,256]{2,1,0:T(8,128)(2,1)S(1)}, bf16[8,32,256]{2,1,0:T(8,128)(2,1)S(1)}, u32[]{:S(2)}, u32[]{:S(2)}) collective-permute-start(bf16[8,32,256]{2,1,0:T(8,128)(2,1)S(1)} %get-tuple-element.31.own.refs_6_), channel_id=1, source_target_pairs={{0,96},{16,176},{32,128},{48,208},{64,160},{80,240},{96,192},{112,... | collective-permute-start | bytes 393224 | tf_op jit(solution)/shard_map/ppermute | solution.py:310
  39.8 1.3 %collective-permute-start.13 = (bf16[24,32,256]{2,1,0:T(8,128)(2,1)S(1)}, bf16[24,32,256]{2,1,0:T(8,128)(2,1)S(1)}, u32[]{:S(2)}, u32[]{:S(2)}) collective-permute-start(bf16[24,32,256]{2,1,0:T(8,128)(2,1)S(1)} %get-tuple-element.35), channel_id=1, source_target_pairs={{0,224},{16,48},{32,0},{48,80},{64,32},{80,112},{96,64},{112,144},... | collective-permute-start | bytes 1179656 | tf_op jit(solution)/shard_map/ppermute | solution.py:310
  41.1 3.1 %collective-permute-done.6.near.refs_7_ = bf16[8,32,256]{2,1,0:T(8,128)(2,1)S(1)} collective-permute-done((bf16[8,32,256]{2,1,0:T(8,128)(2,1)S(1)}, bf16[8,32,256]{2,1,0:T(8,128)(2,1)S(1)}, u32[]{:S(2)}, u32[]{:S(2)}) %collective-permute-start.6) | collective-permute-done | bytes 131104 | tf_op jit(solution)/shard_map/ppermute | solution.py:310
  44.1 1.2 %collective-permute-done.5.far.refs_8_ = bf16[8,32,256]{2,1,0:T(8,128)(2,1)S(1)} collective-permute-done((bf16[8,32,256]{2,1,0:T(8,128)(2,1)S(1)}, bf16[8,32,256]{2,1,0:T(8,128)(2,1)S(1)}, u32[]{:S(2)}, u32[]{:S(2)}) %collective-permute-start.5) | collective-permute-done | bytes 131104 | tf_op jit(solution)/shard_map/ppermute | solution.py:310
  45.3 0.9 %shard_map.111 = (bf16[16,32,256]{2,1,0:T(8,128)(2,1)}, bf16[24,32,256]{2,1,0:T(8,128)(2,1)}) custom-call(bf16[8,32,256]{2,1,0:T(8,128)(2,1)S(1)} %get-tuple-element.31.own.refs_6_, bf16[8,32,256]{2,1,0:T(8,128)(2,1)S(1)} %collective-permute-done.5.far.refs_8_, bf16[8,32,256]{2,1,0:T(8,128)(2,1)S(1)} %collective-permute-done.6.near.refs_7_), custom_call_target="tpu_custom_call" | custom-call | bytes 1048576 | tf_op jit(solution)/shard_map/pallas_call | solution.py:227
  46.3 4.1 %collective-permute-start.12 = (bf16[16,32,256]{2,1,0:T(8,128)(2,1)}, bf16[16,32,256]{2,1,0:T(8,128)(2,1)S(1)}, u32[]{:S(2)}, u32[]{:S(2)}) collective-permute-start(bf16[16,32,256]{2,1,0:T(8,128)(2,1)} %get-tuple-element.34), channel_id=1, source_target_pairs={{0,32},{16,240},{32,64},{48,16},{64,96},{80,48},{96,128},{112,80},... | collective-permute-start | bytes 786440 | tf_op jit(solution)/shard_map/ppermute | solution.py:310
  50.4 1.5 %collective-permute-start.14 = (bf16[16,32,256]{2,1,0:T(8,128)(2,1)}, bf16[16,32,256]{2,1,0:T(8,128)(2,1)S(1)}, u32[]{:S(2)}, u32[]{:S(2)}) collective-permute-start(bf16[16,32,256]{2,1,0:T(8,128)(2,1)} %get-tuple-element.36), channel_id=1, source_target_pairs={{0,32},{16,240},{32,64},{48,16},{64,96},{80,48},{96,128},{112,80},... | collective-permute-start | bytes 786440 | tf_op jit(solution)/shard_map/ppermute | solution.py:310
  52.0 13.1 %all_to_all.5 = f32[16,8,128]{2,1,0:T(8,128)S(1)} all-to-all(f32[16,8,128]{2,1,0:T(8,128)S(1)} %broadcast_in_dim.17), channel_id=1, replica_groups=mesh['z'=8,'core'=2,'y'=4,'x'=4] {'y','x'}, dimensions={0} | all-to-all | bytes 131072 | tf_op jit(solution)/shard_map/all_to_all | solution.py:333
  65.4 2.9 %collective-permute-start.16 = (bf16[2,4,8,32,256]{4,3,2,1,0:T(8,128)(2,1)S(1)}, bf16[2,4,8,32,256]{4,3,2,1,0:T(8,128)(2,1)S(1)}, u32[]{:S(2)}, u32[]{:S(2)}) collective-permute-start(bf16[2,4,8,32,256]{4,3,2,1,0:T(8,128)(2,1)S(1)} %shard_map.113), channel_id=1, source_target_pairs={{0,16},{16,0},{1,17},{17,1},{2,18},{18,2},{3,19},{19,3},{4,20},{20... | collective-permute-start | bytes 3145736 | tf_op jit(solution)/shard_map/ppermute | solution.py:318
  68.3 3.0 %collective-permute-start.7 = (f32[8,128]{1,0:T(8,128)S(1)}, f32[8,128]{1,0:T(8,128)S(1)}, u32[]{:S(2)}, u32[]{:S(2)}) collective-permute-start(f32[8,128]{1,0:T(8,128)S(1)} %broadcast_select_fusion), channel_id=1, source_target_pairs={{0,32},{16,240},{32,64},{48,16},{64,96},{80,48},{96,128},{112,80},... | collective-permute-start | bytes 12296 | tf_op jit(solution)/shard_map/ppermute | solution.py:310
  72.0 2.9 %collective-permute-done.8 = f32[8,128]{1,0:T(8,128)S(1)} collective-permute-done((f32[8,128]{1,0:T(8,128)S(1)}, f32[8,128]{1,0:T(8,128)S(1)}, u32[]{:S(2)}, u32[]{:S(2)}) %collective-permute-start.8) | collective-permute-done | bytes 4128 | tf_op jit(solution)/shard_map/ppermute | solution.py:310
  75.2 0.9 %collective-permute-done.9.refs_2_ = f32[8,128]{1,0:T(8,128)S(1)} collective-permute-done((f32[8,128]{1,0:T(8,128)S(1)}, f32[8,128]{1,0:T(8,128)S(1)}, u32[]{:S(2)}, u32[]{:S(2)}) %collective-permute-start.9) | collective-permute-done | bytes 4128 | tf_op jit(solution)/shard_map/ppermute | solution.py:318
  76.1 2.0 %shard_map.114 = (bf16[4,32,4096]{2,1,0:T(8,128)(2,1)}, f32[8,32,256]{2,1,0:T(8,128)}, f32[8,32,256]{2,1,0:T(8,128)}) custom-call(f32[24,8,256]{2,1,0:T(8,128)S(1)} %copy-done.2, f32[8,128]{1,0:T(8,128)S(1)} %add_add_fusion.refs_1_, f32[8,128]{1,0:T(8,128)S(1)} %collective-permute-done.9.refs_2_, bf16[2,4,8,32,256]{4,3,2,1,0:T(8,128)(2,1)S(1)} %shard_map.112.refs_3_, ...), custom_call_target="tpu_custom_call" | custom-call | bytes 4456448 | tf_op jit(solution)/shard_map/pallas_call | solution.py:264
  (42 shorter events, 4.3 us)
Async XLA Ops:
  0.6 6.3 %copy-start = (f32[1,4,32,4096]{3,2,1,0:T(8,128)S(1)}, f32[1,4,32,4096]{3,2,1,0:T(8,128)}, u32[]{:S(2)}) copy-start(f32[1,4,32,4096]{3,2,1,0:T(8,128)} %param.8) | copy-start | bytes 6291460
  0.6 6.3 %copy-start.3 = (bf16[1,4,32,4096]{3,2,1,0:T(8,128)(2,1)S(1)}, bf16[1,4,32,4096]{3,2,1,0:T(8,128)(2,1)}, u32[]{:S(2)}) copy-start(bf16[1,4,32,4096]{3,2,1,0:T(8,128)(2,1)} %param.7) | copy-start | bytes 3145732
  3.6 5.1 %collective-permute-start = (bf16[4,8,32,256]{3,2,1,0:T(8,128)(2,1)}, bf16[4,8,32,256]{3,2,1,0:T(8,128)(2,1)S(1)}, u32[]{:S(2)}, u32[]{:S(2)}) collective-permute-start(bf16[4,8,32,256]{3,2,1,0:T(8,128)(2,1)} %get-tuple-element.24), channel_id=1, source_target_pairs={{0,16},{16,0},{1,17},{17,1},{2,18},{18,2},{3,19},{19,3},{4,20},{20... | collective-permute-start | bytes 1572872 | tf_op jit(solution)/shard_map/ppermute | solution.py:318
  6.9 0.9 %copy-start.1 = (f32[24,8,256]{2,1,0:T(8,128)S(1)}, f32[24,8,256]{2,1,0:T(8,128)}, u32[]{:S(2)}) copy-start(f32[24,8,256]{2,1,0:T(8,128)} %get-tuple-element.33.table.refs_0_) | copy-start | bytes 589828
  7.9 0.9 %copy-start.2 = (f32[24,8,256]{2,1,0:T(8,128)S(1)}, f32[24,8,256]{2,1,0:T(8,128)}, u32[]{:S(2)}) copy-start(f32[24,8,256]{2,1,0:T(8,128)} %get-tuple-element.33.table.refs_0_) | copy-start | bytes 589828
  7.9 5.1 %copy-start.4 = (f32[4,2,32,256]{3,2,1,0:T(8,128)S(1)}, f32[4,2,32,256]{3,2,1,0:T(8,128)}, u32[]{:S(2)}) copy-start(f32[4,2,32,256]{3,2,1,0:T(8,128)} %param.9) | copy-start | bytes 786436
  7.9 5.1 %copy-start.5 = (f32[4,2,32,256]{3,2,1,0:T(8,128)S(1)}, f32[4,2,32,256]{3,2,1,0:T(8,128)}, u32[]{:S(2)}) copy-start(f32[4,2,32,256]{3,2,1,0:T(8,128)} %param.10) | copy-start | bytes 786436
  9.0 12.3 %collective-permute-start.1 = (bf16[3,8,32,256]{3,2,1,0:T(8,128)(2,1)S(1)}, bf16[3,8,32,256]{3,2,1,0:T(8,128)(2,1)S(1)}, u32[]{:S(2)}, u32[]{:S(2)}) collective-permute-start(bf16[3,8,32,256]{3,2,1,0:T(8,128)(2,1)S(1)} %get-tuple-element.30), channel_id=1, source_target_pairs={{0,32},{16,240},{32,64},{48,16},{64,96},{80,48},{96,128},{112,80},... | collective-permute-start | bytes 1179656 | tf_op jit(solution)/shard_map/ppermute | solution.py:310
  12.9 8.4 %collective-permute-start.2 = (bf16[2,8,32,256]{3,2,1,0:T(8,128)(2,1)S(1)}, bf16[2,8,32,256]{3,2,1,0:T(8,128)(2,1)S(1)}, u32[]{:S(2)}, u32[]{:S(2)}) collective-permute-start(bf16[2,8,32,256]{3,2,1,0:T(8,128)(2,1)S(1)} %get-tuple-element.25), channel_id=1, source_target_pairs={{0,224},{16,48},{32,0},{48,80},{64,32},{80,112},{96,64},{112,144},... | collective-permute-start | bytes 786440 | tf_op jit(solution)/shard_map/ppermute | solution.py:310
  21.4 10.3 %collective-permute-start.4 = (bf16[8,32,256]{2,1,0:T(8,128)(2,1)S(1)}, bf16[8,32,256]{2,1,0:T(8,128)(2,1)S(1)}, u32[]{:S(2)}, u32[]{:S(2)}) collective-permute-start(bf16[8,32,256]{2,1,0:T(8,128)(2,1)S(1)} %get-tuple-element.42), channel_id=1, source_target_pairs={{0,160},{16,112},{32,192},{48,144},{64,224},{80,176},{96,0},{112,2... | collective-permute-start | bytes 393224 | tf_op jit(solution)/shard_map/ppermute | solution.py:310
  21.5 10.3 %collective-permute-start.3 = (bf16[8,32,256]{2,1,0:T(8,128)(2,1)S(1)}, bf16[8,32,256]{2,1,0:T(8,128)(2,1)S(1)}, u32[]{:S(2)}, u32[]{:S(2)}) collective-permute-start(bf16[8,32,256]{2,1,0:T(8,128)(2,1)S(1)} %get-tuple-element.43), channel_id=1, source_target_pairs={{0,64},{16,208},{32,96},{48,240},{64,128},{80,16},{96,160},{112,48... | collective-permute-start | bytes 393224 | tf_op jit(solution)/shard_map/ppermute | solution.py:310
  22.9 16.2 %collective-permute-start.11 = (bf16[8,32,256]{2,1,0:T(8,128)(2,1)S(1)}, bf16[8,32,256]{2,1,0:T(8,128)(2,1)S(1)}, u32[]{:S(2)}, u32[]{:S(2)}) collective-permute-start(bf16[8,32,256]{2,1,0:T(8,128)(2,1)S(1)} %shard_map.105.own.refs_1_), channel_id=1, source_target_pairs={{0,96},{16,176},{32,128},{48,208},{64,160},{80,240},{96,192},{112,... | collective-permute-start | bytes 393224 | tf_op jit(solution)/shard_map/ppermute | solution.py:310
  27.3 11.8 %collective-permute-start.10 = (bf16[8,32,256]{2,1,0:T(8,128)(2,1)S(1)}, bf16[8,32,256]{2,1,0:T(8,128)(2,1)S(1)}, u32[]{:S(2)}, u32[]{:S(2)}) collective-permute-start(bf16[8,32,256]{2,1,0:T(8,128)(2,1)S(1)} %shard_map.105.own.refs_1_), channel_id=1, source_target_pairs={{0,192},{16,80},{32,224},{48,112},{64,0},{80,144},{96,32},{112,176... | collective-permute-start | bytes 393224 | tf_op jit(solution)/shard_map/ppermute | solution.py:310
  31.8 12.3 %collective-permute-start.6 = (bf16[8,32,256]{2,1,0:T(8,128)(2,1)S(1)}, bf16[8,32,256]{2,1,0:T(8,128)(2,1)S(1)}, u32[]{:S(2)}, u32[]{:S(2)}) collective-permute-start(bf16[8,32,256]{2,1,0:T(8,128)(2,1)S(1)} %get-tuple-element.31.own.refs_6_), channel_id=1, source_target_pairs={{0,192},{16,80},{32,224},{48,112},{64,0},{80,144},{96,32},{112,176... | collective-permute-start | bytes 393224 | tf_op jit(solution)/shard_map/ppermute | solution.py:310
  36.2 9.1 %collective-permute-start.5 = (bf16[8,32,256]{2,1,0:T(8,128)(2,1)S(1)}, bf16[8,32,256]{2,1,0:T(8,128)(2,1)S(1)}, u32[]{:S(2)}, u32[]{:S(2)}) collective-permute-start(bf16[8,32,256]{2,1,0:T(8,128)(2,1)S(1)} %get-tuple-element.31.own.refs_6_), channel_id=1, source_target_pairs={{0,96},{16,176},{32,128},{48,208},{64,160},{80,240},{96,192},{112,... | collective-permute-start | bytes 393224 | tf_op jit(solution)/shard_map/ppermute | solution.py:310
  39.8 25.3 %collective-permute-start.13 = (bf16[24,32,256]{2,1,0:T(8,128)(2,1)S(1)}, bf16[24,32,256]{2,1,0:T(8,128)(2,1)S(1)}, u32[]{:S(2)}, u32[]{:S(2)}) collective-permute-start(bf16[24,32,256]{2,1,0:T(8,128)(2,1)S(1)} %get-tuple-element.35), channel_id=1, source_target_pairs={{0,224},{16,48},{32,0},{48,80},{64,32},{80,112},{96,64},{112,144},... | collective-permute-start | bytes 1179656 | tf_op jit(solution)/shard_map/ppermute | solution.py:310
  46.2 18.9 %collective-permute-start.15 = (bf16[24,32,256]{2,1,0:T(8,128)(2,1)}, bf16[24,32,256]{2,1,0:T(8,128)(2,1)S(1)}, u32[]{:S(2)}, u32[]{:S(2)}) collective-permute-start(bf16[24,32,256]{2,1,0:T(8,128)(2,1)} %get-tuple-element.37), channel_id=1, source_target_pairs={{0,224},{16,48},{32,0},{48,80},{64,32},{80,112},{96,64},{112,144},... | collective-permute-start | bytes 1179656 | tf_op jit(solution)/shard_map/ppermute | solution.py:310
  46.3 18.8 %collective-permute-start.12 = (bf16[16,32,256]{2,1,0:T(8,128)(2,1)}, bf16[16,32,256]{2,1,0:T(8,128)(2,1)S(1)}, u32[]{:S(2)}, u32[]{:S(2)}) collective-permute-start(bf16[16,32,256]{2,1,0:T(8,128)(2,1)} %get-tuple-element.34), channel_id=1, source_target_pairs={{0,32},{16,240},{32,64},{48,16},{64,96},{80,48},{96,128},{112,80},... | collective-permute-start | bytes 786440 | tf_op jit(solution)/shard_map/ppermute | solution.py:310
  50.4 14.7 %collective-permute-start.14 = (bf16[16,32,256]{2,1,0:T(8,128)(2,1)}, bf16[16,32,256]{2,1,0:T(8,128)(2,1)S(1)}, u32[]{:S(2)}, u32[]{:S(2)}) collective-permute-start(bf16[16,32,256]{2,1,0:T(8,128)(2,1)} %get-tuple-element.36), channel_id=1, source_target_pairs={{0,32},{16,240},{32,64},{48,16},{64,96},{80,48},{96,128},{112,80},... | collective-permute-start | bytes 786440 | tf_op jit(solution)/shard_map/ppermute | solution.py:310
  65.4 10.7 %collective-permute-start.16 = (bf16[2,4,8,32,256]{4,3,2,1,0:T(8,128)(2,1)S(1)}, bf16[2,4,8,32,256]{4,3,2,1,0:T(8,128)(2,1)S(1)}, u32[]{:S(2)}, u32[]{:S(2)}) collective-permute-start(bf16[2,4,8,32,256]{4,3,2,1,0:T(8,128)(2,1)S(1)} %shard_map.113), channel_id=1, source_target_pairs={{0,16},{16,0},{1,17},{17,1},{2,18},{18,2},{3,19},{19,3},{4,20},{20... | collective-permute-start | bytes 3145736 | tf_op jit(solution)/shard_map/ppermute | solution.py:318
  68.3 3.7 %collective-permute-start.7 = (f32[8,128]{1,0:T(8,128)S(1)}, f32[8,128]{1,0:T(8,128)S(1)}, u32[]{:S(2)}, u32[]{:S(2)}) collective-permute-start(f32[8,128]{1,0:T(8,128)S(1)} %broadcast_select_fusion), channel_id=1, source_target_pairs={{0,32},{16,240},{32,64},{48,16},{64,96},{80,48},{96,128},{112,80},... | collective-permute-start | bytes 12296 | tf_op jit(solution)/shard_map/ppermute | solution.py:310
  71.3 3.7 %collective-permute-start.8 = (f32[8,128]{1,0:T(8,128)S(1)}, f32[8,128]{1,0:T(8,128)S(1)}, u32[]{:S(2)}, u32[]{:S(2)}) collective-permute-start(f32[8,128]{1,0:T(8,128)S(1)} %reduce_sum.9), channel_id=1, source_target_pairs={{0,224},{16,48},{32,0},{48,80},{64,32},{80,112},{96,64},{112,144},... | collective-permute-start | bytes 12296 | tf_op jit(solution)/shard_map/ppermute | solution.py:310
  74.9 1.2 %collective-permute-start.9 = (f32[8,128]{1,0:T(8,128)S(1)}, f32[8,128]{1,0:T(8,128)S(1)}, u32[]{:S(2)}, u32[]{:S(2)}) collective-permute-start(f32[8,128]{1,0:T(8,128)S(1)} %add_add_fusion.refs_1_), channel_id=1, source_target_pairs={{0,16},{16,0},{1,17},{17,1},{2,18},{18,2},{3,19},{19,3},{4,20},{20... | collective-permute-start | bytes 12296 | tf_op jit(solution)/shard_map/ppermute | solution.py:318

commit v4 on v3

--- a/solution.py
+++ b/solution.py
@@ -159,36 +159,38 @@
         out[q : q + 1] = row
 
 
-def second_kernel(own, far, near, plus, minus):
-    for q in range(MODULES):
-        plus[q] = own[q]
-        plus[MODULES + q] = far[q]
-        minus[q] = own[q]
-        minus[MODULES + q] = far[q]
-        minus[2 * MODULES + q] = near[q]
-
-
-def parts_of(own, near, far, plus, minus):
-    def piece(ref, at):
-        return ref.at[pl.ds(at * MODULES, MODULES)]
-
-    return (own, piece(minus, 0), near, piece(minus, 2), piece(plus, 1), far, piece(minus, 1), piece(plus, 0))
-
-
-def select(row, table, parts, out):
+def second_kernel(*refs):
+    *blocks, plus, minus = refs
+    for i, block in enumerate(blocks):
+        which, kind = divmod(i, 3)
+        for q in range(MODULES):
+            value = block[q]
+            minus[(3 * which + kind) * MODULES + q] = value
+            if kind < 2:
+                plus[(2 * which + kind) * MODULES + q] = value
+
+
+def parts_of(which, own, far, near, plus, minus):
+    def above(at):
+        return plus.at[pl.ds((2 * which + at) * MODULES, MODULES)]
+
+    def below(at):
+        return minus.at[pl.ds((3 * which + at) * MODULES, MODULES)]
+
+    return (own, below(0), near, below(2), above(1), far, below(1), above(0))
+
+
+def select_kernel(row, table, *refs):
     z, _, sign = place()
+    *blocks, plus, minus, out = refs
     for which in range(2):
-        for slot, part in enumerate(parts_of(*parts[5 * which : 5 * which + 5])):
+        parts = parts_of(which, *blocks[3 * which : 3 * which + 3], plus, minus)
+        for slot, part in enumerate(parts):
             chip = chip_at(z, sign, slot)
             for l in range(LEVELS):
                 upper = table[row + l][:1]
                 value = jnp.where(upper > 0, part[2 * l + 1].astype(jnp.float32), part[2 * l].astype(jnp.float32))
                 out[which, l, chip] = value.astype(jnp.bfloat16)
-
-
-def select_kernel(row, table, *refs):
-    *parts, out = refs
-    select(row, table, parts, out)
 
 
 def last_kernel(entries, table, sums, other_sums, mine, got, average, params, momentum, path_out, momentum_out, params_out):
@@ -210,7 +212,7 @@
     for half, part in ((core, mine), (1 - core, got)):
         for block in range(CHIPS):
             at = pl.ds(pl.multiple_of((2 * block + half) * BLOCK, BLOCK), BLOCK)
-            new = part[0, l, block].astype(jnp.float32) - scale * part[1, l, block].astype(jnp.float32)
+            new = part[1, l, block].astype(jnp.float32) - scale * part[0, l, block].astype(jnp.float32)
             path_out[0, :, at] = new.astype(jnp.bfloat16)
 
 
@@ -322,10 +324,10 @@
     return jump(x, 3), jump(x, -2)
 
 
-def spread_near(x, far, near):
-    _, *tile = x.shape
-    plus, minus = call(second_kernel, [((n * MODULES, *tile), x.dtype) for n in (2, 3)], x, far, near)
-    return x, near, far, jump(plus, 1), jump(minus, -1)
+def spread_near(*blocks):
+    _, *tile = blocks[0].shape
+    plus, minus = call(second_kernel, [((n * MODULES, *tile), blocks[0].dtype) for n in (4, 6)], *blocks)
+    return *blocks, jump(plus, 1), jump(minus, -1)
 
 
 def over_plane(x):
@@ -352,11 +354,10 @@
     later, _ = lax.optimization_barrier((later, start))
     (hold,) = call(staying_kernel, [((3, *block), bf16)], later, keep, got)
     (feedback_next,) = levelwise(feedback_kernel, [(delta.shape, f32)], (later,), delta, feedback)
-    far, near = spread_far(start)
+    starts = start, *spread_far(start)
     hold, feedback_next = lax.optimization_barrier((hold, feedback_next))
     reduced_near = jump(hold[2] + plus[2], 2)
     reduced_far = jump(hold[1] + plus[1] + minus[1], -3)
-    starts = spread_near(start, far, near)
     average, narrow = call(
         owner_kernel,
         [(block, f32), (block, bf16)],
@@ -367,7 +368,7 @@
         reduced_far,
     )
     far, near = spread_far(narrow)
-    averages = spread_near(narrow, far, near)
+    spread = spread_near(narrow, far, near, *starts)
     (squares,) = call(squares_kernel, [((MODULES, 128), f32)], narrow, far, near)
     sums = over_plane(squares)
     later, sums = lax.optimization_barrier((table, sums))
@@ -379,9 +380,9 @@
         return lambda *refs: kernel(value, *refs)
 
     chosen = [((2, *half), bf16)]
-    (give,) = call(bound(select_kernel, SIBLING_UPPER), chosen, later, *starts, *averages)
+    (give,) = call(bound(select_kernel, SIBLING_UPPER), chosen, later, *spread)
     got = swap(give)
-    (mine,) = call(bound(select_kernel, OWN_UPPER), chosen, later, *starts, *averages)
+    (mine,) = call(bound(select_kernel, OWN_UPPER), chosen, later, *spread)
     path_params, momentum_next, params_next = last(
         entries, table, sums, other_sums, mine, got, average, params, momentum
     )

time: 78.3 us -> 76.1 us (0.972)
  starting transfers between devices: 33.8 us -> 26.8 us
  waiting for transfers between devices: 19.5 us -> 24.9 us
    ppermute x14 -> x12, starting transfers between devices: 27.6 us -> 20.6 us  [moved(): return lax.ppermute(x, PATH, [(p, target(p)) for p in range(PATHS)])]
    ppermute x14 -> x12, waiting for transfers between devices: 18 us -> 23.3 us  [moved(): return lax.ppermute(x, PATH, [(p, target(p)) for p in range(PATHS)])]
    pallas_call x10 -> x9, Pallas kernels: 2.92 us -> 2.43 us  [call(): pl.pallas_call(kernel, out_shape=shapes, in_specs=[VMEM] * len(args), out...]
  transfers between devices with their start and end apart: 17 -> 15, of which waited for: 9 -> 11; matrix products, arithmetic and copies ran while one was open for 0% -> 0% of each run, Pallas kernels for 6% -> 4%
where the time goes in v4:
time: 76.1 us; the launch traced here: 76 us
  starting transfers between devices  26.8 us (35%)
  waiting for transfers between devices  24.9 us (33%)
  blocking collectives  13.1 us (17%)
  Pallas kernels  9.42 us (12%)
  local copies, waits for them, and re-layouts  1.07 us (1%)
    ppermute x12, waiting for transfers between devices, moved(): return lax.ppermute(x, PATH, [(p, target(p)) for p in range(PATHS)])  23.3 us
    ppermute x12, starting transfers between devices, moved(): return lax.ppermute(x, PATH, [(p, target(p)) for p in range(PATHS)])  20.6 us
    all_to_all x1, blocking collectives, over_plane(): return jnp.sum(lax.all_to_all(parts, FSDP, 0, 0), axis=0)  13.1 us
    ppermute x3, starting transfers between devices, swap(): return lax.ppermute(x, 'core', [(0, 1), (1, 0)])  6.21 us
    pallas_call x1, Pallas kernels, given_half(): pl.pallas_call(give_kernel, out_shape=[half, table], in_specs=[HBM] * 5,...  2.94 us
    pallas_call x9, Pallas kernels, call(): pl.pallas_call(kernel, out_shape=shapes, in_specs=[VMEM] * len(args), out...  2.43 us
    pallas_call x1, Pallas kernels, last(): pl.pallas_call(lambda *refs: last_kernel(entries, *refs), grid=(LEVELS,),...  2.03 us
    pallas_call x1, Pallas kernels, levelwise(): pl.pallas_call(kernel, grid=(LEVELS,), out_shape=shapes, in_specs=[VMEM]...  2.02 us
  transfers between devices with their start and end apart: 15, of which 11 were waited for; matrix products, arithmetic and copies ran while one was open for 0% of the time, Pallas kernels for 4%

profile of v4, /device:TPU:1, one launch (start us, length us, event | category | flops | bytes accessed | tf_op | source)
XLA Modules:
  0.0 76.0 jit_solution(16279497902562243168)
XLA Ops:
  0.7 2.9 %shard_map.102 = (bf16[4,8,32,256]{3,2,1,0:T(8,128)(2,1)}, f32[24,8,256]{2,1,0:T(8,128)}) custom-call(s32[4,16]{1,0:T(4,128)} %bitcast.26, s32[4,16]{1,0:T(4,128)} %bitcast.27, s32[2,4]{1,0:T(2,128)} %bitcast.28, bf16[4,32,4096]{2,1,0:T(8,128)(2,1)} %bitcast.18, f32[4,32,4096]{2,1,0:T(8,128)} %bitcast.15), custom_call_target="tpu_custom_call" | custom-call | bytes 4194304 | tf_op jit(solution)/shard_map/pallas_call | solution.py:288
  3.6 3.3 %collective-permute-start = (bf16[4,8,32,256]{3,2,1,0:T(8,128)(2,1)}, bf16[4,8,32,256]{3,2,1,0:T(8,128)(2,1)S(1)}, u32[]{:S(2)}, u32[]{:S(2)}) collective-permute-start(bf16[4,8,32,256]{3,2,1,0:T(8,128)(2,1)} %get-tuple-element.22), channel_id=1, source_target_pairs={{0,16},{16,0},{1,17},{17,1},{2,18},{18,2},{3,19},{19,3},{4,20},{20... | collective-permute-start | bytes 1572872 | tf_op jit(solution)/shard_map/ppermute | solution.py:320
  6.9 0.9 %copy-done.1 = f32[24,8,256]{2,1,0:T(8,128)S(1)} copy-done((f32[24,8,256]{2,1,0:T(8,128)S(1)}, f32[24,8,256]{2,1,0:T(8,128)}, u32[]{:S(2)}) %copy-start.1) | copy-done | bytes 196632
  8.0 0.6 collective-permute-done.got
  9.0 3.9 %collective-permute-start.1 = (bf16[3,8,32,256]{3,2,1,0:T(8,128)(2,1)S(1)}, bf16[3,8,32,256]{3,2,1,0:T(8,128)(2,1)S(1)}, u32[]{:S(2)}, u32[]{:S(2)}) collective-permute-start(bf16[3,8,32,256]{3,2,1,0:T(8,128)(2,1)S(1)} %get-tuple-element.28), channel_id=1, source_target_pairs={{0,32},{16,240},{32,64},{48,16},{64,96},{80,48},{96,128},{112,80},... | collective-permute-start | bytes 1179656 | tf_op jit(solution)/shard_map/ppermute | solution.py:312
  13.0 2.0 %shard_map.107 = f32[4,32,4096]{2,1,0:T(8,128)} custom-call(f32[24,8,256]{2,1,0:T(8,128)S(1)} %copy-done.2, bf16[4,32,4096]{2,1,0:T(8,128)(2,1)S(1)} %bitcast.20, f32[4,32,4096]{2,1,0:T(8,128)S(1)} %bitcast.17), custom_call_target="tpu_custom_call" | custom-call | bytes 5242880 | tf_op jit(solution)/shard_map/pallas_call | solution.py:245
  15.1 6.2 %collective-permute-done.2.minus = bf16[2,8,32,256]{3,2,1,0:T(8,128)(2,1)S(1)} collective-permute-done((bf16[2,8,32,256]{3,2,1,0:T(8,128)(2,1)S(1)}, bf16[2,8,32,256]{3,2,1,0:T(8,128)(2,1)S(1)}, u32[]{:S(2)}, u32[]{:S(2)}) %collective-permute-start.2) | collective-permute-done | bytes 262176 | tf_op jit(solution)/shard_map/ppermute | solution.py:312
  21.5 1.4 %collective-permute-start.3 = (bf16[8,32,256]{2,1,0:T(8,128)(2,1)S(1)}, bf16[8,32,256]{2,1,0:T(8,128)(2,1)S(1)}, u32[]{:S(2)}, u32[]{:S(2)}) collective-permute-start(bf16[8,32,256]{2,1,0:T(8,128)(2,1)S(1)} %get-tuple-element.39), channel_id=1, source_target_pairs={{0,64},{16,208},{32,96},{48,240},{64,128},{80,16},{96,160},{112,48... | collective-permute-start | bytes 393224 | tf_op jit(solution)/shard_map/ppermute | solution.py:312
  22.9 1.5 %collective-permute-start.11 = (bf16[8,32,256]{2,1,0:T(8,128)(2,1)S(1)}, bf16[8,32,256]{2,1,0:T(8,128)(2,1)S(1)}, u32[]{:S(2)}, u32[]{:S(2)}) collective-permute-start(bf16[8,32,256]{2,1,0:T(8,128)(2,1)S(1)} %shard_map.105.refs_3_.refs_4_), channel_id=1, source_target_pairs={{0,192},{16,80},{32,224},{48,112},{64,0},{80,144},{96,32},{112,176... | collective-permute-start | bytes 393224 | tf_op jit(solution)/shard_map/ppermute | solution.py:312
  24.4 3.9 %collective-permute-start.10 = (bf16[8,32,256]{2,1,0:T(8,128)(2,1)S(1)}, bf16[8,32,256]{2,1,0:T(8,128)(2,1)S(1)}, u32[]{:S(2)}, u32[]{:S(2)}) collective-permute-start(bf16[8,32,256]{2,1,0:T(8,128)(2,1)S(1)} %shard_map.105.refs_3_.refs_4_), channel_id=1, source_target_pairs={{0,96},{16,176},{32,128},{48,208},{64,160},{80,240},{96,192},{112,... | collective-permute-start | bytes 393224 | tf_op jit(solution)/shard_map/ppermute | solution.py:312
  28.3 3.4 %collective-permute-done.4.far = bf16[8,32,256]{2,1,0:T(8,128)(2,1)S(1)} collective-permute-done((bf16[8,32,256]{2,1,0:T(8,128)(2,1)S(1)}, bf16[8,32,256]{2,1,0:T(8,128)(2,1)S(1)}, u32[]{:S(2)}, u32[]{:S(2)}) %collective-permute-start.4) | collective-permute-done | bytes 131104 | tf_op jit(solution)/shard_map/ppermute | solution.py:312
  31.8 5.0 %collective-permute-start.6 = (bf16[8,32,256]{2,1,0:T(8,128)(2,1)S(1)}, bf16[8,32,256]{2,1,0:T(8,128)(2,1)S(1)}, u32[]{:S(2)}, u32[]{:S(2)}) collective-permute-start(bf16[8,32,256]{2,1,0:T(8,128)(2,1)S(1)} %get-tuple-element.29.own.refs_0_.refs_1_), channel_id=1, source_target_pairs={{0,192},{16,80},{32,224},{48,112},{64,0},{80,144},{96,32},{112,176... | collective-permute-start | bytes 393224 | tf_op jit(solution)/shard_map/ppermute | solution.py:312
  36.9 5.1 %collective-permute-done.10.refs_4_.refs_5_ = bf16[8,32,256]{2,1,0:T(8,128)(2,1)S(1)} collective-permute-done((bf16[8,32,256]{2,1,0:T(8,128)(2,1)S(1)}, bf16[8,32,256]{2,1,0:T(8,128)(2,1)S(1)}, u32[]{:S(2)}, u32[]{:S(2)}) %collective-permute-start.10) | collective-permute-done | bytes 131104 | tf_op jit(solution)/shard_map/ppermute | solution.py:312
  42.1 2.1 %collective-permute-done.6.near.refs_2_.refs_3_ = bf16[8,32,256]{2,1,0:T(8,128)(2,1)S(1)} collective-permute-done((bf16[8,32,256]{2,1,0:T(8,128)(2,1)S(1)}, bf16[8,32,256]{2,1,0:T(8,128)(2,1)S(1)}, u32[]{:S(2)}, u32[]{:S(2)}) %collective-permute-start.6) | collective-permute-done | bytes 131104 | tf_op jit(solution)/shard_map/ppermute | solution.py:312
  44.1 2.0 %collective-permute-done.5.far.refs_1_.refs_2_ = bf16[8,32,256]{2,1,0:T(8,128)(2,1)S(1)} collective-permute-done((bf16[8,32,256]{2,1,0:T(8,128)(2,1)S(1)}, bf16[8,32,256]{2,1,0:T(8,128)(2,1)S(1)}, u32[]{:S(2)}, u32[]{:S(2)}) %collective-permute-start.5) | collective-permute-done | bytes 131104 | tf_op jit(solution)/shard_map/ppermute | solution.py:312
  46.1 1.1 %shard_map.110 = (bf16[32,32,256]{2,1,0:T(8,128)(2,1)}, bf16[48,32,256]{2,1,0:T(8,128)(2,1)}) custom-call(bf16[8,32,256]{2,1,0:T(8,128)(2,1)S(1)} %get-tuple-element.29.own.refs_0_.refs_1_, bf16[8,32,256]{2,1,0:T(8,128)(2,1)S(1)} %collective-permute-done.5.far.refs_1_.refs_2_, bf16[8,32,256]{2,1,0:T(8,128)(2,1)S(1)} %collective-permute-done.6.near.refs_2_.refs_3_, ...), custom_call_target="tpu_custom_call" | custom-call | bytes 2097152 | tf_op jit(solution)/shard_map/pallas_call | solution.py:229
  47.3 2.7 %collective-permute-start.12 = (bf16[32,32,256]{2,1,0:T(8,128)(2,1)}, bf16[32,32,256]{2,1,0:T(8,128)(2,1)S(1)}, u32[]{:S(2)}, u32[]{:S(2)}) collective-permute-start(bf16[32,32,256]{2,1,0:T(8,128)(2,1)} %get-tuple-element.32), channel_id=1, source_target_pairs={{0,32},{16,240},{32,64},{48,16},{64,96},{80,48},{96,128},{112,80},... | collective-permute-start | bytes 1572872 | tf_op jit(solution)/shard_map/ppermute | solution.py:312
  50.1 13.1 %all_to_all.5 = f32[16,8,128]{2,1,0:T(8,128)S(1)} all-to-all(f32[16,8,128]{2,1,0:T(8,128)S(1)} %broadcast_in_dim.17), channel_id=1, replica_groups=mesh['z'=8,'core'=2,'y'=4,'x'=4] {'y','x'}, dimensions={0} | all-to-all | bytes 131072 | tf_op jit(solution)/shard_map/all_to_all | solution.py:335
  64.3 2.9 %collective-permute-start.14 = (bf16[2,4,8,32,256]{4,3,2,1,0:T(8,128)(2,1)S(1)}, bf16[2,4,8,32,256]{4,3,2,1,0:T(8,128)(2,1)S(1)}, u32[]{:S(2)}, u32[]{:S(2)}) collective-permute-start(bf16[2,4,8,32,256]{4,3,2,1,0:T(8,128)(2,1)S(1)} %shard_map.112), channel_id=1, source_target_pairs={{0,16},{16,0},{1,17},{17,1},{2,18},{18,2},{3,19},{19,3},{4,20},{20... | collective-permute-start | bytes 3145736 | tf_op jit(solution)/shard_map/ppermute | solution.py:320
  67.2 1.9 %collective-permute-start.7 = (f32[8,128]{1,0:T(8,128)S(1)}, f32[8,128]{1,0:T(8,128)S(1)}, u32[]{:S(2)}, u32[]{:S(2)}) collective-permute-start(f32[8,128]{1,0:T(8,128)S(1)} %broadcast_select_fusion), channel_id=1, source_target_pairs={{0,32},{16,240},{32,64},{48,16},{64,96},{80,48},{96,128},{112,80},... | collective-permute-start | bytes 12296 | tf_op jit(solution)/shard_map/ppermute | solution.py:312
  69.1 0.8 collective-permute-done.7
  69.9 2.9 %collective-permute-done.8 = f32[8,128]{1,0:T(8,128)S(1)} collective-permute-done((f32[8,128]{1,0:T(8,128)S(1)}, f32[8,128]{1,0:T(8,128)S(1)}, u32[]{:S(2)}, u32[]{:S(2)}) %collective-permute-start.8) | collective-permute-done | bytes 4128 | tf_op jit(solution)/shard_map/ppermute | solution.py:312
  73.1 0.9 %collective-permute-done.9.refs_2_ = f32[8,128]{1,0:T(8,128)S(1)} collective-permute-done((f32[8,128]{1,0:T(8,128)S(1)}, f32[8,128]{1,0:T(8,128)S(1)}, u32[]{:S(2)}, u32[]{:S(2)}) %collective-permute-start.9) | collective-permute-done | bytes 4128 | tf_op jit(solution)/shard_map/ppermute | solution.py:320
  74.0 2.0 %shard_map.113 = (bf16[4,32,4096]{2,1,0:T(8,128)(2,1)}, f32[8,32,256]{2,1,0:T(8,128)}, f32[8,32,256]{2,1,0:T(8,128)}) custom-call(f32[24,8,256]{2,1,0:T(8,128)S(1)} %copy-done.2, f32[8,128]{1,0:T(8,128)S(1)} %add_add_fusion.refs_1_, f32[8,128]{1,0:T(8,128)S(1)} %collective-permute-done.9.refs_2_, bf16[2,4,8,32,256]{4,3,2,1,0:T(8,128)(2,1)S(1)} %shard_map.111.refs_3_, ...), custom_call_target="tpu_custom_call" | custom-call | bytes 4456448 | tf_op jit(solution)/shard_map/pallas_call | solution.py:266
  (37 shorter events, 2.5 us)
Async XLA Ops:
  0.6 6.3 %copy-start = (f32[1,4,32,4096]{3,2,1,0:T(8,128)S(1)}, f32[1,4,32,4096]{3,2,1,0:T(8,128)}, u32[]{:S(2)}) copy-start(f32[1,4,32,4096]{3,2,1,0:T(8,128)} %param.8) | copy-start | bytes 6291460
  0.6 6.3 %copy-start.3 = (bf16[1,4,32,4096]{3,2,1,0:T(8,128)(2,1)S(1)}, bf16[1,4,32,4096]{3,2,1,0:T(8,128)(2,1)}, u32[]{:S(2)}) copy-start(bf16[1,4,32,4096]{3,2,1,0:T(8,128)(2,1)} %param.7) | copy-start | bytes 3145732
  3.6 5.1 %collective-permute-start = (bf16[4,8,32,256]{3,2,1,0:T(8,128)(2,1)}, bf16[4,8,32,256]{3,2,1,0:T(8,128)(2,1)S(1)}, u32[]{:S(2)}, u32[]{:S(2)}) collective-permute-start(bf16[4,8,32,256]{3,2,1,0:T(8,128)(2,1)} %get-tuple-element.22), channel_id=1, source_target_pairs={{0,16},{16,0},{1,17},{17,1},{2,18},{18,2},{3,19},{19,3},{4,20},{20... | collective-permute-start | bytes 1572872 | tf_op jit(solution)/shard_map/ppermute | solution.py:320
  6.9 0.9 %copy-start.1 = (f32[24,8,256]{2,1,0:T(8,128)S(1)}, f32[24,8,256]{2,1,0:T(8,128)}, u32[]{:S(2)}) copy-start(f32[24,8,256]{2,1,0:T(8,128)} %get-tuple-element.31.table.refs_0_) | copy-start | bytes 589828
  7.9 0.9 %copy-start.2 = (f32[24,8,256]{2,1,0:T(8,128)S(1)}, f32[24,8,256]{2,1,0:T(8,128)}, u32[]{:S(2)}) copy-start(f32[24,8,256]{2,1,0:T(8,128)} %get-tuple-element.31.table.refs_0_) | copy-start | bytes 589828
  7.9 5.1 %copy-start.4 = (f32[4,2,32,256]{3,2,1,0:T(8,128)S(1)}, f32[4,2,32,256]{3,2,1,0:T(8,128)}, u32[]{:S(2)}) copy-start(f32[4,2,32,256]{3,2,1,0:T(8,128)} %param.9) | copy-start | bytes 786436
  7.9 5.1 %copy-start.5 = (f32[4,2,32,256]{3,2,1,0:T(8,128)S(1)}, f32[4,2,32,256]{3,2,1,0:T(8,128)}, u32[]{:S(2)}) copy-start(f32[4,2,32,256]{3,2,1,0:T(8,128)} %param.10) | copy-start | bytes 786436
  9.0 12.3 %collective-permute-start.1 = (bf16[3,8,32,256]{3,2,1,0:T(8,128)(2,1)S(1)}, bf16[3,8,32,256]{3,2,1,0:T(8,128)(2,1)S(1)}, u32[]{:S(2)}, u32[]{:S(2)}) collective-permute-start(bf16[3,8,32,256]{3,2,1,0:T(8,128)(2,1)S(1)} %get-tuple-element.28), channel_id=1, source_target_pairs={{0,32},{16,240},{32,64},{48,16},{64,96},{80,48},{96,128},{112,80},... | collective-permute-start | bytes 1179656 | tf_op jit(solution)/shard_map/ppermute | solution.py:312
  12.9 8.4 %collective-permute-start.2 = (bf16[2,8,32,256]{3,2,1,0:T(8,128)(2,1)S(1)}, bf16[2,8,32,256]{3,2,1,0:T(8,128)(2,1)S(1)}, u32[]{:S(2)}, u32[]{:S(2)}) collective-permute-start(bf16[2,8,32,256]{3,2,1,0:T(8,128)(2,1)S(1)} %get-tuple-element.23), channel_id=1, source_target_pairs={{0,224},{16,48},{32,0},{48,80},{64,32},{80,112},{96,64},{112,144},... | collective-permute-start | bytes 786440 | tf_op jit(solution)/shard_map/ppermute | solution.py:312
  21.4 10.3 %collective-permute-start.4 = (bf16[8,32,256]{2,1,0:T(8,128)(2,1)S(1)}, bf16[8,32,256]{2,1,0:T(8,128)(2,1)S(1)}, u32[]{:S(2)}, u32[]{:S(2)}) collective-permute-start(bf16[8,32,256]{2,1,0:T(8,128)(2,1)S(1)} %get-tuple-element.38), channel_id=1, source_target_pairs={{0,160},{16,112},{32,192},{48,144},{64,224},{80,176},{96,0},{112,2... | collective-permute-start | bytes 393224 | tf_op jit(solution)/shard_map/ppermute | solution.py:312
  21.5 10.3 %collective-permute-start.3 = (bf16[8,32,256]{2,1,0:T(8,128)(2,1)S(1)}, bf16[8,32,256]{2,1,0:T(8,128)(2,1)S(1)}, u32[]{:S(2)}, u32[]{:S(2)}) collective-permute-start(bf16[8,32,256]{2,1,0:T(8,128)(2,1)S(1)} %get-tuple-element.39), channel_id=1, source_target_pairs={{0,64},{16,208},{32,96},{48,240},{64,128},{80,16},{96,160},{112,48... | collective-permute-start | bytes 393224 | tf_op jit(solution)/shard_map/ppermute | solution.py:312
  22.9 14.1 %collective-permute-start.11 = (bf16[8,32,256]{2,1,0:T(8,128)(2,1)S(1)}, bf16[8,32,256]{2,1,0:T(8,128)(2,1)S(1)}, u32[]{:S(2)}, u32[]{:S(2)}) collective-permute-start(bf16[8,32,256]{2,1,0:T(8,128)(2,1)S(1)} %shard_map.105.refs_3_.refs_4_), channel_id=1, source_target_pairs={{0,192},{16,80},{32,224},{48,112},{64,0},{80,144},{96,32},{112,176... | collective-permute-start | bytes 393224 | tf_op jit(solution)/shard_map/ppermute | solution.py:312
  24.4 17.6 %collective-permute-start.10 = (bf16[8,32,256]{2,1,0:T(8,128)(2,1)S(1)}, bf16[8,32,256]{2,1,0:T(8,128)(2,1)S(1)}, u32[]{:S(2)}, u32[]{:S(2)}) collective-permute-start(bf16[8,32,256]{2,1,0:T(8,128)(2,1)S(1)} %shard_map.105.refs_3_.refs_4_), channel_id=1, source_target_pairs={{0,96},{16,176},{32,128},{48,208},{64,160},{80,240},{96,192},{112,... | collective-permute-start | bytes 393224 | tf_op jit(solution)/shard_map/ppermute | solution.py:312
  31.8 12.3 %collective-permute-start.6 = (bf16[8,32,256]{2,1,0:T(8,128)(2,1)S(1)}, bf16[8,32,256]{2,1,0:T(8,128)(2,1)S(1)}, u32[]{:S(2)}, u32[]{:S(2)}) collective-permute-start(bf16[8,32,256]{2,1,0:T(8,128)(2,1)S(1)} %get-tuple-element.29.own.refs_0_.refs_1_), channel_id=1, source_target_pairs={{0,192},{16,80},{32,224},{48,112},{64,0},{80,144},{96,32},{112,176... | collective-permute-start | bytes 393224 | tf_op jit(solution)/shard_map/ppermute | solution.py:312
  36.8 9.3 %collective-permute-start.5 = (bf16[8,32,256]{2,1,0:T(8,128)(2,1)S(1)}, bf16[8,32,256]{2,1,0:T(8,128)(2,1)S(1)}, u32[]{:S(2)}, u32[]{:S(2)}) collective-permute-start(bf16[8,32,256]{2,1,0:T(8,128)(2,1)S(1)} %get-tuple-element.29.own.refs_0_.refs_1_), channel_id=1, source_target_pairs={{0,96},{16,176},{32,128},{48,208},{64,160},{80,240},{96,192},{112,... | collective-permute-start | bytes 393224 | tf_op jit(solution)/shard_map/ppermute | solution.py:312
  47.3 16.7 %collective-permute-start.13 = (bf16[48,32,256]{2,1,0:T(8,128)(2,1)}, bf16[48,32,256]{2,1,0:T(8,128)(2,1)S(1)}, u32[]{:S(2)}, u32[]{:S(2)}) collective-permute-start(bf16[48,32,256]{2,1,0:T(8,128)(2,1)} %get-tuple-element.33), channel_id=1, source_target_pairs={{0,224},{16,48},{32,0},{48,80},{64,32},{80,112},{96,64},{112,144},... | collective-permute-start | bytes 2359304 | tf_op jit(solution)/shard_map/ppermute | solution.py:312
  47.3 16.4 %collective-permute-start.12 = (bf16[32,32,256]{2,1,0:T(8,128)(2,1)}, bf16[32,32,256]{2,1,0:T(8,128)(2,1)S(1)}, u32[]{:S(2)}, u32[]{:S(2)}) collective-permute-start(bf16[32,32,256]{2,1,0:T(8,128)(2,1)} %get-tuple-element.32), channel_id=1, source_target_pairs={{0,32},{16,240},{32,64},{48,16},{64,96},{80,48},{96,128},{112,80},... | collective-permute-start | bytes 1572872 | tf_op jit(solution)/shard_map/ppermute | solution.py:312
  64.3 9.7 %collective-permute-start.14 = (bf16[2,4,8,32,256]{4,3,2,1,0:T(8,128)(2,1)S(1)}, bf16[2,4,8,32,256]{4,3,2,1,0:T(8,128)(2,1)S(1)}, u32[]{:S(2)}, u32[]{:S(2)}) collective-permute-start(bf16[2,4,8,32,256]{4,3,2,1,0:T(8,128)(2,1)S(1)} %shard_map.112), channel_id=1, source_target_pairs={{0,16},{16,0},{1,17},{17,1},{2,18},{18,2},{3,19},{19,3},{4,20},{20... | collective-permute-start | bytes 3145736 | tf_op jit(solution)/shard_map/ppermute | solution.py:320
  67.2 2.7 %collective-permute-start.7 = (f32[8,128]{1,0:T(8,128)S(1)}, f32[8,128]{1,0:T(8,128)S(1)}, u32[]{:S(2)}, u32[]{:S(2)}) collective-permute-start(f32[8,128]{1,0:T(8,128)S(1)} %broadcast_select_fusion), channel_id=1, source_target_pairs={{0,32},{16,240},{32,64},{48,16},{64,96},{80,48},{96,128},{112,80},... | collective-permute-start | bytes 12296 | tf_op jit(solution)/shard_map/ppermute | solution.py:312
  69.1 3.7 %collective-permute-start.8 = (f32[8,128]{1,0:T(8,128)S(1)}, f32[8,128]{1,0:T(8,128)S(1)}, u32[]{:S(2)}, u32[]{:S(2)}) collective-permute-start(f32[8,128]{1,0:T(8,128)S(1)} %reduce_sum.9), channel_id=1, source_target_pairs={{0,224},{16,48},{32,0},{48,80},{64,32},{80,112},{96,64},{112,144},... | collective-permute-start | bytes 12296 | tf_op jit(solution)/shard_map/ppermute | solution.py:312
  72.8 1.2 %collective-permute-start.9 = (f32[8,128]{1,0:T(8,128)S(1)}, f32[8,128]{1,0:T(8,128)S(1)}, u32[]{:S(2)}, u32[]{:S(2)}) collective-permute-start(f32[8,128]{1,0:T(8,128)S(1)} %add_add_fusion.refs_1_), channel_id=1, source_target_pairs={{0,16},{16,0},{1,17},{17,1},{2,18},{18,2},{3,19},{19,3},{4,20},{20... | collective-permute-start | bytes 12296 | tf_op jit(solution)/shard_map/ppermute | solution.py:320

commit v5 on v4

--- a/solution.py
+++ b/solution.py
@@ -8,11 +8,13 @@
 
 PATH = ("z", "core")
 FSDP = ("y", "x")
+PLANE = ("core", "y", "x")
 CHIPS = 8
 PATHS = 16
 LEVELS = 4
 MODULES = 8
 BLOCK = 256
+STEPS = 4
 
 CLIP_RMS = 0.2
 OUTER_RATE = 0.7
@@ -149,7 +151,7 @@
 
 
 def squares_kernel(own, far, near, out):
-    lane = lax.broadcasted_iota(jnp.int32, (1, out.shape[1]), 1)
+    lane = lax.broadcasted_iota(jnp.int32, (1, out.shape[1]), 1) - 3 * lax.axis_index("core")
     for q in range(MODULES):
         row = jnp.zeros(lane.shape, jnp.float32)
         for i, block in enumerate((own, far, near)):
@@ -193,27 +195,30 @@
                 out[which, l, chip] = value.astype(jnp.bfloat16)
 
 
-def last_kernel(entries, table, sums, other_sums, mine, got, average, params, momentum, path_out, momentum_out, params_out):
-    l = pl.program_id(0)
+def last_kernel(entries, table, sums, side, other_side, mine, got, average, params, momentum, *outs):
+    path_out, momentum_out, params_out = outs
     core = lax.axis_index("core")
-    total = jnp.sum(sums[...] + other_sums[...], axis=1, keepdims=True)
+    total = jnp.sum(sums[...] + side[...] + other_side[...], axis=1, keepdims=True)
     factor = jnp.minimum(1.0, CLIP_RMS / jnp.sqrt(total / entries + EPSILON_SQ))
     row = lax.broadcasted_iota(jnp.int32, factor.shape, 0)
-    low, high = (jnp.sum(jnp.where(row == 2 * l + m, factor, 0.0), axis=0, keepdims=True) for m in range(2))
-    for m, scale in enumerate((low, high)):
-        skipped = table[SKIPPED + 2 * l + m][:1] > 0
-        clipped = scale * average[m]
-        before, old = momentum[m], params[m]
-        after = jnp.where(skipped, before, MOMENTUM_COEF * before + clipped)
-        momentum_out[m] = after
-        params_out[m] = jnp.where(skipped, old, old - OUTER_RATE * (clipped + MOMENTUM_COEF * after))
-    upper = table[OWN_UPPER + l][:1] > 0
-    scale = CLIPPED_COEF * jnp.where(upper, high, low)
-    for half, part in ((core, mine), (1 - core, got)):
-        for block in range(CHIPS):
-            at = pl.ds(pl.multiple_of((2 * block + half) * BLOCK, BLOCK), BLOCK)
-            new = part[1, l, block].astype(jnp.float32) - scale * part[0, l, block].astype(jnp.float32)
-            path_out[0, :, at] = new.astype(jnp.bfloat16)
+    for k in range(LEVELS // STEPS):
+        l = pl.program_id(0) * (LEVELS // STEPS) + k
+        low, high = (jnp.sum(jnp.where(row == 2 * l + m, factor, 0.0), axis=0, keepdims=True) for m in range(2))
+        for m, scale in enumerate((low, high)):
+            at = 2 * k + m
+            skipped = table[SKIPPED + 2 * l + m][:1] > 0
+            clipped = scale * average[at]
+            before, old = momentum[at], params[at]
+            after = jnp.where(skipped, before, MOMENTUM_COEF * before + clipped)
+            momentum_out[at] = after
+            params_out[at] = jnp.where(skipped, old, old - OUTER_RATE * (clipped + MOMENTUM_COEF * after))
+        upper = table[OWN_UPPER + l][:1] > 0
+        scale = CLIPPED_COEF * jnp.where(upper, high, low)
+        for half, part in ((core, mine), (1 - core, got)):
+            for block in range(CHIPS):
+                at = pl.ds(pl.multiple_of((2 * block + half) * BLOCK, BLOCK), BLOCK)
+                new = part[1, l, block].astype(jnp.float32) - scale * part[0, l, block].astype(jnp.float32)
+                path_out[k, :, at] = new.astype(jnp.bfloat16)
 
 
 def cost(bytes_accessed):
@@ -253,7 +258,7 @@
     )(*fixed, *args)
 
 
-def last(entries, table, sums, other_sums, mine, got, average, params, momentum):
+def last(entries, table, sums, side, other_side, mine, got, average, params, momentum):
     _, _, _, rows, _ = mine.shape
     outs = [
         jax.ShapeDtypeStruct((LEVELS, rows, 2 * CHIPS * BLOCK), jnp.bfloat16),
@@ -261,24 +266,20 @@
     ]
 
     def one(shape):
-        return pl.BlockSpec((shape[0] // LEVELS, *shape[1:]), lambda l: (l, *[0] * (len(shape) - 1)))
+        return pl.BlockSpec((shape[0] // STEPS, *shape[1:]), lambda l: (l, *[0] * (len(shape) - 1)))
 
     return pl.pallas_call(
         lambda *refs: last_kernel(entries, *refs),
-        grid=(LEVELS,),
+        grid=(STEPS,),
         out_shape=outs,
         in_specs=[
-            VMEM,
-            VMEM,
-            VMEM,
-            VMEM,
-            VMEM,
+            *[VMEM] * 6,
             *[one(average.shape)] * 3,
         ],
         out_specs=[one(o.shape) for o in outs],
         cost_estimate=cost(size_of((mine, got, average, params, momentum)) + size_of(outs)),
         compiler_params=pltpu.CompilerParams(vmem_limit_bytes=24 * 2**20),
-    )(table, sums, other_sums, mine, got, average, params, momentum)
+    )(table, sums, side, other_side, mine, got, average, params, momentum)
 
 
 def given_half(routes, counts, flags, delta, feedback):
@@ -331,8 +332,8 @@
 
 
 def over_plane(x):
-    parts = jnp.broadcast_to(x[None], (lax.axis_size(FSDP), *x.shape))
-    return jnp.sum(lax.all_to_all(parts, FSDP, 0, 0), axis=0)
+    parts = jnp.broadcast_to(x[None], (lax.axis_size(PLANE), *x.shape))
+    return jnp.sum(lax.all_to_all(parts, PLANE, 0, 0), axis=0)
 
 
 def on_device(path_delta, feedback, global_params, momentum, routes, token_counts, skip_flags):
@@ -373,8 +374,8 @@
     sums = over_plane(squares)
     later, sums = lax.optimization_barrier((table, sums))
     lane = lax.broadcasted_iota(jnp.int32, sums.shape, 1)
-    sums = sums + jump(jnp.where(lane < 2, sums, 0.0), 1) + jump(sums, -1)
-    other_sums = swap(sums)
+    side = jump(jnp.where(lane == 3 * lax.axis_index("core") + 2, 0.0, sums), 1)
+    other_side = swap(side)
 
     def bound(kernel, value):
         return lambda *refs: kernel(value, *refs)
@@ -384,7 +385,7 @@
     got = swap(give)
     (mine,) = call(bound(select_kernel, OWN_UPPER), chosen, later, *spread)
     path_params, momentum_next, params_next = last(
-        entries, table, sums, other_sums, mine, got, average, params, momentum
+        entries, table, sums, side, other_side, mine, got, average, params, momentum
     )
     shape = global_params.shape
     return feedback_next[None], momentum_next.reshape(shape), params_next.reshape(shape), path_params[None]

time: 76.1 us -> 76 us (level)
  waiting for transfers between devices: 24.9 us -> 20.8 us
  blocking collectives: 13.1 us -> 15.5 us
  Pallas kernels: 9.42 us -> 10.4 us
    ppermute x12 -> x11, waiting for transfers between devices: 23.3 us -> 19.6 us  [moved(): return lax.ppermute(x, PATH, [(p, target(p)) for p in range(PATHS)])]
    all_to_all x1, blocking collectives: 13.1 us -> 15.5 us  [over_plane(): return jnp.sum(lax.all_to_all(parts, PLANE, 0, 0), axis=0)]
    pallas_call x1, Pallas kernels: 2.03 us -> 3.29 us  [last(): pl.pallas_call(lambda *refs: last_kernel(entries, *refs), grid=(STEPS,),...]
    ppermute x12 -> x11, starting transfers between devices: 20.6 us -> 21.2 us  [moved(): return lax.ppermute(x, PATH, [(p, target(p)) for p in range(PATHS)])]
  transfers between devices with their start and end apart: 15 -> 14, of which waited for: 11 -> 8; matrix products, arithmetic and copies ran while one was open for 0% -> 0% of each run, Pallas kernels for 4% -> 4%
where the time goes in v5:
time: 76 us; the launch traced here: 75.8 us
  starting transfers between devices  27.2 us (36%)
  waiting for transfers between devices  20.8 us (27%)
  blocking collectives  15.5 us (20%)
  Pallas kernels  10.4 us (14%)
  local copies, waits for them, and re-layouts  1.09 us (1%)
  between operations  0.76 us (1%)
    ppermute x11, starting transfers between devices, moved(): return lax.ppermute(x, PATH, [(p, target(p)) for p in range(PATHS)])  21.2 us
    ppermute x11, waiting for transfers between devices, moved(): return lax.ppermute(x, PATH, [(p, target(p)) for p in range(PATHS)])  19.6 us
    all_to_all x1, blocking collectives, over_plane(): return jnp.sum(lax.all_to_all(parts, PLANE, 0, 0), axis=0)  15.5 us
    ppermute x3, starting transfers between devices, swap(): return lax.ppermute(x, 'core', [(0, 1), (1, 0)])  5.96 us
    pallas_call x1, Pallas kernels, last(): pl.pallas_call(lambda *refs: last_kernel(entries, *refs), grid=(STEPS,),...  3.29 us
    pallas_call x1, Pallas kernels, given_half(): pl.pallas_call(give_kernel, out_shape=[half, table], in_specs=[HBM] * 5,...  2.94 us
    pallas_call x9, Pallas kernels, call(): pl.pallas_call(kernel, out_shape=shapes, in_specs=[VMEM] * len(args), out...  2.18 us
    pallas_call x1, Pallas kernels, levelwise(): pl.pallas_call(kernel, grid=(LEVELS,), out_shape=shapes, in_specs=[VMEM]...  2.02 us
  transfers between devices with their start and end apart: 14, of which 8 were waited for; matrix products, arithmetic and copies ran while one was open for 0% of the time, Pallas kernels for 4%

profile of v5, /device:TPU:1, one launch (start us, length us, event | category | flops | bytes accessed | tf_op | source)
XLA Modules:
  0.0 75.8 jit_solution(13358397508378125454)
XLA Ops:
  0.7 2.9 %shard_map.102 = (bf16[4,8,32,256]{3,2,1,0:T(8,128)(2,1)}, f32[24,8,256]{2,1,0:T(8,128)}) custom-call(s32[4,16]{1,0:T(4,128)} %bitcast.26, s32[4,16]{1,0:T(4,128)} %bitcast.27, s32[2,4]{1,0:T(2,128)} %bitcast.28, bf16[4,32,4096]{2,1,0:T(8,128)(2,1)} %bitcast.18, f32[4,32,4096]{2,1,0:T(8,128)} %bitcast.15), custom_call_target="tpu_custom_call" | custom-call | bytes 4194304 | tf_op jit(solution)/shard_map/pallas_call | solution.py:289
  3.6 3.3 %collective-permute-start = (bf16[4,8,32,256]{3,2,1,0:T(8,128)(2,1)}, bf16[4,8,32,256]{3,2,1,0:T(8,128)(2,1)S(1)}, u32[]{:S(2)}, u32[]{:S(2)}) collective-permute-start(bf16[4,8,32,256]{3,2,1,0:T(8,128)(2,1)} %get-tuple-element.22), channel_id=1, source_target_pairs={{0,16},{16,0},{1,17},{17,1},{2,18},{18,2},{3,19},{19,3},{4,20},{20... | collective-permute-start | bytes 1572872 | tf_op jit(solution)/shard_map/ppermute | solution.py:321
  6.9 0.9 %copy-done.1 = f32[24,8,256]{2,1,0:T(8,128)S(1)} copy-done((f32[24,8,256]{2,1,0:T(8,128)S(1)}, f32[24,8,256]{2,1,0:T(8,128)}, u32[]{:S(2)}) %copy-start.1) | copy-done | bytes 196632
  8.0 0.6 collective-permute-done.got
  9.0 3.9 %collective-permute-start.1 = (bf16[3,8,32,256]{3,2,1,0:T(8,128)(2,1)S(1)}, bf16[3,8,32,256]{3,2,1,0:T(8,128)(2,1)S(1)}, u32[]{:S(2)}, u32[]{:S(2)}) collective-permute-start(bf16[3,8,32,256]{3,2,1,0:T(8,128)(2,1)S(1)} %get-tuple-element.28), channel_id=1, source_target_pairs={{0,32},{16,240},{32,64},{48,16},{64,96},{80,48},{96,128},{112,80},... | collective-permute-start | bytes 1179656 | tf_op jit(solution)/shard_map/ppermute | solution.py:313
  13.0 2.0 %shard_map.107 = f32[4,32,4096]{2,1,0:T(8,128)} custom-call(f32[24,8,256]{2,1,0:T(8,128)S(1)} %copy-done.2, bf16[4,32,4096]{2,1,0:T(8,128)(2,1)S(1)} %bitcast.20, f32[4,32,4096]{2,1,0:T(8,128)S(1)} %bitcast.17), custom_call_target="tpu_custom_call" | custom-call | bytes 5242880 | tf_op jit(solution)/shard_map/pallas_call | solution.py:250
  15.1 6.2 %collective-permute-done.2.minus = bf16[2,8,32,256]{3,2,1,0:T(8,128)(2,1)S(1)} collective-permute-done((bf16[2,8,32,256]{3,2,1,0:T(8,128)(2,1)S(1)}, bf16[2,8,32,256]{3,2,1,0:T(8,128)(2,1)S(1)}, u32[]{:S(2)}, u32[]{:S(2)}) %collective-permute-start.2) | collective-permute-done | bytes 262176 | tf_op jit(solution)/shard_map/ppermute | solution.py:313
  21.5 1.4 %collective-permute-start.3 = (bf16[8,32,256]{2,1,0:T(8,128)(2,1)S(1)}, bf16[8,32,256]{2,1,0:T(8,128)(2,1)S(1)}, u32[]{:S(2)}, u32[]{:S(2)}) collective-permute-start(bf16[8,32,256]{2,1,0:T(8,128)(2,1)S(1)} %get-tuple-element.39), channel_id=1, source_target_pairs={{0,64},{16,208},{32,96},{48,240},{64,128},{80,16},{96,160},{112,48... | collective-permute-start | bytes 393224 | tf_op jit(solution)/shard_map/ppermute | solution.py:313
  22.9 1.5 %collective-permute-start.10 = (bf16[8,32,256]{2,1,0:T(8,128)(2,1)S(1)}, bf16[8,32,256]{2,1,0:T(8,128)(2,1)S(1)}, u32[]{:S(2)}, u32[]{:S(2)}) collective-permute-start(bf16[8,32,256]{2,1,0:T(8,128)(2,1)S(1)} %shard_map.105.refs_3_.refs_4_), channel_id=1, source_target_pairs={{0,192},{16,80},{32,224},{48,112},{64,0},{80,144},{96,32},{112,176... | collective-permute-start | bytes 393224 | tf_op jit(solution)/shard_map/ppermute | solution.py:313
  24.4 3.9 %collective-permute-start.9 = (bf16[8,32,256]{2,1,0:T(8,128)(2,1)S(1)}, bf16[8,32,256]{2,1,0:T(8,128)(2,1)S(1)}, u32[]{:S(2)}, u32[]{:S(2)}) collective-permute-start(bf16[8,32,256]{2,1,0:T(8,128)(2,1)S(1)} %shard_map.105.refs_3_.refs_4_), channel_id=1, source_target_pairs={{0,96},{16,176},{32,128},{48,208},{64,160},{80,240},{96,192},{112,... | collective-permute-start | bytes 393224 | tf_op jit(solution)/shard_map/ppermute | solution.py:313
  28.3 3.4 %collective-permute-done.4.far = bf16[8,32,256]{2,1,0:T(8,128)(2,1)S(1)} collective-permute-done((bf16[8,32,256]{2,1,0:T(8,128)(2,1)S(1)}, bf16[8,32,256]{2,1,0:T(8,128)(2,1)S(1)}, u32[]{:S(2)}, u32[]{:S(2)}) %collective-permute-start.4) | collective-permute-done | bytes 131104 | tf_op jit(solution)/shard_map/ppermute | solution.py:313
  31.8 5.0 %collective-permute-start.6 = (bf16[8,32,256]{2,1,0:T(8,128)(2,1)S(1)}, bf16[8,32,256]{2,1,0:T(8,128)(2,1)S(1)}, u32[]{:S(2)}, u32[]{:S(2)}) collective-permute-start(bf16[8,32,256]{2,1,0:T(8,128)(2,1)S(1)} %get-tuple-element.29.own.refs_0_.refs_1_), channel_id=1, source_target_pairs={{0,192},{16,80},{32,224},{48,112},{64,0},{80,144},{96,32},{112,176... | collective-permute-start | bytes 393224 | tf_op jit(solution)/shard_map/ppermute | solution.py:313
  36.9 5.1 %collective-permute-done.9.refs_4_.refs_5_ = bf16[8,32,256]{2,1,0:T(8,128)(2,1)S(1)} collective-permute-done((bf16[8,32,256]{2,1,0:T(8,128)(2,1)S(1)}, bf16[8,32,256]{2,1,0:T(8,128)(2,1)S(1)}, u32[]{:S(2)}, u32[]{:S(2)}) %collective-permute-start.9) | collective-permute-done | bytes 131104 | tf_op jit(solution)/shard_map/ppermute | solution.py:313
  42.1 2.1 %collective-permute-done.6.near.refs_2_.refs_3_ = bf16[8,32,256]{2,1,0:T(8,128)(2,1)S(1)} collective-permute-done((bf16[8,32,256]{2,1,0:T(8,128)(2,1)S(1)}, bf16[8,32,256]{2,1,0:T(8,128)(2,1)S(1)}, u32[]{:S(2)}, u32[]{:S(2)}) %collective-permute-start.6) | collective-permute-done | bytes 131104 | tf_op jit(solution)/shard_map/ppermute | solution.py:313
  44.2 2.0 %collective-permute-done.5.far.refs_1_.refs_2_ = bf16[8,32,256]{2,1,0:T(8,128)(2,1)S(1)} collective-permute-done((bf16[8,32,256]{2,1,0:T(8,128)(2,1)S(1)}, bf16[8,32,256]{2,1,0:T(8,128)(2,1)S(1)}, u32[]{:S(2)}, u32[]{:S(2)}) %collective-permute-start.5) | collective-permute-done | bytes 131104 | tf_op jit(solution)/shard_map/ppermute | solution.py:313
  46.1 0.9 %shard_map.110 = (bf16[32,32,256]{2,1,0:T(8,128)(2,1)}, bf16[48,32,256]{2,1,0:T(8,128)(2,1)S(1)}) custom-call(bf16[8,32,256]{2,1,0:T(8,128)(2,1)S(1)} %get-tuple-element.29.own.refs_0_.refs_1_, bf16[8,32,256]{2,1,0:T(8,128)(2,1)S(1)} %collective-permute-done.5.far.refs_1_.refs_2_, bf16[8,32,256]{2,1,0:T(8,128)(2,1)S(1)} %collective-permute-done.6.near.refs_2_.refs_3_, ...), custom_call_target="tpu_custom_call" | custom-call | bytes 2097152 | tf_op jit(solution)/shard_map/pallas_call | solution.py:234
  47.0 2.7 %collective-permute-start.11 = (bf16[32,32,256]{2,1,0:T(8,128)(2,1)}, bf16[32,32,256]{2,1,0:T(8,128)(2,1)S(1)}, u32[]{:S(2)}, u32[]{:S(2)}) collective-permute-start(bf16[32,32,256]{2,1,0:T(8,128)(2,1)} %get-tuple-element.32), channel_id=1, source_target_pairs={{0,32},{16,240},{32,64},{48,16},{64,96},{80,48},{96,128},{112,80},... | collective-permute-start | bytes 1572872 | tf_op jit(solution)/shard_map/ppermute | solution.py:313
  49.9 15.5 %all_to_all.5 = f32[32,8,128]{2,1,0:T(8,128)S(1)} all-to-all(f32[32,8,128]{2,1,0:T(8,128)S(1)} %broadcast_in_dim.17), channel_id=1, replica_groups=mesh['z'=8,'core'=2,'y'=4,'x'=4] {'core','y','x'}, dimensions={0} | all-to-all | bytes 262144 | tf_op jit(solution)/shard_map/all_to_all | solution.py:336
  65.7 1.0 %collective-permute-start.13 = (bf16[2,4,8,32,256]{4,3,2,1,0:T(8,128)(2,1)S(1)}, bf16[2,4,8,32,256]{4,3,2,1,0:T(8,128)(2,1)}, u32[]{:S(2)}, u32[]{:S(2)}) collective-permute-start(bf16[2,4,8,32,256]{4,3,2,1,0:T(8,128)(2,1)S(1)} %shard_map.112), channel_id=1, source_target_pairs={{0,16},{16,0},{1,17},{17,1},{2,18},{18,2},{3,19},{19,3},{4,20},{20... | collective-permute-start | bytes 3145736 | tf_op jit(solution)/shard_map/ppermute | solution.py:321
  66.8 2.6 %collective-permute-start.7 = (f32[8,128]{1,0:T(8,128)S(1)}, f32[8,128]{1,0:T(8,128)S(1)}, u32[]{:S(2)}, u32[]{:S(2)}) collective-permute-start(f32[8,128]{1,0:T(8,128)S(1)} %broadcast_select_fusion), channel_id=1, source_target_pairs={{0,32},{16,240},{32,64},{48,16},{64,96},{80,48},{96,128},{112,80},... | collective-permute-start | bytes 12296 | tf_op jit(solution)/shard_map/ppermute | solution.py:313
  69.4 0.8 collective-permute-done.7.refs_2_
  70.1 1.6 %collective-permute-start.8 = (f32[8,128]{1,0:T(8,128)S(1)}, f32[8,128]{1,0:T(8,128)S(1)}, u32[]{:S(2)}, u32[]{:S(2)}) collective-permute-start(f32[8,128]{1,0:T(8,128)S(1)} %collective-permute-done.7.refs_2_), channel_id=1, source_target_pairs={{0,16},{16,0},{1,17},{17,1},{2,18},{18,2},{3,19},{19,3},{4,20},{20... | collective-permute-start | bytes 12296 | tf_op jit(solution)/shard_map/ppermute | solution.py:321
  72.0 0.6 collective-permute-done.8.refs_3_
  72.6 3.3 %shard_map.113 = (bf16[4,32,4096]{2,1,0:T(8,128)(2,1)}, f32[8,32,256]{2,1,0:T(8,128)}, f32[8,32,256]{2,1,0:T(8,128)}) custom-call(f32[24,8,256]{2,1,0:T(8,128)S(1)} %copy-done.2, f32[8,128]{1,0:T(8,128)S(1)} %reduce_sum.9.refs_1_, f32[8,128]{1,0:T(8,128)S(1)} %collective-permute-done.7.refs_2_, f32[8,128]{1,0:T(8,128)S(1)} %collective-permute-done.8.refs_3_, ...), custom_call_target="tpu_custom_call" | custom-call | bytes 4456448 | tf_op jit(solution)/shard_map/pallas_call | solution.py:271
  (42 shorter events, 1.8 us)
Async XLA Ops:
  0.6 6.3 %copy-start = (f32[1,4,32,4096]{3,2,1,0:T(8,128)S(1)}, f32[1,4,32,4096]{3,2,1,0:T(8,128)}, u32[]{:S(2)}) copy-start(f32[1,4,32,4096]{3,2,1,0:T(8,128)} %param.8) | copy-start | bytes 6291460
  0.6 6.3 %copy-start.3 = (bf16[1,4,32,4096]{3,2,1,0:T(8,128)(2,1)S(1)}, bf16[1,4,32,4096]{3,2,1,0:T(8,128)(2,1)}, u32[]{:S(2)}) copy-start(bf16[1,4,32,4096]{3,2,1,0:T(8,128)(2,1)} %param.7) | copy-start | bytes 3145732
  3.6 5.1 %collective-permute-start = (bf16[4,8,32,256]{3,2,1,0:T(8,128)(2,1)}, bf16[4,8,32,256]{3,2,1,0:T(8,128)(2,1)S(1)}, u32[]{:S(2)}, u32[]{:S(2)}) collective-permute-start(bf16[4,8,32,256]{3,2,1,0:T(8,128)(2,1)} %get-tuple-element.22), channel_id=1, source_target_pairs={{0,16},{16,0},{1,17},{17,1},{2,18},{18,2},{3,19},{19,3},{4,20},{20... | collective-permute-start | bytes 1572872 | tf_op jit(solution)/shard_map/ppermute | solution.py:321
  6.9 0.9 %copy-start.1 = (f32[24,8,256]{2,1,0:T(8,128)S(1)}, f32[24,8,256]{2,1,0:T(8,128)}, u32[]{:S(2)}) copy-start(f32[24,8,256]{2,1,0:T(8,128)} %get-tuple-element.31.table.refs_0_) | copy-start | bytes 589828
  7.9 0.9 %copy-start.2 = (f32[24,8,256]{2,1,0:T(8,128)S(1)}, f32[24,8,256]{2,1,0:T(8,128)}, u32[]{:S(2)}) copy-start(f32[24,8,256]{2,1,0:T(8,128)} %get-tuple-element.31.table.refs_0_) | copy-start | bytes 589828
  7.9 5.1 %copy-start.4 = (f32[4,2,32,256]{3,2,1,0:T(8,128)S(1)}, f32[4,2,32,256]{3,2,1,0:T(8,128)}, u32[]{:S(2)}) copy-start(f32[4,2,32,256]{3,2,1,0:T(8,128)} %param.9) | copy-start | bytes 786436
  7.9 5.1 %copy-start.6 = (f32[4,2,32,256]{3,2,1,0:T(8,128)S(1)}, f32[4,2,32,256]{3,2,1,0:T(8,128)}, u32[]{:S(2)}) copy-start(f32[4,2,32,256]{3,2,1,0:T(8,128)} %param.10) | copy-start | bytes 786436
  9.0 12.3 %collective-permute-start.1 = (bf16[3,8,32,256]{3,2,1,0:T(8,128)(2,1)S(1)}, bf16[3,8,32,256]{3,2,1,0:T(8,128)(2,1)S(1)}, u32[]{:S(2)}, u32[]{:S(2)}) collective-permute-start(bf16[3,8,32,256]{3,2,1,0:T(8,128)(2,1)S(1)} %get-tuple-element.28), channel_id=1, source_target_pairs={{0,32},{16,240},{32,64},{48,16},{64,96},{80,48},{96,128},{112,80},... | collective-permute-start | bytes 1179656 | tf_op jit(solution)/shard_map/ppermute | solution.py:313
  12.9 8.4 %collective-permute-start.2 = (bf16[2,8,32,256]{3,2,1,0:T(8,128)(2,1)S(1)}, bf16[2,8,32,256]{3,2,1,0:T(8,128)(2,1)S(1)}, u32[]{:S(2)}, u32[]{:S(2)}) collective-permute-start(bf16[2,8,32,256]{3,2,1,0:T(8,128)(2,1)S(1)} %get-tuple-element.23), channel_id=1, source_target_pairs={{0,224},{16,48},{32,0},{48,80},{64,32},{80,112},{96,64},{112,144},... | collective-permute-start | bytes 786440 | tf_op jit(solution)/shard_map/ppermute | solution.py:313
  21.4 10.3 %collective-permute-start.4 = (bf16[8,32,256]{2,1,0:T(8,128)(2,1)S(1)}, bf16[8,32,256]{2,1,0:T(8,128)(2,1)S(1)}, u32[]{:S(2)}, u32[]{:S(2)}) collective-permute-start(bf16[8,32,256]{2,1,0:T(8,128)(2,1)S(1)} %get-tuple-element.38), channel_id=1, source_target_pairs={{0,160},{16,112},{32,192},{48,144},{64,224},{80,176},{96,0},{112,2... | collective-permute-start | bytes 393224 | tf_op jit(solution)/shard_map/ppermute | solution.py:313
  21.5 10.3 %collective-permute-start.3 = (bf16[8,32,256]{2,1,0:T(8,128)(2,1)S(1)}, bf16[8,32,256]{2,1,0:T(8,128)(2,1)S(1)}, u32[]{:S(2)}, u32[]{:S(2)}) collective-permute-start(bf16[8,32,256]{2,1,0:T(8,128)(2,1)S(1)} %get-tuple-element.39), channel_id=1, source_target_pairs={{0,64},{16,208},{32,96},{48,240},{64,128},{80,16},{96,160},{112,48... | collective-permute-start | bytes 393224 | tf_op jit(solution)/shard_map/ppermute | solution.py:313
  22.9 14.1 %collective-permute-start.10 = (bf16[8,32,256]{2,1,0:T(8,128)(2,1)S(1)}, bf16[8,32,256]{2,1,0:T(8,128)(2,1)S(1)}, u32[]{:S(2)}, u32[]{:S(2)}) collective-permute-start(bf16[8,32,256]{2,1,0:T(8,128)(2,1)S(1)} %shard_map.105.refs_3_.refs_4_), channel_id=1, source_target_pairs={{0,192},{16,80},{32,224},{48,112},{64,0},{80,144},{96,32},{112,176... | collective-permute-start | bytes 393224 | tf_op jit(solution)/shard_map/ppermute | solution.py:313
  24.4 17.6 %collective-permute-start.9 = (bf16[8,32,256]{2,1,0:T(8,128)(2,1)S(1)}, bf16[8,32,256]{2,1,0:T(8,128)(2,1)S(1)}, u32[]{:S(2)}, u32[]{:S(2)}) collective-permute-start(bf16[8,32,256]{2,1,0:T(8,128)(2,1)S(1)} %shard_map.105.refs_3_.refs_4_), channel_id=1, source_target_pairs={{0,96},{16,176},{32,128},{48,208},{64,160},{80,240},{96,192},{112,... | collective-permute-start | bytes 393224 | tf_op jit(solution)/shard_map/ppermute | solution.py:313
  31.8 15.2 %copy-start.8 = (f32[8,32,256]{2,1,0:T(8,128)}, f32[8,32,256]{2,1,0:T(8,128)S(1)}, u32[]{:S(2)}) copy-start(f32[8,32,256]{2,1,0:T(8,128)S(1)} %get-tuple-element.34.refs_6_) | copy-start | bytes 786436
  31.8 12.3 %collective-permute-start.6 = (bf16[8,32,256]{2,1,0:T(8,128)(2,1)S(1)}, bf16[8,32,256]{2,1,0:T(8,128)(2,1)S(1)}, u32[]{:S(2)}, u32[]{:S(2)}) collective-permute-start(bf16[8,32,256]{2,1,0:T(8,128)(2,1)S(1)} %get-tuple-element.29.own.refs_0_.refs_1_), channel_id=1, source_target_pairs={{0,192},{16,80},{32,224},{48,112},{64,0},{80,144},{96,32},{112,176... | collective-permute-start | bytes 393224 | tf_op jit(solution)/shard_map/ppermute | solution.py:313
  36.8 9.3 %collective-permute-start.5 = (bf16[8,32,256]{2,1,0:T(8,128)(2,1)S(1)}, bf16[8,32,256]{2,1,0:T(8,128)(2,1)S(1)}, u32[]{:S(2)}, u32[]{:S(2)}) collective-permute-start(bf16[8,32,256]{2,1,0:T(8,128)(2,1)S(1)} %get-tuple-element.29.own.refs_0_.refs_1_), channel_id=1, source_target_pairs={{0,96},{16,176},{32,128},{48,208},{64,160},{80,240},{96,192},{112,... | collective-permute-start | bytes 393224 | tf_op jit(solution)/shard_map/ppermute | solution.py:313
  47.0 18.4 %collective-permute-start.12 = (bf16[48,32,256]{2,1,0:T(8,128)(2,1)S(1)}, bf16[48,32,256]{2,1,0:T(8,128)(2,1)S(1)}, u32[]{:S(2)}, u32[]{:S(2)}) collective-permute-start(bf16[48,32,256]{2,1,0:T(8,128)(2,1)S(1)} %get-tuple-element.33), channel_id=1, source_target_pairs={{0,224},{16,48},{32,0},{48,80},{64,32},{80,112},{96,64},{112,144},... | collective-permute-start | bytes 2359304 | tf_op jit(solution)/shard_map/ppermute | solution.py:313
  47.0 18.4 %collective-permute-start.11 = (bf16[32,32,256]{2,1,0:T(8,128)(2,1)}, bf16[32,32,256]{2,1,0:T(8,128)(2,1)S(1)}, u32[]{:S(2)}, u32[]{:S(2)}) collective-permute-start(bf16[32,32,256]{2,1,0:T(8,128)(2,1)} %get-tuple-element.32), channel_id=1, source_target_pairs={{0,32},{16,240},{32,64},{48,16},{64,96},{80,48},{96,128},{112,80},... | collective-permute-start | bytes 1572872 | tf_op jit(solution)/shard_map/ppermute | solution.py:313
  65.7 6.8 %collective-permute-start.13 = (bf16[2,4,8,32,256]{4,3,2,1,0:T(8,128)(2,1)S(1)}, bf16[2,4,8,32,256]{4,3,2,1,0:T(8,128)(2,1)}, u32[]{:S(2)}, u32[]{:S(2)}) collective-permute-start(bf16[2,4,8,32,256]{4,3,2,1,0:T(8,128)(2,1)S(1)} %shard_map.112), channel_id=1, source_target_pairs={{0,16},{16,0},{1,17},{17,1},{2,18},{18,2},{3,19},{19,3},{4,20},{20... | collective-permute-start | bytes 3145736 | tf_op jit(solution)/shard_map/ppermute | solution.py:321
  66.7 5.8 %copy-start.5 = (f32[4,2,32,256]{3,2,1,0:T(8,128)S(1)}, f32[4,2,32,256]{3,2,1,0:T(8,128)}, u32[]{:S(2)}) copy-start(f32[4,2,32,256]{3,2,1,0:T(8,128)} %param.9) | copy-start | bytes 786436
  66.7 5.8 %copy-start.7 = (f32[4,2,32,256]{3,2,1,0:T(8,128)S(1)}, f32[4,2,32,256]{3,2,1,0:T(8,128)}, u32[]{:S(2)}) copy-start(f32[4,2,32,256]{3,2,1,0:T(8,128)} %param.10) | copy-start | bytes 786436
  66.7 5.8 %copy-start.9 = (f32[8,32,256]{2,1,0:T(8,128)S(1)}, f32[8,32,256]{2,1,0:T(8,128)}, u32[]{:S(2)}) copy-start(f32[8,32,256]{2,1,0:T(8,128)} %copy-done.8) | copy-start | bytes 786436
  66.8 3.4 %collective-permute-start.7 = (f32[8,128]{1,0:T(8,128)S(1)}, f32[8,128]{1,0:T(8,128)S(1)}, u32[]{:S(2)}, u32[]{:S(2)}) collective-permute-start(f32[8,128]{1,0:T(8,128)S(1)} %broadcast_select_fusion), channel_id=1, source_target_pairs={{0,32},{16,240},{32,64},{48,16},{64,96},{80,48},{96,128},{112,80},... | collective-permute-start | bytes 12296 | tf_op jit(solution)/shard_map/ppermute | solution.py:313
  70.1 2.4 %collective-permute-start.8 = (f32[8,128]{1,0:T(8,128)S(1)}, f32[8,128]{1,0:T(8,128)S(1)}, u32[]{:S(2)}, u32[]{:S(2)}) collective-permute-start(f32[8,128]{1,0:T(8,128)S(1)} %collective-permute-done.7.refs_2_), channel_id=1, source_target_pairs={{0,16},{16,0},{1,17},{17,1},{2,18},{18,2},{3,19},{19,3},{4,20},{20... | collective-permute-start | bytes 12296 | tf_op jit(solution)/shard_map/ppermute | solution.py:321

commit v6 on v5

--- a/solution.py
+++ b/solution.py
@@ -382,7 +382,7 @@
 
     chosen = [((2, *half), bf16)]
     (give,) = call(bound(select_kernel, SIBLING_UPPER), chosen, later, *spread)
-    got = swap(give)
+    got = jnp.stack([swap(give[0]), swap(give[1])])
     (mine,) = call(bound(select_kernel, OWN_UPPER), chosen, later, *spread)
     path_params, momentum_next, params_next = last(
         entries, table, sums, side, other_side, mine, got, average, params, momentum

time: 76 us -> 78 us (1.026)
  starting transfers between devices: 27.2 us -> 23.5 us
  waiting for transfers between devices: 20.8 us -> 24.2 us
  other arithmetic: 0.08 us -> 1.38 us
  local copies, waits for them, and re-layouts: 1.09 us -> 2.12 us
  Pallas kernels: 10.4 us -> 9.46 us
  blocking collectives: 15.5 us -> 16.4 us
    ppermute x11, waiting for transfers between devices: 19.6 us -> 23.6 us  [moved(): return lax.ppermute(x, PATH, [(p, target(p)) for p in range(PATHS)])]
    ppermute x11, starting transfers between devices: 21.2 us -> 17.4 us  [moved(): return lax.ppermute(x, PATH, [(p, target(p)) for p in range(PATHS)])]
    another operation x0 -> x1, other arithmetic: none -> 1.3 us  [on_device(): got = jnp.stack([swap(give[0]), swap(give[1])])]
    pallas_call x1, Pallas kernels: 3.29 us -> 2.07 us  [last(): pl.pallas_call(lambda *refs: last_kernel(entries, *refs), grid=(STEPS,),...]
    squeeze x0 -> x1, local copies, waits for them, and re-layouts: none -> 1.05 us  [on_device(): got = jnp.stack([swap(give[0]), swap(give[1])])]
    all_to_all x1, blocking collectives: 15.5 us -> 16.4 us  [over_plane(): return jnp.sum(lax.all_to_all(parts, PLANE, 0, 0), axis=0)]
    ppermute x3 -> x4, starting transfers between devices: 5.96 us -> 6.1 us  [swap(): return lax.ppermute(x, 'core', [(0, 1), (1, 0)])]
  transfers between devices with their start and end apart: 14 -> 15, of which waited for: 8 -> 8; matrix products, arithmetic and copies ran while one was open for 0% -> 2% of each run, Pallas kernels for 4% -> 4%
where the time goes in v6:
time: 78 us; the launch traced here: 77.9 us
  waiting for transfers between devices  24.2 us (31%)
  starting transfers between devices  23.5 us (30%)
  blocking collectives  16.4 us (21%)
  Pallas kernels  9.46 us (12%)
  local copies, waits for them, and re-layouts  2.12 us (3%)
  other arithmetic  1.38 us (2%)
    ppermute x11, waiting for transfers between devices, moved(): return lax.ppermute(x, PATH, [(p, target(p)) for p in range(PATHS)])  23.6 us
    ppermute x11, starting transfers between devices, moved(): return lax.ppermute(x, PATH, [(p, target(p)) for p in range(PATHS)])  17.4 us
    all_to_all x1, blocking collectives, over_plane(): return jnp.sum(lax.all_to_all(parts, PLANE, 0, 0), axis=0)  16.4 us
    ppermute x4, starting transfers between devices, swap(): return lax.ppermute(x, 'core', [(0, 1), (1, 0)])  6.1 us
    pallas_call x1, Pallas kernels, given_half(): pl.pallas_call(give_kernel, out_shape=[half, table], in_specs=[HBM] * 5,...  2.94 us
    pallas_call x9, Pallas kernels, call(): pl.pallas_call(kernel, out_shape=shapes, in_specs=[VMEM] * len(args), out...  2.43 us
    pallas_call x1, Pallas kernels, last(): pl.pallas_call(lambda *refs: last_kernel(entries, *refs), grid=(STEPS,),...  2.07 us
    pallas_call x1, Pallas kernels, levelwise(): pl.pallas_call(kernel, grid=(LEVELS,), out_shape=shapes, in_specs=[VMEM]...  2.02 us
  transfers between devices with their start and end apart: 15, of which 8 were waited for; matrix products, arithmetic and copies ran while one was open for 2% of the time, Pallas kernels for 4%

profile of v6, /device:TPU:1, one launch (start us, length us, event | category | flops | bytes accessed | tf_op | source)
XLA Modules:
  0.0 77.9 jit_solution(13549511766156903231)
XLA Ops:
  0.7 2.9 %shard_map.102 = (bf16[4,8,32,256]{3,2,1,0:T(8,128)(2,1)}, f32[24,8,256]{2,1,0:T(8,128)}) custom-call(s32[4,16]{1,0:T(4,128)} %bitcast.32, s32[4,16]{1,0:T(4,128)} %bitcast.33, s32[2,4]{1,0:T(2,128)} %bitcast.34, bf16[4,32,4096]{2,1,0:T(8,128)(2,1)} %bitcast.24, f32[4,32,4096]{2,1,0:T(8,128)} %bitcast.21), custom_call_target="tpu_custom_call" | custom-call | bytes 4194304 | tf_op jit(solution)/shard_map/pallas_call | solution.py:289
  3.6 3.3 %collective-permute-start = (bf16[4,8,32,256]{3,2,1,0:T(8,128)(2,1)}, bf16[4,8,32,256]{3,2,1,0:T(8,128)(2,1)S(1)}, u32[]{:S(2)}, u32[]{:S(2)}) collective-permute-start(bf16[4,8,32,256]{3,2,1,0:T(8,128)(2,1)} %get-tuple-element.22), channel_id=1, source_target_pairs={{0,16},{16,0},{1,17},{17,1},{2,18},{18,2},{3,19},{19,3},{4,20},{20... | collective-permute-start | bytes 1572872 | tf_op jit(solution)/shard_map/ppermute | solution.py:321
  6.9 0.9 %copy-done.1 = f32[24,8,256]{2,1,0:T(8,128)S(1)} copy-done((f32[24,8,256]{2,1,0:T(8,128)S(1)}, f32[24,8,256]{2,1,0:T(8,128)}, u32[]{:S(2)}) %copy-start.1) | copy-done | bytes 196632
  8.0 0.6 collective-permute-done.got
  9.0 3.9 %collective-permute-start.1 = (bf16[3,8,32,256]{3,2,1,0:T(8,128)(2,1)S(1)}, bf16[3,8,32,256]{3,2,1,0:T(8,128)(2,1)S(1)}, u32[]{:S(2)}, u32[]{:S(2)}) collective-permute-start(bf16[3,8,32,256]{3,2,1,0:T(8,128)(2,1)S(1)} %get-tuple-element.28), channel_id=1, source_target_pairs={{0,32},{16,240},{32,64},{48,16},{64,96},{80,48},{96,128},{112,80},... | collective-permute-start | bytes 1179656 | tf_op jit(solution)/shard_map/ppermute | solution.py:313
  13.0 2.0 %shard_map.107 = f32[4,32,4096]{2,1,0:T(8,128)} custom-call(f32[24,8,256]{2,1,0:T(8,128)S(1)} %copy-done.2, bf16[4,32,4096]{2,1,0:T(8,128)(2,1)S(1)} %bitcast.26, f32[4,32,4096]{2,1,0:T(8,128)S(1)} %bitcast.23), custom_call_target="tpu_custom_call" | custom-call | bytes 5242880 | tf_op jit(solution)/shard_map/pallas_call | solution.py:250
  15.1 6.2 %collective-permute-done.2.minus = bf16[2,8,32,256]{3,2,1,0:T(8,128)(2,1)S(1)} collective-permute-done((bf16[2,8,32,256]{3,2,1,0:T(8,128)(2,1)S(1)}, bf16[2,8,32,256]{3,2,1,0:T(8,128)(2,1)S(1)}, u32[]{:S(2)}, u32[]{:S(2)}) %collective-permute-start.2) | collective-permute-done | bytes 262176 | tf_op jit(solution)/shard_map/ppermute | solution.py:313
  21.4 1.4 %collective-permute-start.3 = (bf16[8,32,256]{2,1,0:T(8,128)(2,1)S(1)}, bf16[8,32,256]{2,1,0:T(8,128)(2,1)S(1)}, u32[]{:S(2)}, u32[]{:S(2)}) collective-permute-start(bf16[8,32,256]{2,1,0:T(8,128)(2,1)S(1)} %get-tuple-element.41), channel_id=1, source_target_pairs={{0,64},{16,208},{32,96},{48,240},{64,128},{80,16},{96,160},{112,48... | collective-permute-start | bytes 393224 | tf_op jit(solution)/shard_map/ppermute | solution.py:313
  22.8 1.7 %collective-permute-start.10 = (bf16[8,32,256]{2,1,0:T(8,128)(2,1)S(1)}, bf16[8,32,256]{2,1,0:T(8,128)(2,1)S(1)}, u32[]{:S(2)}, u32[]{:S(2)}) collective-permute-start(bf16[8,32,256]{2,1,0:T(8,128)(2,1)S(1)} %shard_map.105.refs_3_.refs_4_), channel_id=1, source_target_pairs={{0,192},{16,80},{32,224},{48,112},{64,0},{80,144},{96,32},{112,176... | collective-permute-start | bytes 393224 | tf_op jit(solution)/shard_map/ppermute | solution.py:313
  24.5 3.8 %collective-permute-start.9 = (bf16[8,32,256]{2,1,0:T(8,128)(2,1)S(1)}, bf16[8,32,256]{2,1,0:T(8,128)(2,1)S(1)}, u32[]{:S(2)}, u32[]{:S(2)}) collective-permute-start(bf16[8,32,256]{2,1,0:T(8,128)(2,1)S(1)} %shard_map.105.refs_3_.refs_4_), channel_id=1, source_target_pairs={{0,96},{16,176},{32,128},{48,208},{64,160},{80,240},{96,192},{112,... | collective-permute-start | bytes 393224 | tf_op jit(solution)/shard_map/ppermute | solution.py:313
  28.3 6.8 %collective-permute-done.4.far = bf16[8,32,256]{2,1,0:T(8,128)(2,1)S(1)} collective-permute-done((bf16[8,32,256]{2,1,0:T(8,128)(2,1)S(1)}, bf16[8,32,256]{2,1,0:T(8,128)(2,1)S(1)}, u32[]{:S(2)}, u32[]{:S(2)}) %collective-permute-start.4) | collective-permute-done | bytes 131104 | tf_op jit(solution)/shard_map/ppermute | solution.py:313
  35.3 1.4 %collective-permute-start.6 = (bf16[8,32,256]{2,1,0:T(8,128)(2,1)S(1)}, bf16[8,32,256]{2,1,0:T(8,128)(2,1)S(1)}, u32[]{:S(2)}, u32[]{:S(2)}) collective-permute-start(bf16[8,32,256]{2,1,0:T(8,128)(2,1)S(1)} %get-tuple-element.29.own.refs_0_.refs_1_), channel_id=1, source_target_pairs={{0,192},{16,80},{32,224},{48,112},{64,0},{80,144},{96,32},{112,176... | collective-permute-start | bytes 393224 | tf_op jit(solution)/shard_map/ppermute | solution.py:313
  37.0 1.0 %collective-permute-done.9.refs_4_.refs_5_ = bf16[8,32,256]{2,1,0:T(8,128)(2,1)S(1)} collective-permute-done((bf16[8,32,256]{2,1,0:T(8,128)(2,1)S(1)}, bf16[8,32,256]{2,1,0:T(8,128)(2,1)S(1)}, u32[]{:S(2)}, u32[]{:S(2)}) %collective-permute-start.9) | collective-permute-done | bytes 131104 | tf_op jit(solution)/shard_map/ppermute | solution.py:313
  38.0 5.7 %collective-permute-done.5.far.refs_1_.refs_2_ = bf16[8,32,256]{2,1,0:T(8,128)(2,1)S(1)} collective-permute-done((bf16[8,32,256]{2,1,0:T(8,128)(2,1)S(1)}, bf16[8,32,256]{2,1,0:T(8,128)(2,1)S(1)}, u32[]{:S(2)}, u32[]{:S(2)}) %collective-permute-start.5) | collective-permute-done | bytes 131104 | tf_op jit(solution)/shard_map/ppermute | solution.py:313
  43.8 2.7 %collective-permute-done.6.near.refs_2_.refs_3_ = bf16[8,32,256]{2,1,0:T(8,128)(2,1)S(1)} collective-permute-done((bf16[8,32,256]{2,1,0:T(8,128)(2,1)S(1)}, bf16[8,32,256]{2,1,0:T(8,128)(2,1)S(1)}, u32[]{:S(2)}, u32[]{:S(2)}) %collective-permute-start.6) | collective-permute-done | bytes 131104 | tf_op jit(solution)/shard_map/ppermute | solution.py:313
  46.5 1.1 %shard_map.110 = (bf16[32,32,256]{2,1,0:T(8,128)(2,1)}, bf16[48,32,256]{2,1,0:T(8,128)(2,1)}) custom-call(bf16[8,32,256]{2,1,0:T(8,128)(2,1)S(1)} %get-tuple-element.29.own.refs_0_.refs_1_, bf16[8,32,256]{2,1,0:T(8,128)(2,1)S(1)} %collective-permute-done.5.far.refs_1_.refs_2_, bf16[8,32,256]{2,1,0:T(8,128)(2,1)S(1)} %collective-permute-done.6.near.refs_2_.refs_3_, ...), custom_call_target="tpu_custom_call" | custom-call | bytes 2097152 | tf_op jit(solution)/shard_map/pallas_call | solution.py:234
  47.6 2.7 %collective-permute-start.11 = (bf16[32,32,256]{2,1,0:T(8,128)(2,1)}, bf16[32,32,256]{2,1,0:T(8,128)(2,1)S(1)}, u32[]{:S(2)}, u32[]{:S(2)}) collective-permute-start(bf16[32,32,256]{2,1,0:T(8,128)(2,1)} %get-tuple-element.32), channel_id=1, source_target_pairs={{0,32},{16,240},{32,64},{48,16},{64,96},{80,48},{96,128},{112,80},... | collective-permute-start | bytes 1572872 | tf_op jit(solution)/shard_map/ppermute | solution.py:313
  50.5 16.4 %all_to_all.5 = f32[32,8,128]{2,1,0:T(8,128)S(1)} all-to-all(f32[32,8,128]{2,1,0:T(8,128)S(1)} %broadcast_in_dim.17), channel_id=1, replica_groups=mesh['z'=8,'core'=2,'y'=4,'x'=4] {'core','y','x'}, dimensions={0} | all-to-all | bytes 262144 | tf_op jit(solution)/shard_map/all_to_all | solution.py:336
  67.2 1.0 %slice_bitcast_fusion.1 = (bf16[4,8,32,256]{3,2,1,0:T(8,128)(2,1)}, bf16[4,8,32,256]{3,2,1,0:T(8,128)(2,1)}) fusion(bf16[2,4,8,32,256]{4,3,2,1,0:T(8,128)(2,1)S(1)} %shard_map.112), kind=kLoop, calls=%fused_computation.2 | loop fusion | bytes 2097152 | tf_op jit(solution)/shard_map/squeeze | solution.py:385
  68.8 2.4 %collective-permute-start.7 = (f32[8,128]{1,0:T(8,128)S(1)}, f32[8,128]{1,0:T(8,128)S(1)}, u32[]{:S(2)}, u32[]{:S(2)}) collective-permute-start(f32[8,128]{1,0:T(8,128)S(1)} %broadcast_select_fusion), channel_id=1, source_target_pairs={{0,32},{16,240},{32,64},{48,16},{64,96},{80,48},{96,128},{112,80},... | collective-permute-start | bytes 12296 | tf_op jit(solution)/shard_map/ppermute | solution.py:313
  71.2 0.8 collective-permute-done.7.refs_2_
  72.0 2.2 %collective-permute-start.8 = (f32[8,128]{1,0:T(8,128)S(1)}, f32[8,128]{1,0:T(8,128)S(1)}, u32[]{:S(2)}, u32[]{:S(2)}) collective-permute-start(f32[8,128]{1,0:T(8,128)S(1)} %collective-permute-done.7.refs_2_), channel_id=1, source_target_pairs={{0,16},{16,0},{1,17},{17,1},{2,18},{18,2},{3,19},{19,3},{4,20},{20... | collective-permute-start | bytes 12296 | tf_op jit(solution)/shard_map/ppermute | solution.py:321
  74.5 1.3 %pad_maximum_fusion.refs_5_ = bf16[2,4,8,32,256]{4,3,2,1,0:T(8,128)(2,1)S(1)} fusion(bf16[1,4,8,32,256]{4,3,2,1,0:T(8,128)(2,1)} %bitcast.13, bf16[1,4,8,32,256]{4,3,2,1,0:T(8,128)(2,1)} %bitcast.11), kind=kLoop, calls=%fused_computation | loop fusion | flops 524288 | bytes 2097152 | tf_op jit(solution)/shard_map/stack | solution.py:385
  75.8 2.1 %shard_map.113 = (bf16[4,32,4096]{2,1,0:T(8,128)(2,1)}, f32[8,32,256]{2,1,0:T(8,128)}, f32[8,32,256]{2,1,0:T(8,128)}) custom-call(f32[24,8,256]{2,1,0:T(8,128)S(1)} %copy-done.2, f32[8,128]{1,0:T(8,128)S(1)} %reduce_sum.9.refs_1_, f32[8,128]{1,0:T(8,128)S(1)} %collective-permute-done.7.refs_2_, f32[8,128]{1,0:T(8,128)S(1)} %collective-permute-done.8.refs_3_, ...), custom_call_target="tpu_custom_call" | custom-call | bytes 4456448 | tf_op jit(solution)/shard_map/pallas_call | solution.py:271
  (38 shorter events, 2.5 us)
Async XLA Ops:
  0.6 6.3 %copy-start.3 = (bf16[1,4,32,4096]{3,2,1,0:T(8,128)(2,1)S(1)}, bf16[1,4,32,4096]{3,2,1,0:T(8,128)(2,1)}, u32[]{:S(2)}) copy-start(bf16[1,4,32,4096]{3,2,1,0:T(8,128)(2,1)} %param.7) | copy-start | bytes 3145732
  0.6 6.3 %copy-start = (f32[1,4,32,4096]{3,2,1,0:T(8,128)S(1)}, f32[1,4,32,4096]{3,2,1,0:T(8,128)}, u32[]{:S(2)}) copy-start(f32[1,4,32,4096]{3,2,1,0:T(8,128)} %param.8) | copy-start | bytes 6291460
  3.6 5.1 %collective-permute-start = (bf16[4,8,32,256]{3,2,1,0:T(8,128)(2,1)}, bf16[4,8,32,256]{3,2,1,0:T(8,128)(2,1)S(1)}, u32[]{:S(2)}, u32[]{:S(2)}) collective-permute-start(bf16[4,8,32,256]{3,2,1,0:T(8,128)(2,1)} %get-tuple-element.22), channel_id=1, source_target_pairs={{0,16},{16,0},{1,17},{17,1},{2,18},{18,2},{3,19},{19,3},{4,20},{20... | collective-permute-start | bytes 1572872 | tf_op jit(solution)/shard_map/ppermute | solution.py:321
  6.9 0.9 %copy-start.1 = (f32[24,8,256]{2,1,0:T(8,128)S(1)}, f32[24,8,256]{2,1,0:T(8,128)}, u32[]{:S(2)}) copy-start(f32[24,8,256]{2,1,0:T(8,128)} %get-tuple-element.31.table.refs_0_) | copy-start | bytes 589828
  7.9 0.9 %copy-start.2 = (f32[24,8,256]{2,1,0:T(8,128)S(1)}, f32[24,8,256]{2,1,0:T(8,128)}, u32[]{:S(2)}) copy-start(f32[24,8,256]{2,1,0:T(8,128)} %get-tuple-element.31.table.refs_0_) | copy-start | bytes 589828
  7.9 5.1 %copy-start.4 = (f32[4,2,32,256]{3,2,1,0:T(8,128)S(1)}, f32[4,2,32,256]{3,2,1,0:T(8,128)}, u32[]{:S(2)}) copy-start(f32[4,2,32,256]{3,2,1,0:T(8,128)} %param.9) | copy-start | bytes 786436
  7.9 5.1 %copy-start.5 = (f32[4,2,32,256]{3,2,1,0:T(8,128)S(1)}, f32[4,2,32,256]{3,2,1,0:T(8,128)}, u32[]{:S(2)}) copy-start(f32[4,2,32,256]{3,2,1,0:T(8,128)} %param.10) | copy-start | bytes 786436
  9.0 12.3 %collective-permute-start.1 = (bf16[3,8,32,256]{3,2,1,0:T(8,128)(2,1)S(1)}, bf16[3,8,32,256]{3,2,1,0:T(8,128)(2,1)S(1)}, u32[]{:S(2)}, u32[]{:S(2)}) collective-permute-start(bf16[3,8,32,256]{3,2,1,0:T(8,128)(2,1)S(1)} %get-tuple-element.28), channel_id=1, source_target_pairs={{0,32},{16,240},{32,64},{48,16},{64,96},{80,48},{96,128},{112,80},... | collective-permute-start | bytes 1179656 | tf_op jit(solution)/shard_map/ppermute | solution.py:313
  12.9 8.4 %collective-permute-start.2 = (bf16[2,8,32,256]{3,2,1,0:T(8,128)(2,1)S(1)}, bf16[2,8,32,256]{3,2,1,0:T(8,128)(2,1)S(1)}, u32[]{:S(2)}, u32[]{:S(2)}) collective-permute-start(bf16[2,8,32,256]{3,2,1,0:T(8,128)(2,1)S(1)} %get-tuple-element.23), channel_id=1, source_target_pairs={{0,224},{16,48},{32,0},{48,80},{64,32},{80,112},{96,64},{112,144},... | collective-permute-start | bytes 786440 | tf_op jit(solution)/shard_map/ppermute | solution.py:313
  21.4 6.9 %collective-permute-start.3 = (bf16[8,32,256]{2,1,0:T(8,128)(2,1)S(1)}, bf16[8,32,256]{2,1,0:T(8,128)(2,1)S(1)}, u32[]{:S(2)}, u32[]{:S(2)}) collective-permute-start(bf16[8,32,256]{2,1,0:T(8,128)(2,1)S(1)} %get-tuple-element.41), channel_id=1, source_target_pairs={{0,64},{16,208},{32,96},{48,240},{64,128},{80,16},{96,160},{112,48... | collective-permute-start | bytes 393224 | tf_op jit(solution)/shard_map/ppermute | solution.py:313
  22.8 12.3 %collective-permute-start.4 = (bf16[8,32,256]{2,1,0:T(8,128)(2,1)S(1)}, bf16[8,32,256]{2,1,0:T(8,128)(2,1)S(1)}, u32[]{:S(2)}, u32[]{:S(2)}) collective-permute-start(bf16[8,32,256]{2,1,0:T(8,128)(2,1)S(1)} %get-tuple-element.40), channel_id=1, source_target_pairs={{0,160},{16,112},{32,192},{48,144},{64,224},{80,176},{96,0},{112,2... | collective-permute-start | bytes 393224 | tf_op jit(solution)/shard_map/ppermute | solution.py:313
  22.8 14.3 %collective-permute-start.10 = (bf16[8,32,256]{2,1,0:T(8,128)(2,1)S(1)}, bf16[8,32,256]{2,1,0:T(8,128)(2,1)S(1)}, u32[]{:S(2)}, u32[]{:S(2)}) collective-permute-start(bf16[8,32,256]{2,1,0:T(8,128)(2,1)S(1)} %shard_map.105.refs_3_.refs_4_), channel_id=1, source_target_pairs={{0,192},{16,80},{32,224},{48,112},{64,0},{80,144},{96,32},{112,176... | collective-permute-start | bytes 393224 | tf_op jit(solution)/shard_map/ppermute | solution.py:313
  24.5 13.5 %collective-permute-start.9 = (bf16[8,32,256]{2,1,0:T(8,128)(2,1)S(1)}, bf16[8,32,256]{2,1,0:T(8,128)(2,1)S(1)}, u32[]{:S(2)}, u32[]{:S(2)}) collective-permute-start(bf16[8,32,256]{2,1,0:T(8,128)(2,1)S(1)} %shard_map.105.refs_3_.refs_4_), channel_id=1, source_target_pairs={{0,96},{16,176},{32,128},{48,208},{64,160},{80,240},{96,192},{112,... | collective-permute-start | bytes 393224 | tf_op jit(solution)/shard_map/ppermute | solution.py:313
  35.2 8.6 %collective-permute-start.5 = (bf16[8,32,256]{2,1,0:T(8,128)(2,1)S(1)}, bf16[8,32,256]{2,1,0:T(8,128)(2,1)S(1)}, u32[]{:S(2)}, u32[]{:S(2)}) collective-permute-start(bf16[8,32,256]{2,1,0:T(8,128)(2,1)S(1)} %get-tuple-element.29.own.refs_0_.refs_1_), channel_id=1, source_target_pairs={{0,96},{16,176},{32,128},{48,208},{64,160},{80,240},{96,192},{112,... | collective-permute-start | bytes 393224 | tf_op jit(solution)/shard_map/ppermute | solution.py:313
  35.3 11.2 %collective-permute-start.6 = (bf16[8,32,256]{2,1,0:T(8,128)(2,1)S(1)}, bf16[8,32,256]{2,1,0:T(8,128)(2,1)S(1)}, u32[]{:S(2)}, u32[]{:S(2)}) collective-permute-start(bf16[8,32,256]{2,1,0:T(8,128)(2,1)S(1)} %get-tuple-element.29.own.refs_0_.refs_1_), channel_id=1, source_target_pairs={{0,192},{16,80},{32,224},{48,112},{64,0},{80,144},{96,32},{112,176... | collective-permute-start | bytes 393224 | tf_op jit(solution)/shard_map/ppermute | solution.py:313
  47.6 19.3 %collective-permute-start.12 = (bf16[48,32,256]{2,1,0:T(8,128)(2,1)}, bf16[48,32,256]{2,1,0:T(8,128)(2,1)S(1)}, u32[]{:S(2)}, u32[]{:S(2)}) collective-permute-start(bf16[48,32,256]{2,1,0:T(8,128)(2,1)} %get-tuple-element.33), channel_id=1, source_target_pairs={{0,224},{16,48},{32,0},{48,80},{64,32},{80,112},{96,64},{112,144},... | collective-permute-start | bytes 2359304 | tf_op jit(solution)/shard_map/ppermute | solution.py:313
  47.6 19.3 %collective-permute-start.11 = (bf16[32,32,256]{2,1,0:T(8,128)(2,1)}, bf16[32,32,256]{2,1,0:T(8,128)(2,1)S(1)}, u32[]{:S(2)}, u32[]{:S(2)}) collective-permute-start(bf16[32,32,256]{2,1,0:T(8,128)(2,1)} %get-tuple-element.32), channel_id=1, source_target_pairs={{0,32},{16,240},{32,64},{48,16},{64,96},{80,48},{96,128},{112,80},... | collective-permute-start | bytes 1572872 | tf_op jit(solution)/shard_map/ppermute | solution.py:313
  68.3 6.2 %collective-permute-start.13 = (bf16[4,8,32,256]{3,2,1,0:T(8,128)(2,1)}, bf16[4,8,32,256]{3,2,1,0:T(8,128)(2,1)}, u32[]{:S(2)}, u32[]{:S(2)}) collective-permute-start(bf16[4,8,32,256]{3,2,1,0:T(8,128)(2,1)} %get-tuple-element.38), channel_id=1, source_target_pairs={{0,16},{16,0},{1,17},{17,1},{2,18},{18,2},{3,19},{19,3},{4,20},{20... | collective-permute-start | bytes 1572872 | tf_op jit(solution)/shard_map/ppermute | solution.py:321
  68.8 5.7 %collective-permute-start.14 = (bf16[4,8,32,256]{3,2,1,0:T(8,128)(2,1)}, bf16[4,8,32,256]{3,2,1,0:T(8,128)(2,1)}, u32[]{:S(2)}, u32[]{:S(2)}) collective-permute-start(bf16[4,8,32,256]{3,2,1,0:T(8,128)(2,1)} %get-tuple-element.39), channel_id=1, source_target_pairs={{0,16},{16,0},{1,17},{17,1},{2,18},{18,2},{3,19},{19,3},{4,20},{20... | collective-permute-start | bytes 1572872 | tf_op jit(solution)/shard_map/ppermute | solution.py:321
  68.8 3.2 %collective-permute-start.7 = (f32[8,128]{1,0:T(8,128)S(1)}, f32[8,128]{1,0:T(8,128)S(1)}, u32[]{:S(2)}, u32[]{:S(2)}) collective-permute-start(f32[8,128]{1,0:T(8,128)S(1)} %broadcast_select_fusion), channel_id=1, source_target_pairs={{0,32},{16,240},{32,64},{48,16},{64,96},{80,48},{96,128},{112,80},... | collective-permute-start | bytes 12296 | tf_op jit(solution)/shard_map/ppermute | solution.py:313
  72.0 3.8 %collective-permute-start.8 = (f32[8,128]{1,0:T(8,128)S(1)}, f32[8,128]{1,0:T(8,128)S(1)}, u32[]{:S(2)}, u32[]{:S(2)}) collective-permute-start(f32[8,128]{1,0:T(8,128)S(1)} %collective-permute-done.7.refs_2_), channel_id=1, source_target_pairs={{0,16},{16,0},{1,17},{17,1},{2,18},{18,2},{3,19},{19,3},{4,20},{20... | collective-permute-start | bytes 12296 | tf_op jit(solution)/shard_map/ppermute | solution.py:321
